TPU v7x, 256 devices: a whole 4x4x8 slice. The times are simulated.
256 devices in a mesh: sess: 32 (over x_hi, z, core), exp: 8 (over y, x_lo).
Axes of the slice: x: 4 (x_hi: 2, x_lo: 2; x = x_hi * 2 + x_lo), y: 4, z: 8, core: 2. Of those that a mesh axis runs over, the one named last changes fastest.
Arguments:
- tokens: bfloat16 [32, 256, 4096], P('sess'), may hold values from -6 to 6
- routes: int32 [32, 256, 2], P('sess'), may hold values from 0 to 31, all different within a row; in each aligned block of 256 rows (0 to 255, 256 to 511, ..., all dimensions but the last counted through in order) at most 32 rows name the same one
- gates: float32 [32, 256, 2], P('sess'), may hold values from 0.2 to 1
- w_gate: bfloat16 [32, 4096, 1408], P('sess', None, 'exp'), may hold values from -0.09375 to 0.09375
- w_up: bfloat16 [32, 4096, 1408], P('sess', None, 'exp'), may hold values from -0.09375 to 0.09375
- w_down: bfloat16 [32, 1408, 4096], P('sess', 'exp'), may hold values from -0.15625 to 0.15625
- feat_gain: float32 [4096], replicated, may hold values from 0.25 to 1.75
- w_proj: bfloat16 [4096, 256], replicated, may hold values from -0.09375 to 0.09375
- conv_time: bfloat16 [3, 3, 3, 256, 256], replicated, may hold values from -0.078125 to 0.078125
- bias_time: float32 [256], replicated, may hold values from -3 to 3
- conv_space: bfloat16 [3, 3, 256, 256], replicated, may hold values from -0.125 to 0.125
- bias_space: float32 [256], replicated, may hold values from -3 to 3
- frame_cache: bfloat16 [3, 32, 64, 16, 256], P(None, 'sess', 'exp'), may hold values from -6 to 6
- cache_head: int32 [32], P('sess'), may hold values from 0 to 2
Outputs:
- out_frame: bfloat16 [32, 64, 16, 256], P('sess', 'exp')
Inputs may be any that keep to these rules, and one draw needn't show every extreme that they name: `routes`: each token names 2 different experts; among the tokens of one session no expert is named more than 32 times, and in some sessions one is named exactly 32 times. The frame before the previous one is in slot (cache_head + 2) mod 3.
All inputs are finite; a program needn't handle non-finite values.
Results may differ from a plain program's by a relative error of at most 0.017.
Values may be sent and summed in bfloat16 or wider, within the bound.
No kernel may reach another device: no remote copies, remote signals or barrier semaphores. Data moves between devices by JAX's collectives and lax.ppermute only.
A program may use at most 64 MiB of HBM per device.

v0:
```python
import jax
import jax.numpy as jnp
from jax import lax
from jax.sharding import Mesh
from jax.sharding import PartitionSpec as P

TOPK = 2
GRID_W = 8
TROW = 4
EXP = ("exp_0", "exp_1")


epsilon = 1e-06


def summed_rows(x, axes, dim):
    for axis in axes:
        x = lax.psum_scatter(x, axis, scatter_dimension=dim, tiled=True)
    return x


def in_blocks(x, dim, count):
    before, after = (x.shape[:dim], x.shape[dim + 1 :])
    return jnp.moveaxis(x.reshape(*before, count, -1, *after), dim, 0)


def sent_and_summed(x, axis, dim):
    blocks = in_blocks(x, dim, lax.axis_size(axis))
    arrived = lax.all_to_all(blocks, axis, split_axis=0, concat_axis=0, tiled=True)
    return arrived.astype(jnp.float32).sum(axis=0)


def extended(cells, sides, width):
    for axis, dim in sides:
        count = lax.axis_size(axis)
        ends = count - 1
        head = lax.slice_in_dim(cells, 0, width, axis=dim)
        tail = lax.slice_in_dim(cells, cells.shape[dim] - width, cells.shape[dim], axis=dim)
        cells = jnp.concatenate(
            [
                lax.ppermute(tail, axis, [(i, (i + 1) % count) for i in range(ends)]),
                cells,
                lax.ppermute(head, axis, [((i + 1) % count, i) for i in range(ends)]),
            ],
            axis=dim,
        )
    return cells


def slot_targets(routes, experts, capacity):
    flat = routes.reshape(-1)
    onehot = (flat[:, None] == jnp.arange(experts, dtype=jnp.int32)[None, :]).astype(jnp.int32)
    before = jnp.cumsum(onehot, axis=0) - onehot
    position = jnp.sum(before * onehot, axis=1)
    return flat * capacity + position


def pick_slot(cache, heads):
    choose = (jnp.arange(3, dtype=jnp.int32)[:, None] == heads[None, :]).astype(jnp.float32)
    return jnp.sum(choose[:, :, None, None, None] * cache.astype(jnp.float32), axis=0).astype(
        jnp.bfloat16
    )


def expert_rows(rows, w_gate, w_up, w_down):
    leading = rows.shape[:-1]
    flat_rows = rows.reshape(-1, rows.shape[-1])
    gate = jnp.dot(flat_rows, w_gate[0], preferred_element_type=jnp.float32)
    upward = jnp.dot(flat_rows, w_up[0], preferred_element_type=jnp.float32)
    hidden = (jax.nn.silu(gate) * upward).astype(jnp.bfloat16)
    output = jnp.dot(hidden, w_down[0], preferred_element_type=jnp.float32).astype(jnp.bfloat16)
    return output.reshape(leading + (output.shape[-1],))


def space_patches(field, height, breadth):
    return jnp.concatenate(
        [
            field[:, row_step : row_step + height, col_step : col_step + breadth, :]
            for row_step in range(3)
            for col_step in range(3)
        ],
        axis=-1,
    )


def time_patches(frames, height, breadth):
    return jnp.concatenate(
        [space_patches(frames[frame_step], height, breadth) for frame_step in range(3)], axis=-1
    )


def apply_kernel(patches, kernel):
    channels = kernel.shape[-1]
    return jnp.dot(
        patches.reshape(-1, patches.shape[-1]),
        kernel.reshape(-1, channels),
        preferred_element_type=jnp.float32,
    )


def body(
    tokens,
    routes,
    gates,
    w_gate,
    w_up,
    w_down,
    feat_gain,
    w_proj,
    conv_time,
    bias_time,
    conv_space,
    bias_space,
    frame_cache,
    cache_head,
):
    sess_count = lax.axis_size("sess")
    exp_count = lax.axis_size(EXP)
    tile = lax.axis_index(EXP)
    width = tokens.shape[-1]
    channels = w_proj.shape[-1]
    local = tokens[0]
    tok_count = local.shape[0]
    capacity = 2 * tok_count * TOPK // sess_count
    count = tok_count * TOPK
    dest = slot_targets(routes[0], sess_count, capacity)
    source = jnp.arange(count, dtype=jnp.int32) // TOPK
    weight_rows = gates[0].reshape(count, 1)
    share = width // exp_count
    offset = tile * share
    portion = lax.dynamic_slice_in_dim(local, offset, share, 1)
    outgoing = jnp.zeros((sess_count * capacity, share), jnp.bfloat16).at[dest].set(portion[source])
    outgoing = outgoing.reshape(sess_count, capacity, share)
    arrived = lax.all_to_all(outgoing, "sess", split_axis=0, concat_axis=0, tiled=True)
    joined = lax.all_gather(arrived, EXP, axis=2, tiled=True)
    answer = expert_rows(joined, w_gate, w_up, w_down)
    reduced = summed_rows(answer.astype(jnp.float32).astype(jnp.bfloat16), EXP, 2).astype(
        jnp.float32
    )
    returned = (
        lax.all_to_all(
            reduced.astype(jnp.bfloat16), "sess", split_axis=0, concat_axis=0, tiled=True
        )
        .astype(reduced.dtype)
        .reshape(sess_count * capacity, share)
    )
    combined = jnp.sum((returned[dest] * weight_rows).reshape(-1, TOPK, share), axis=1)
    feat = (portion.astype(jnp.float32) + combined).astype(jnp.bfloat16)
    square = lax.psum(jnp.sum(jnp.square(feat.astype(jnp.float32)), axis=-1), EXP)
    scale = lax.rsqrt(square / width + epsilon)[:, None]
    gain_share = lax.dynamic_slice_in_dim(feat_gain, offset, share, 0)
    normed = (feat.astype(jnp.float32) * scale * gain_share).astype(jnp.bfloat16)
    proj_share = lax.dynamic_slice_in_dim(w_proj, offset, share, 0)
    partial_value = jnp.dot(normed, proj_share, preferred_element_type=jnp.float32)
    coarse = sent_and_summed(partial_value.astype(jnp.bfloat16), EXP, 0).astype(jnp.bfloat16)
    coarse = coarse.reshape(1, TROW, GRID_W, channels)
    fine = jnp.repeat(jnp.repeat(coarse, 2, axis=1), 2, axis=2)
    latest = pick_slot(frame_cache, cache_head)
    older = pick_slot(frame_cache, (cache_head + 2) % 3)
    stack = jnp.stack([older, latest, fine])
    height = fine.shape[1]
    breadth = fine.shape[2]
    framed = extended(stack, ((EXP, 2),), 1)
    framed = jnp.pad(framed, ((0, 0), (0, 0), (0, 0), (1, 1), (0, 0)))
    first = apply_kernel(time_patches(framed, height, breadth), conv_time) + bias_time
    active = jax.nn.silu(first).astype(jnp.bfloat16).reshape(-1, height, breadth, channels)
    bordered = extended(active, ((EXP, 1),), 1)
    bordered = jnp.pad(bordered, ((0, 0), (0, 0), (1, 1), (0, 0)))
    second = apply_kernel(space_patches(bordered, height, breadth), conv_space)
    result = fine.astype(jnp.float32).reshape(-1, channels) + second + bias_space
    return result.astype(jnp.bfloat16).reshape(fine.shape)


def solution(mesh):
    finer = Mesh(mesh.devices.reshape(mesh.shape["sess"], 4, 2), ("sess", "exp_0", "exp_1"))
    return jax.shard_map(
        body,
        mesh=finer,
        in_specs=(
            P("sess", None, None),
            P("sess", None, None),
            P("sess", None, None),
            P("sess", None, EXP),
            P("sess", None, EXP),
            P("sess", EXP, None),
            P(),
            P(),
            P(),
            P(),
            P(),
            P(),
            P(None, "sess", EXP, None, None),
            P("sess"),
        ),
        out_specs=P("sess", EXP, None, None),
        check_vma=False,
    )
```

profile of v0, /device:TPU:64, one launch (start us, length us, event | category | flops | bytes accessed | tf_op | source)
XLA Modules:
  0.0 496.7 jit_solution(864282610397550757)
XLA Ops:
  11.6 3.2 reduce-window.6
  22.8 7.2 %scatter_custom_fusion = bf16[1024,512]{1,0:T(8,128)(2,1)} fusion(s32[512]{0:T(512)S(1)} %bitcast.109, bf16[256,512]{1,0:T(8,128)(2,1)} %dynamic-slice_bitcast_fusion, s32[1024]{0:T(1024)} %pad_clamp_fusion.1, bf16[]{:T(256)} %constant.61.clone.1), kind=kCustom, calls=%fused_computation.26 | custom fusion | bytes 1049088 | tf_op jit(solution)/shard_map/scatter | solution.py:132
  29.9 39.2 %all_to_all.15 = bf16[32,32,512]{2,1,0:T(8,128)(2,1)} all-to-all(bf16[32,32,512]{2,1,0:T(8,128)(2,1)} %bitcast.87), channel_id=1, replica_groups=mesh['sess'=32,'exp_0'=4,'exp_1'=2] {'sess'}, dimensions={0} | all-to-all | bytes 2097152 | tf_op jit(solution)/shard_map/all_to_all | solution.py:134
  69.4 167.9 %all-gather.2.cloned.1.call-done = bf16[32,32,4096]{2,1,0:T(8,128)(2,1)} async-done(((bf16[32,32,512]{2,1,0:T(8,128)(2,1)}), bf16[32,32,4096]{2,1,0:T(8,128)(2,1)}) %all-gather.2.cloned.1.call-update) | async-done | bytes 8388624 | tf_op jit(solution)/shard_map/all_gather | solution.py:135
  237.3 6.8 %fusion.3 = f32[1024,176]{0,1:T(8,128)S(1)} fusion(bf16[1024,4096]{1,0:T(8,128)(2,1)} %bitcast.114, bf16[1,4096,176]{1,2,0:T(8,128)(2,1)} %param.17), kind=kOutput, calls=%fused_computation.7 | convolution fusion | flops 1476395008 | bytes 10551296 | tf_op jit(solution)/shard_map/dot_general | solution.py:68
  244.2 3.0 fusion.8
  247.2 5.6 %convolution_convert_fusion = bf16[1024,4096]{1,0:T(8,128)(2,1)} fusion(bf16[1024,176]{0,1:T(8,128)(2,1)S(1)} %fusion.8, bf16[1,176,4096]{2,1,0:T(8,128)(2,1)S(1)} %copy-done.2), kind=kOutput, calls=%fused_computation.3 | convolution fusion | flops 1480589312 | bytes 10190848 | tf_op jit(solution)/shard_map/dot_general | solution.py:71
  252.8 84.3 %reduce-scatter.3.cloned.1.call-done = bf16[32,32,1024]{2,1,0:T(8,128)(2,1)} async-done(((bf16[32,32,4096]{2,1,0:T(8,128)(2,1)}), bf16[32,32,1024]{2,1,0:T(8,128)(2,1)}) %reduce-scatter.3.cloned.1.call-update) | async-done | bytes 2097168 | tf_op jit(solution)/shard_map/reduce_scatter | solution.py:18
  337.1 39.1 %reduce-scatter.5.cloned.1.call-done = bf16[32,32,512]{2,1,0:T(8,128)(2,1)} async-done(((bf16[32,32,1024]{2,1,0:T(8,128)(2,1)}), bf16[32,32,512]{2,1,0:T(8,128)(2,1)}) %reduce-scatter.5.cloned.1.call-update) | async-done | bytes 1048592 | tf_op jit(solution)/shard_map/reduce_scatter | solution.py:18
  376.3 9.7 %all-to-all-start.1 = ((bf16[32,32,512]{2,1,0:T(8,128)(2,1)}), bf16[32,32,512]{2,1,0:T(8,128)(2,1)}, u32[]{:S(2)}, u32[]{:S(2)}) async-start(bf16[32,32,512]{2,1,0:T(8,128)(2,1)} %reduce-scatter.5.cloned.1.call-done), calls=%async_computation.3 | async-start | bytes 2097152 | tf_op jit(solution)/shard_map/all_to_all | solution.py:141
  388.7 25.7 %all-to-all-done.1 = bf16[32,32,512]{2,1,0:T(8,128)(2,1)} async-done(((bf16[32,32,512]{2,1,0:T(8,128)(2,1)}), bf16[32,32,512]{2,1,0:T(8,128)(2,1)}, u32[]{:S(2)}, u32[]{:S(2)}) %all-to-all-start.1) | async-done | bytes 1048608 | tf_op jit(solution)/shard_map/all_to_all | solution.py:141
  414.4 2.9 bitcast_convert_fusion
  417.3 4.3 gather_fusion
  421.6 2.8 gather.10
  424.4 2.6 multiply_reduce_fusion
  428.9 18.5 %psum.7 = f32[256]{0:T(256)S(1)} all-reduce(f32[256]{0:T(256)S(1)} %fusion.14), channel_id=1, replica_groups=mesh['sess'=32,'exp_0'=4,'exp_1'=2] {'exp_0','exp_1'}, use_global_device_ids=true, to_apply=%region_8.9 | all-reduce | flops 256 | bytes 2048 | tf_op jit(solution)/shard_map/psum | solution.py:149
  447.4 2.1 convolution_convert_fusion.1
  449.5 4.0 all-to-all-start.2
  453.5 1.8 fusion.20
  455.3 4.9 all-to-all-done.2
  464.1 2.6 collective-permute-start
  468.2 4.2 collective-permute-done.1
  476.2 4.5 collective-permute-start.2
  484.3 2.2 collective-permute-done.3
  (105 shorter events, 33.3 us)
Async XLA Ops:
  6.5 467.7 %copy-start = (bf16[3,3,3,256,256]{4,3,2,1,0:T(8,128)(2,1)S(1)}, bf16[3,3,3,256,256]{4,3,2,1,0:T(8,128)(2,1)}, u32[]{:S(2)}) copy-start(bf16[3,3,3,256,256]{4,3,2,1,0:T(8,128)(2,1)} %param.22) | copy-start | bytes 10616836
  6.5 230.8 %all-gather.2.cloned.1.call-start = ((), (), s32[]{:S(2)}) async-start(), calls=%async_computation.5 | async-start | bytes 9437184 | tf_op jit(solution)/shard_map/all_gather | solution.py:135
  69.2 268.0 %reduce-scatter.3.cloned.1.call-start = ((), (), s32[]{:S(2)}) async-start(), calls=%async_computation.6 | async-start | bytes 10485760 | tf_op jit(solution)/shard_map/reduce_scatter | solution.py:18
  237.3 6.8 %copy-start.9 = (bf16[32,32,4096]{2,1,0:T(8,128)(2,1)S(1)}, bf16[32,32,4096]{2,1,0:T(8,128)(2,1)}, u32[]{:S(2)}) copy-start(bf16[32,32,4096]{2,1,0:T(8,128)(2,1)} %all-gather.2.cloned.1.call-done) | copy-start | bytes 25165828
  237.3 6.8 %copy-start.10 = (bf16[1,4096,176]{1,2,0:T(8,128)(2,1)S(1)}, bf16[1,4096,176]{1,2,0:T(8,128)(2,1)}, u32[]{:S(2)}) copy-start(bf16[1,4096,176]{1,2,0:T(8,128)(2,1)} %param.18) | copy-start | bytes 4325380
  244.2 3.0 copy-start.2
  252.8 123.5 %reduce-scatter.5.cloned.1.call-start = ((), (), s32[]{:S(2)}) async-start(), calls=%async_computation.7 | async-start | bytes 3145728 | tf_op jit(solution)/shard_map/reduce_scatter | solution.py:18
  337.1 49.5 %copy-start.7 = (f32[1,256,2]{1,2,0:T(2,128)S(1)}, f32[1,256,2]{1,2,0:T(2,128)}, u32[]{:S(2)}) copy-start(f32[1,256,2]{1,2,0:T(2,128)} %param.16) | copy-start | bytes 6148
  376.3 38.1 %all-to-all-start.1 = ((bf16[32,32,512]{2,1,0:T(8,128)(2,1)}), bf16[32,32,512]{2,1,0:T(8,128)(2,1)}, u32[]{:S(2)}, u32[]{:S(2)}) async-start(bf16[32,32,512]{2,1,0:T(8,128)(2,1)} %reduce-scatter.5.cloned.1.call-done), calls=%async_computation.3 | async-start | bytes 2097152 | tf_op jit(solution)/shard_map/all_to_all | solution.py:141
  427.0 0.8 copy-start.1
  449.5 10.7 %all-to-all-start.2 = ((bf16[8,32,256]{2,1,0:T(8,128)(2,1)}), bf16[8,32,256]{2,1,0:T(8,128)(2,1)}, u32[]{:S(2)}, u32[]{:S(2)}) async-start(bf16[8,32,256]{2,1,0:T(8,128)(2,1)} %bitcast.97), calls=%async_computation.4 | async-start | bytes 262144 | tf_op jit(solution)/shard_map/all_to_all | solution.py:29
  464.1 4.2 collective-permute-start
  466.7 5.7 %collective-permute-start.1 = (bf16[3,1,1,16,256]{4,3,2,1,0:T(8,128)(2,1)S(1)}, bf16[3,1,1,16,256]{4,3,2,1,0:T(8,128)(2,1)S(1)}, u32[]{:S(2)}, u32[]{:S(2)}) collective-permute-start(bf16[3,1,1,16,256]{4,3,2,1,0:T(8,128)(2,1)S(1)} %get-tuple-element.11), channel_id=1, source_target_pairs={{1,0},{2,1},{3,2},{4,3},{5,4},{6,5},{7,6},{9,8},{10,9},{11,10},{12... | collective-permute-start | bytes 73736 | tf_op jit(solution)/shard_map/ppermute | solution.py:43
  473.6 0.7 copy-start.8
  475.0 0.6 copy-start.3
  476.2 8.2 %collective-permute-start.2 = (bf16[1,1,16,256]{3,2,1,0:T(8,128)(2,1)}, bf16[1,1,16,256]{3,2,1,0:T(8,128)(2,1)}, u32[]{:S(2)}, u32[]{:S(2)}) collective-permute-start(bf16[1,1,16,256]{3,2,1,0:T(8,128)(2,1)} %get-tuple-element.20), channel_id=1, source_target_pairs={{0,1},{1,2},{2,3},{3,4},{4,5},{5,6},{6,7},{8,9},{9,10},{10,11},{11... | collective-permute-start | bytes 24584 | tf_op jit(solution)/shard_map/ppermute | solution.py:41
  480.7 5.8 %collective-permute-start.3 = (bf16[1,1,16,256]{3,2,1,0:T(8,128)(2,1)}, bf16[1,1,16,256]{3,2,1,0:T(8,128)(2,1)}, u32[]{:S(2)}, u32[]{:S(2)}) collective-permute-start(bf16[1,1,16,256]{3,2,1,0:T(8,128)(2,1)} %get-tuple-element.21), channel_id=1, source_target_pairs={{1,0},{2,1},{3,2},{4,3},{5,4},{6,5},{7,6},{9,8},{10,9},{11,10},{12... | collective-permute-start | bytes 24584 | tf_op jit(solution)/shard_map/ppermute | solution.py:43
  484.3 4.1 copy-start.4
  484.3 4.2 copy-start.5
  484.3 4.2 copy-start.6
Sparse Core Ops, SparseCore 0:
  69.3 167.9 all-gather.1
  252.9 84.1 reduce-scatter.2
  339.6 36.5 reduce-scatter.4
where the time goes:
time: 501 us; the launch traced here: 497 us
  waiting for transfers between devices  329 us (66%)
  blocking collectives  57.6 us (11%)
  local copies, waits for them, and re-layouts  32.4 us (6%)
  starting transfers between devices  23.7 us (5%)
  other arithmetic  20.3 us (4%)
  matrix products  19.8 us (4%)
  between operations  14.3 us (3%)
    all_gather x1, waiting for transfers between devices, body(): joined = lax.all_gather(arrived, EXP, axis=2, tiled=True)  168 us
    reduce_scatter x2, waiting for transfers between devices, summed_rows(): x = lax.psum_scatter(x, axis, scatter_dimension=dim, tiled=True)  123 us
    all_to_all x1, blocking collectives, body(): lax.all_to_all(outgoing, 'sess', split_axis=0, concat_axis=0, tiled=True)  39.2 us
    all_to_all x1, waiting for transfers between devices, body(): lax.all_to_all(reduced.astype(jnp.bfloat16), 'sess', split_axis=0, concat...  25.7 us
    psum x1, blocking collectives, body(): lax.psum(jnp.sum(jnp.square(feat.astype(jnp.float32)), axis=-1), EXP)  18.5 us
  transfers between devices with their start and end apart: 9, of which 8 were waited for; matrix products, arithmetic and copies ran while one was open for 1% of the time, Pallas kernels for 0%

commit v1 on v0

v1 whole, which is shorter than its diff:
```python
import jax
import jax.numpy as jnp
from jax import lax
from jax.experimental import pallas as pl
from jax.experimental.pallas import tpu as pltpu
from jax.sharding import Mesh
from jax.sharding import PartitionSpec as P

EXP = ("yh", "yl", "x")
EPS = 1e-06
F32 = jnp.float32
BF16 = jnp.bfloat16
PARAMS = pltpu.CompilerParams(vmem_limit_bytes=48 * 1024 * 1024)


def whole(shape):
    zeros = (0,) * len(shape)
    return pl.BlockSpec(shape, lambda i, s: zeros)


def call(kernel, name, scalars, operands, specs, outs, scratch=(), aliases=None):
    single = not isinstance(outs, (list, tuple))
    out_list = [outs] if single else list(outs)
    result = pl.pallas_call(
        kernel,
        name=name,
        out_shape=out_list,
        grid_spec=pltpu.PrefetchScalarGridSpec(
            num_scalar_prefetch=1,
            grid=(1,),
            in_specs=specs,
            out_specs=[whole(o.shape) for o in out_list],
            scratch_shapes=list(scratch),
        ),
        compiler_params=PARAMS,
        input_output_aliases=aliases or {},
    )(scalars, *operands)
    return result[0] if single else result


def iota(shape, dim):
    return lax.broadcasted_iota(jnp.int32, shape, dim)


def dispatch_kernel(sc, routes_ref, gates_ref, tok_ref, out_ref, col_ref):
    half = sc[1]
    count = routes_ref.shape[1]
    rows = out_ref.shape[0]
    experts = iota((32, count), 0)
    first = routes_ref[0:1, :]
    second = routes_ref[1:2, :]
    is_first = experts == first
    is_second = experts == second
    named = jnp.where(is_first | is_second, 1.0, 0.0).astype(BF16)
    earlier = jnp.where(iota((count, count), 0) < iota((count, count), 1), 1.0, 0.0).astype(BF16)
    before = jnp.dot(named, earlier, preferred_element_type=F32)
    pos_a = jnp.sum(jnp.where(is_first, before, 0.0), axis=0, keepdims=True).astype(jnp.int32)
    pos_b = jnp.sum(jnp.where(is_second, before, 0.0), axis=0, keepdims=True).astype(jnp.int32)
    place_a = (pos_a >> 4) * rows + first * 16 + (pos_a & 15)
    place_b = (pos_b >> 4) * rows + second * 16 + (pos_b & 15)
    slot = iota((rows, count), 0) + half * rows
    pick = jnp.where((slot == place_a) | (slot == place_b), 1.0, 0.0).astype(BF16)
    out_ref[...] = jnp.dot(pick, tok_ref[...], preferred_element_type=F32).astype(BF16)
    line = iota((128, count), 0)
    table = jnp.where(
        line == 0,
        place_a.astype(F32),
        jnp.where(
            line == 1,
            place_b.astype(F32),
            jnp.where(line == 2, gates_ref[0:1, :], jnp.where(line == 3, gates_ref[1:2, :], 0.0)),
        ),
    )
    col_ref[...] = table.T


def weights_kernel(sc, col_ref, high_ref, low_ref):
    slot = iota(high_ref.shape, 1)
    place_a = col_ref[:, 0:1].astype(jnp.int32)
    place_b = col_ref[:, 1:2].astype(jnp.int32)
    gate = jnp.where(slot == place_a, col_ref[:, 2:3], 0.0) + jnp.where(
        slot == place_b, col_ref[:, 3:4], 0.0
    )
    high = gate.astype(BF16)
    high_ref[...] = high
    low_ref[...] = (gate - high.astype(F32)).astype(BF16)


def product(rows, weights):
    return lax.dot_general(rows, weights, (((1,), (1,)), ((), ())), preferred_element_type=F32)


def joined_weights(refs, gate_w, up_w):
    own_gate, other_gate, own_up, other_up = refs
    part = own_gate.shape[0]
    gate_w[0:part, :] = own_gate[...]
    gate_w[part : 2 * part, :] = other_gate[...]
    up_w[0:part, :] = own_up[...]
    up_w[part : 2 * part, :] = other_up[...]


def start_kernel(sc, x_ref, w0, w1, w2, w3, gate_ref, up_ref, gate_w, up_w):
    joined_weights((w0, w1, w2, w3), gate_w, up_w)
    gate_ref[...] = product(x_ref[...], gate_w[...])
    up_ref[...] = product(x_ref[...], up_w[...])


def more_kernel(sc, x_ref, w0, w1, w2, w3, gate_in, up_in, gate_ref, up_ref, gate_w, up_w):
    joined_weights((w0, w1, w2, w3), gate_w, up_w)
    gate_ref[...] = gate_in[...] + product(x_ref[...], gate_w[...])
    up_ref[...] = up_in[...] + product(x_ref[...], up_w[...])


def last_kernel(sc, top_ref, low_ref, w0, w1, w2, w3, gate_in, up_in, out_ref, gate_w, up_w):
    joined_weights((w0, w1, w2, w3), gate_w, up_w)
    middle = top_ref.shape[0]
    for ref, begin in ((top_ref, 0), (low_ref, middle)):
        rows = slice(begin, begin + middle)
        gate = gate_in[rows, :] + product(ref[...], gate_w[...])
        up = up_in[rows, :] + product(ref[...], up_w[...])
        out_ref[rows, :] = (gate / (1.0 + jnp.exp(-gate)) * up).astype(BF16)


def down_kernel(sc, h0, h1, h2, h3, wd_ref, out_ref):
    share = out_ref.shape[2]
    for part in range(2):
        cols = slice(part * share, (part + 1) * share)
        total = jnp.dot(h0[...], wd_ref[0, :, cols], preferred_element_type=F32)
        total += jnp.dot(h1[...], wd_ref[1, :, cols], preferred_element_type=F32)
        total += jnp.dot(h2[...], wd_ref[2, :, cols], preferred_element_type=F32)
        total += jnp.dot(h3[...], wd_ref[3, :, cols], preferred_element_type=F32)
        out_ref[part] = total.astype(BF16)


def combine_kernel(sc, ret_ref, high_ref, low_ref, tok_ref, gain_ref, proj_ref, out_ref):
    mixed = jnp.dot(high_ref[...], ret_ref[...], preferred_element_type=F32)
    mixed += jnp.dot(low_ref[...], ret_ref[...], preferred_element_type=F32)
    feat = (tok_ref[...].astype(F32) + mixed).astype(BF16).astype(F32)
    square = jnp.sum(feat * feat, axis=1, keepdims=True)
    part = jnp.dot(
        (feat * gain_ref[...]).astype(BF16), proj_ref[...], preferred_element_type=F32
    )
    tiles, block, _ = out_ref.shape
    count, channels = part.shape
    lane = iota((count, 128), 1)
    high = square.astype(BF16).astype(F32)
    extra = jnp.where(lane == 0, high, jnp.where(lane == 1, square - high, 0.0))
    own = count // tiles
    border = (block - own) // 2
    for tile in range(tiles):
        begin = tile * own - border
        low, top = max(begin, 0), min(begin + block, count)
        for value, cols in (
            (part, slice(0, channels)),
            (extra, slice(channels, channels + 128)),
        ):
            pieces = [value[low:top, :]]
            if low > begin:
                pieces = [jnp.zeros((low - begin, value.shape[1]), F32)] + pieces
            if top < begin + block:
                pieces = pieces + [jnp.zeros((begin + block - top, value.shape[1]), F32)]
            joined = pieces[0] if len(pieces) == 1 else jnp.concatenate(pieces, axis=0)
            out_ref[tile, :, cols] = joined.astype(BF16)


def convolved(field, weights, rows):
    sums = []
    for col_step in range(3):
        total = None
        for row_step in range(3):
            term = jnp.dot(
                field[row_step * 16 : row_step * 16 + rows, :],
                weights(row_step, col_step),
                preferred_element_type=F32,
            )
            total = term if total is None else total + term
        sums.append(total)
    col = iota(sums[0].shape, 0) & 15
    left = jnp.where(col == 0, 0.0, pltpu.roll(sums[0], 1, 0))
    right = jnp.where(col == 15, 0.0, pltpu.roll(sums[2], rows - 1, 0))
    return sums[1] + left + right


def cache_kernel(sc, cache_ref, above_ref, below_ref, weight_ref, bias_ref, out_ref):
    head = sc[2]
    older = lax.rem(head + 2, 3)
    total = jnp.broadcast_to(bias_ref[...], out_ref.shape)
    for step, slot in ((0, older), (1, head)):
        field = jnp.concatenate([above_ref[slot], cache_ref[slot], below_ref[slot]], axis=0)
        total = total + convolved(field, lambda r, c: weight_ref[step, r, c], out_ref.shape[0])
    out_ref[...] = total


def tail_kernel(sc, arr_ref, past_ref, time_ref, space_ref, bias_ref, out_ref):
    tile = sc[0]
    total = arr_ref[0].astype(F32)
    for source in range(1, arr_ref.shape[0]):
        total = total + arr_ref[source].astype(F32)
    channels = out_ref.shape[1]
    square = total[:, channels : channels + 1] + total[:, channels + 1 : channels + 2]
    scale = lax.rsqrt(square / 4096.0 + EPS)
    coarse = (total[:, :channels] * scale).astype(BF16)
    block = coarse.shape[0]
    pixel = iota((4 * block, block), 0)
    spread = jnp.where(
        iota((4 * block, block), 1) == (pixel >> 5) * 8 + ((pixel & 15) >> 1), 1.0, 0.0
    ).astype(BF16)
    fine = jnp.dot(spread, coarse, preferred_element_type=F32)
    field = fine.astype(BF16)
    rows = past_ref.shape[0]
    first = past_ref[...] + convolved(field, lambda r, c: time_ref[0, r, c], rows)
    active = first / (1.0 + jnp.exp(-first))
    place = (iota(active.shape, 0) >> 4) + tile * 8 - 1
    active = jnp.where((place >= 0) & (place < 64), active, 0.0).astype(BF16)
    own = out_ref.shape[0]
    second = convolved(active, lambda r, c: space_ref[r, c], own)
    out_ref[...] = (fine[32 : 32 + own, :] + second + bias_ref[...]).astype(BF16)


def swapped(x, axis):
    return lax.ppermute(x, axis, [(0, 1), (1, 0)])


def body(
    tokens,
    routes,
    gates,
    w_gate,
    w_up,
    w_down,
    feat_gain,
    w_proj,
    conv_time,
    bias_time,
    conv_space,
    bias_space,
    frame_cache,
    cache_head,
):
    tile = lax.axis_index(EXP).astype(jnp.int32)
    half, quarter = tile >> 2, tile & 3
    scalars = jnp.stack([tile, half, cache_head[0], quarter, quarter ^ 1, quarter ^ 2, quarter ^ 3])
    count, width = tokens.shape[1:]
    hid = w_gate.shape[2]
    channels = w_proj.shape[1]
    fourth = width // 4
    share = width // 8
    own_gate, own_up = w_gate[0].T, w_up[0].T

    with jax.named_scope("exchange_weights"):
        pairs = [(i, i ^ 6) for i in range(8)]
        other_gate = lax.ppermute(own_gate, EXP, pairs)
        other_up = lax.ppermute(own_up, EXP, pairs)
        slabs = jnp.moveaxis(w_down[0].reshape(hid, 4, fourth), 1, 0)
        slabs = jnp.concatenate([slabs, slabs], axis=0)
        down = lax.all_to_all(slabs, EXP, 0, 0, tiled=True)
        order = [tile, tile ^ 6, tile ^ 2, tile ^ 4, tile ^ 1, tile ^ 7, tile ^ 3, tile ^ 5]
        down = jnp.concatenate(
            [lax.dynamic_slice_in_dim(down, i, 1, 0) for i in order], axis=0
        ).reshape(4, 2 * hid, fourth)

    with jax.named_scope("cache"):
        frames = frame_cache.reshape(3, 128, channels)
        above = lax.ppermute(frames[:, 96:], EXP, [(i, i + 1) for i in range(7)])
        below = lax.ppermute(frames[:, :32], EXP, [(i + 1, i) for i in range(7)])
        past = call(
            cache_kernel,
            "cache",
            scalars,
            (frames, above, below, conv_time, bias_time.reshape(1, channels)),
            [
                whole(frames.shape),
                whole(above.shape),
                whole(below.shape),
                pl.BlockSpec((2, 3, 3, channels, channels), lambda i, s: (0, 0, 0, 0, 0)),
                whole((1, channels)),
            ],
            jax.ShapeDtypeStruct((160, channels), F32),
        )

    with jax.named_scope("dispatch"):
        outgoing, columns = call(
            dispatch_kernel,
            "dispatch",
            scalars,
            (routes[0].T, gates[0].T, tokens[0]),
            [
                whole((2, count)),
                whole((2, count)),
                pl.BlockSpec((count, fourth), lambda i, s: (0, s[3])),
            ],
            [
                jax.ShapeDtypeStruct((512, fourth), BF16),
                jax.ShapeDtypeStruct((count, 128), F32),
            ],
        )
        arrived = lax.all_to_all(
            outgoing.reshape(32, 16, fourth), "sess", 0, 0, tiled=True
        ).reshape(512, fourth)
        high, low = call(
            weights_kernel,
            "weights",
            scalars,
            (columns,),
            [whole((count, 128))],
            [jax.ShapeDtypeStruct((count, 1024), BF16)] * 2,
        )

    with jax.named_scope("gather"):
        from_y = swapped(arrived, "yl")
        from_x = swapped(arrived, "x")
        corner_top = swapped(from_y[:256], "x")
        corner_low = swapped(from_x[256:], "yl")

    with jax.named_scope("experts"):
        weights = (own_gate, other_gate, own_up, other_up)
        pair = [jax.ShapeDtypeStruct((512, 2 * hid), F32)] * 2
        scratch = [pltpu.VMEM((2 * hid, fourth), BF16)] * 2
        rows = whole((512, fourth))
        acc = whole((512, 2 * hid))

        def columns_of(which):
            return [pl.BlockSpec((hid, fourth), lambda i, s: (0, s[which]))] * 4

        gate, up = call(
            start_kernel, "start", scalars, (arrived, *weights), [rows] + columns_of(3), pair, scratch
        )
        for name, piece, which in (("from_x", from_x, 4), ("from_y", from_y, 5)):
            gate, up = call(
                more_kernel,
                name,
                scalars,
                (piece, *weights, gate, up),
                [rows] + columns_of(which) + [acc, acc],
                pair,
                scratch,
                {6: 0, 7: 1},
            )
        hidden = call(
            last_kernel,
            "hidden",
            scalars,
            (corner_top, corner_low, *weights, gate, up),
            [whole((256, fourth))] * 2 + columns_of(6) + [acc, acc],
            jax.ShapeDtypeStruct((512, 2 * hid), BF16),
            scratch,
        )

    with jax.named_scope("hidden_gather"):
        hidden_y = swapped(hidden, "yl")
        hidden_x = swapped(hidden, "x")
        hidden_c = lax.ppermute(hidden, ("yl", "x"), [(i, 3 - i) for i in range(4)])

    with jax.named_scope("down"):
        answer = call(
            down_kernel,
            "down",
            scalars,
            (hidden, hidden_y, hidden_x, hidden_c, down),
            [whole((512, 2 * hid))] * 4 + [whole(down.shape)],
            jax.ShapeDtypeStruct((2, 512, share), BF16),
        )
        returned = lax.all_to_all(
            answer.reshape(64, 16, share), ("yh", "sess"), 0, 0, tiled=True
        ).reshape(1024, share)

    with jax.named_scope("combine"):
        blocks = call(
            combine_kernel,
            "combine",
            scalars,
            (returned, high, low, tokens[0], feat_gain.reshape(1, width), w_proj),
            [
                whole((1024, share)),
                whole((count, 1024)),
                whole((count, 1024)),
                pl.BlockSpec((count, share), lambda i, s: (0, s[3] * 2 + s[1])),
                pl.BlockSpec((1, share), lambda i, s: (0, s[3] * 2 + s[1])),
                pl.BlockSpec((share, channels), lambda i, s: (s[3] * 2 + s[1], 0)),
            ],
            jax.ShapeDtypeStruct((8, 48, channels + 128), BF16),
        )
        blocks = lax.all_to_all(blocks, EXP, 0, 0, tiled=True)

    with jax.named_scope("decode"):
        out = call(
            tail_kernel,
            "decode",
            scalars,
            (blocks, past, conv_time, conv_space, bias_space.reshape(1, channels)),
            [
                whole(blocks.shape),
                whole((160, channels)),
                pl.BlockSpec((1, 3, 3, channels, channels), lambda i, s: (2, 0, 0, 0, 0)),
                whole(conv_space.shape),
                whole((1, channels)),
            ],
            jax.ShapeDtypeStruct((128, channels), BF16),
        )
    return out.reshape(1, 8, 16, channels)


def solution(mesh):
    finer = Mesh(
        mesh.devices.reshape(mesh.shape["sess"], 2, 2, 2), ("sess", "yh", "yl", "x")
    )
    return jax.shard_map(
        body,
        mesh=finer,
        in_specs=(
            P("sess", None, None),
            P("sess", None, None),
            P("sess", None, None),
            P("sess", None, EXP),
            P("sess", None, EXP),
            P("sess", EXP, None),
            P(),
            P(),
            P(),
            P(),
            P(),
            P(),
            P(None, "sess", EXP, None, None),
            P("sess"),
        ),
        out_specs=P("sess", EXP, None, None),
        check_vma=False,
    )
```

time: 501 us -> 272 us (0.54)
  waiting for transfers between devices: 329 us -> 158 us
  blocking collectives: 57.6 us -> 0 us
  Pallas kernels: 0 us -> 26.6 us
  starting transfers between devices: 23.7 us -> 43.9 us
  matrix products: 19.8 us -> 0 us
  other arithmetic: 20.3 us -> 1.85 us
  between operations: 14.3 us -> 0.87 us
    all_gather x1 -> x0, waiting for transfers between devices: 168 us -> none  [body(): joined = lax.all_gather(arrived, EXP, axis=2, tiled=True)]
    reduce_scatter x2 -> x0, waiting for transfers between devices: 123 us -> none  [summed_rows(): x = lax.psum_scatter(x, axis, scatter_dimension=dim, tiled=True)]
    ppermute x4 -> x11, waiting for transfers between devices: 6.62 us -> 109 us  [the longest x1 61.3 us: body(): other_gate = lax.ppermute(own_gate, EXP, pairs)]
    all_to_all x1 -> x0, blocking collectives: 39.2 us -> none  [body(): lax.all_to_all(outgoing, 'sess', split_axis=0, concat_axis=0, tiled=True)]
    pallas_call x0 -> x10, Pallas kernels: none -> 26.6 us  [call(): pl.pallas_call(kernel, name=name, out_shape=out_list, grid_spec=pltpu.Pre...]
    unnamed x57 -> x59, local copies, waits for them, and re-layouts: 3.54 us -> 26.9 us
    dot_general x6 -> x0, matrix products: 19.8 us -> none  [the longest x1 6.83 us: expert_rows(): gate = jnp.dot(flat_rows, w_gate[0], preferred_element_type=jnp.float32)]
    all_to_all x2 -> x4, waiting for transfers between devices: 30.6 us -> 49.2 us  [the longest x1 26.6 us: body(): lax.all_to_all(answer.reshape(64, 16, share), ('yh', 'sess'), 0, 0, tiled...]
  transfers between devices with their start and end apart: 9 -> 15, of which waited for: 8 -> 10; matrix products, arithmetic and copies ran while one was open for 1% -> 7% of each run, Pallas kernels for 0% -> 4%
where the time goes in v1:
time: 272 us; the launch traced here: 268 us
  waiting for transfers between devices  158 us (58%)
  starting transfers between devices  43.9 us (16%)
  local copies, waits for them, and re-layouts  36.5 us (13%)
  Pallas kernels  26.6 us (10%)
    ppermute x1, waiting for transfers between devices, body(): other_gate = lax.ppermute(own_gate, EXP, pairs)  61.3 us
    ppermute x1, waiting for transfers between devices, body(): other_up = lax.ppermute(own_up, EXP, pairs)  29.2 us
    unnamed x59, local copies, waits for them, and re-layouts  26.9 us
    pallas_call x10, Pallas kernels, call(): pl.pallas_call(kernel, name=name, out_shape=out_list, grid_spec=pltpu.Pre...  26.6 us
    all_to_all x1, waiting for transfers between devices, body(): lax.all_to_all(answer.reshape(64, 16, share), ('yh', 'sess'), 0, 0, tiled...  26.6 us
    all_to_all x1, waiting for transfers between devices, body(): lax.all_to_all(outgoing.reshape(32, 16, fourth), 'sess', 0, 0, tiled=True)  22.6 us
    all_to_all x1, starting transfers between devices, body(): lax.all_to_all(outgoing.reshape(32, 16, fourth), 'sess', 0, 0, tiled=True)  10.7 us
    all_to_all x1, starting transfers between devices, body(): lax.all_to_all(answer.reshape(64, 16, share), ('yh', 'sess'), 0, 0, tiled...  8.23 us
  transfers between devices with their start and end apart: 15, of which 10 were waited for; matrix products, arithmetic and copies ran while one was open for 7% of the time, Pallas kernels for 4%

profile of v1, /device:TPU:64, one launch (start us, length us, event | category | flops | bytes accessed | tf_op | source)
XLA Modules:
  0.0 267.7 jit_solution(15666957669401975334)
XLA Ops:
  3.7 2.1 dispatch.1
  5.8 10.7 %all-to-all-start = ((bf16[32,16,1024]{2,1,0:T(8,128)(2,1)}), bf16[32,16,1024]{2,1,0:T(8,128)(2,1)S(1)}, u32[]{:S(2)}, u32[]{:S(2)}) async-start(bf16[32,16,1024]{2,1,0:T(8,128)(2,1)} %bitcast.11), calls=%async_computation | async-start | bytes 2097152 | tf_op jit(solution)/shard_map/dispatch/all_to_all | solution.py:297
  16.6 3.5 %squeeze.24 = bf16[176,4,1024]{2,1,0:T(4,128)(2,1)S(1)} reshape(bf16[1,176,4096]{2,1,0:T(8,128)(2,1)} %param.19) | data formatting | bytes 2883584 | tf_op jit(solution)/shard_map/exchange_weights/reshape;exchange_weights/squeeze | solution.py:254
  22.3 22.6 %all-to-all-done = bf16[32,16,1024]{2,1,0:T(8,128)(2,1)S(1)} async-done(((bf16[32,16,1024]{2,1,0:T(8,128)(2,1)}), bf16[32,16,1024]{2,1,0:T(8,128)(2,1)S(1)}, u32[]{:S(2)}, u32[]{:S(2)}) %all-to-all-start) | async-done | bytes 1048608 | tf_op jit(solution)/shard_map/dispatch/all_to_all | solution.py:297
  45.9 4.5 %all-to-all-start.1 = ((bf16[8,176,1024]{2,1,0:T(8,128)(2,1)}), bf16[8,176,1024]{2,1,0:T(8,128)(2,1)}, u32[]{:S(2)}, u32[]{:S(2)}) async-start(bf16[8,176,1024]{2,1,0:T(8,128)(2,1)} %pad_maximum_fusion), calls=%async_computation.1 | async-start | bytes 5767168 | tf_op jit(solution)/shard_map/exchange_weights/all_to_all | solution.py:256
  50.4 3.2 %collective-permute-start.4 = (bf16[176,4096]{1,0:T(8,128)(2,1)S(1)}, bf16[176,4096]{1,0:T(8,128)(2,1)S(1)}, u32[]{:S(2)}, u32[]{:S(2)}) collective-permute-start(bf16[176,4096]{1,0:T(8,128)(2,1)S(1)} %bitcast.32), channel_id=1, source_target_pairs={{0,6},{1,7},{2,4},{3,5},{4,2},{5,3},{6,0},{7,1},{8,14},{9,15},{10,... | collective-permute-start | bytes 4325384 | tf_op jit(solution)/shard_map/exchange_weights/ppermute | solution.py:252
  55.9 61.3 %collective-permute-done.4.w1 = bf16[176,4096]{1,0:T(8,128)(2,1)S(1)} collective-permute-done((bf16[176,4096]{1,0:T(8,128)(2,1)S(1)}, bf16[176,4096]{1,0:T(8,128)(2,1)S(1)}, u32[]{:S(2)}, u32[]{:S(2)}) %collective-permute-start.4) | collective-permute-done | bytes 1441824 | tf_op jit(solution)/shard_map/exchange_weights/ppermute | solution.py:252
  117.2 29.2 %collective-permute-done.5.w3 = bf16[176,4096]{1,0:T(8,128)(2,1)} collective-permute-done((bf16[176,4096]{1,0:T(8,128)(2,1)}, bf16[176,4096]{1,0:T(8,128)(2,1)}, u32[]{:S(2)}, u32[]{:S(2)}) %collective-permute-start.5) | collective-permute-done | bytes 1441824 | tf_op jit(solution)/shard_map/exchange_weights/ppermute | solution.py:253
  147.6 2.9 %start.1 = (f32[512,352]{1,0:T(8,128)S(1)}, f32[512,352]{1,0:T(8,128)S(1)}) custom-call(s32[7]{0:T(128)S(1)} %stack.27.sc, bf16[512,1024]{1,0:T(8,128)(2,1)S(1)} %bitcast.41, bf16[176,4096]{1,0:T(8,128)(2,1)S(1)} %bitcast.33, bf16[176,4096]{1,0:T(8,128)(2,1)S(1)} %collective-permute-done.4.w1, bf16[176,4096]{1,0:T(8,128)(2,1)} %bitcast.52, ...), custom_call_target="tpu_custom_call" | custom-call | tf_op jit(solution)/shard_map/experts/start/pallas_call | solution.py:24
  163.0 3.3 %from_x.1 = (f32[512,352]{1,0:T(8,128)S(1)}, f32[512,352]{1,0:T(8,128)S(1)}) custom-call(s32[7]{0:T(128)S(1)} %stack.27.sc, bf16[512,1024]{1,0:T(8,128)(2,1)} %collective-permute-done.2.x_ref, bf16[176,4096]{1,0:T(8,128)(2,1)S(1)} %bitcast.34, bf16[176,4096]{1,0:T(8,128)(2,1)S(1)} %collective-permute-done.4.w1, ...), custom_call_target="tpu_custom_call", output_to_operand_aliasing={{0}: (6, {}), {1}: (7, {})} | custom-call | tf_op jit(solution)/shard_map/experts/from_x/pallas_call | solution.py:24
  166.3 3.3 %from_y.1 = (f32[512,352]{1,0:T(8,128)S(1)}, f32[512,352]{1,0:T(8,128)S(1)}) custom-call(s32[7]{0:T(128)S(1)} %stack.27.sc, bf16[512,1024]{1,0:T(8,128)(2,1)} %collective-permute-done.x_ref, bf16[176,4096]{1,0:T(8,128)(2,1)S(1)} %bitcast.35, bf16[176,4096]{1,0:T(8,128)(2,1)S(1)} %collective-permute-done.4.w1, ...), custom_call_target="tpu_custom_call", output_to_operand_aliasing={{0}: (6, {}), {1}: (7, {})} | custom-call | tf_op jit(solution)/shard_map/experts/from_y/pallas_call | solution.py:24
  169.9 3.1 %hidden.1.h0 = bf16[512,352]{1,0:T(8,128)(2,1)S(1)} custom-call(s32[7]{0:T(128)S(1)} %stack.27.sc, bf16[256,1024]{1,0:T(8,128)(2,1)S(1)} %collective-permute-done.1.top_ref, bf16[256,1024]{1,0:T(8,128)(2,1)} %collective-permute-done.3.low_ref, bf16[176,4096]{1,0:T(8,128)(2,1)S(1)} %bitcast.36, bf16[176,4096]{1,0:T(8,128)(2,1)S(1)} %collective-permute-done.4.w1, ...), custom_call_target="tpu_custom_call" | custom-call | tf_op jit(solution)/shard_map/experts/hidden/pallas_call | solution.py:24
  172.9 2.0 collective-permute-start.6
  179.7 4.6 %collective-permute-done.6.h1 = bf16[512,352]{1,0:T(8,128)(2,1)S(1)} collective-permute-done((bf16[512,352]{1,0:T(8,128)(2,1)S(1)}, bf16[512,352]{1,0:T(8,128)(2,1)S(1)}, u32[]{:S(2)}, u32[]{:S(2)}) %collective-permute-start.6) | collective-permute-done | bytes 360480 | tf_op jit(solution)/shard_map/hidden_gather/ppermute | solution.py:221
  184.4 2.6 collective-permute-done.7.h2
  187.0 6.0 %collective-permute-done.8.h3 = bf16[512,352]{1,0:T(8,128)(2,1)S(1)} collective-permute-done((bf16[512,352]{1,0:T(8,128)(2,1)S(1)}, bf16[512,352]{1,0:T(8,128)(2,1)S(1)}, u32[]{:S(2)}, u32[]{:S(2)}) %collective-permute-start.8) | collective-permute-done | bytes 360480 | tf_op jit(solution)/shard_map/hidden_gather/ppermute | solution.py:352
  193.0 3.9 %down.1 = bf16[2,512,512]{2,1,0:T(8,128)(2,1)} custom-call(s32[7]{0:T(128)S(1)} %stack.27.sc, bf16[512,352]{1,0:T(8,128)(2,1)S(1)} %hidden.1.h0, bf16[512,352]{1,0:T(8,128)(2,1)S(1)} %collective-permute-done.6.h1, bf16[512,352]{1,0:T(8,128)(2,1)S(1)} %collective-permute-done.7.h2, bf16[512,352]{1,0:T(8,128)(2,1)S(1)} %collective-permute-done.8.h3, ...), custom_call_target="tpu_custom_call" | custom-call | tf_op jit(solution)/shard_map/down/down/pallas_call | solution.py:24
  196.9 8.2 %all-to-all-start.2 = ((bf16[64,16,512]{2,1,0:T(8,128)(2,1)}), bf16[64,16,512]{2,1,0:T(8,128)(2,1)S(1)}, u32[]{:S(2)}, u32[]{:S(2)}) async-start(bf16[64,16,512]{2,1,0:T(8,128)(2,1)} %bitcast.21), calls=%async_computation.2 | async-start | bytes 2097152 | tf_op jit(solution)/shard_map/down/all_to_all | solution.py:363
  207.8 26.6 %all-to-all-done.2 = bf16[64,16,512]{2,1,0:T(8,128)(2,1)S(1)} async-done(((bf16[64,16,512]{2,1,0:T(8,128)(2,1)}), bf16[64,16,512]{2,1,0:T(8,128)(2,1)S(1)}, u32[]{:S(2)}, u32[]{:S(2)}) %all-to-all-start.2) | async-done | bytes 1048608 | tf_op jit(solution)/shard_map/down/all_to_all | solution.py:363
  241.0 2.7 %combine.1 = bf16[8,48,384]{2,1,0:T(8,128)(2,1)S(1)} custom-call(s32[7]{0:T(128)S(1)} %stack.27.sc, bf16[1024,512]{1,0:T(8,128)(2,1)S(1)} %bitcast.42, bf16[256,1024]{1,0:T(8,128)(2,1)S(1)} %copy-done.17, bf16[256,1024]{1,0:T(8,128)(2,1)S(1)} %copy-done.19, bf16[256,4096]{1,0:T(8,128)(2,1)S(1)} %bitcast.38, f32[1,4096]{1,0:T(1,128)S(1)} %bitcast.46, ...), custom_call_target="tpu_custom_call" | custom-call | tf_op jit(solution)/shard_map/combine/combine/pallas_call | solution.py:24
  244.5 4.4 %all-to-all-start.3 = ((bf16[8,48,384]{2,1,0:T(8,128)(2,1)}), bf16[8,48,384]{2,1,0:T(8,128)(2,1)}, u32[]{:S(2)}, u32[]{:S(2)}) async-start(bf16[8,48,384]{2,1,0:T(8,128)(2,1)} %copy-done.13), calls=%async_computation.3 | async-start | bytes 589824 | tf_op jit(solution)/shard_map/combine/all_to_all | solution.py:383
  249.7 3.9 %collective-permute-start.9 = (bf16[3,32,256]{2,1,0:T(8,128)(2,1)S(1)}, bf16[3,32,256]{2,1,0:T(8,128)(2,1)S(1)}, u32[]{:S(2)}, u32[]{:S(2)}) collective-permute-start(bf16[3,32,256]{2,1,0:T(8,128)(2,1)S(1)} %get-tuple-element.26), channel_id=1, source_target_pairs={{0,1},{1,2},{2,3},{3,4},{4,5},{5,6},{6,7},{8,9},{9,10},{10,11},{11... | collective-permute-start | bytes 147464 | tf_op jit(solution)/shard_map/cache/ppermute | solution.py:264
  255.3 4.3 %collective-permute-done.10.below_ref = bf16[3,32,256]{2,1,0:T(8,128)(2,1)S(1)} collective-permute-done((bf16[3,32,256]{2,1,0:T(8,128)(2,1)S(1)}, bf16[3,32,256]{2,1,0:T(8,128)(2,1)S(1)}, u32[]{:S(2)}, u32[]{:S(2)}) %collective-permute-start.10) | collective-permute-done | bytes 49184 | tf_op jit(solution)/shard_map/cache/ppermute | solution.py:265
  264.5 3.2 %decode.1 = bf16[128,256]{1,0:T(8,128)(2,1)} custom-call(s32[7]{0:T(128)S(1)} %stack.27.sc, bf16[8,48,384]{2,1,0:T(8,128)(2,1)} %all-to-all-done.3.arr_ref, f32[160,256]{1,0:T(8,128)S(1)} %copy-done.15, bf16[3,3,3,256,256]{4,3,2,1,0:T(8,128)(2,1)S(1)} %copy-done.1, bf16[3,3,256,256]{3,2,1,0:T(8,128)(2,1)S(1)} %copy-done.12, f32[1,256]{1,0:T(1,128)S(1)} %bitcast.50), custom_call_target="tpu_custom_call" | custom-call | tf_op jit(solution)/shard_map/decode/decode/pallas_call | solution.py:24
  (83 shorter events, 44.7 us)
Async XLA Ops:
  0.7 1.6 copy-start.2
  5.8 39.1 %all-to-all-start = ((bf16[32,16,1024]{2,1,0:T(8,128)(2,1)}), bf16[32,16,1024]{2,1,0:T(8,128)(2,1)S(1)}, u32[]{:S(2)}, u32[]{:S(2)}) async-start(bf16[32,16,1024]{2,1,0:T(8,128)(2,1)} %bitcast.11), calls=%async_computation | async-start | bytes 2097152 | tf_op jit(solution)/shard_map/dispatch/all_to_all | solution.py:297
  22.3 28.1 %copy-start = (bf16[1,4096,176]{1,2,0:T(8,128)(2,1)S(1)}, bf16[1,4096,176]{1,2,0:T(8,128)(2,1)}, u32[]{:S(2)}) copy-start(bf16[1,4096,176]{1,2,0:T(8,128)(2,1)} %param.17) | copy-start | bytes 4325380
  45.9 111.8 %all-to-all-start.1 = ((bf16[8,176,1024]{2,1,0:T(8,128)(2,1)}), bf16[8,176,1024]{2,1,0:T(8,128)(2,1)}, u32[]{:S(2)}, u32[]{:S(2)}) async-start(bf16[8,176,1024]{2,1,0:T(8,128)(2,1)} %pad_maximum_fusion), calls=%async_computation.1 | async-start | bytes 5767168 | tf_op jit(solution)/shard_map/exchange_weights/all_to_all | solution.py:256
  50.4 66.8 %collective-permute-start.4 = (bf16[176,4096]{1,0:T(8,128)(2,1)S(1)}, bf16[176,4096]{1,0:T(8,128)(2,1)S(1)}, u32[]{:S(2)}, u32[]{:S(2)}) collective-permute-start(bf16[176,4096]{1,0:T(8,128)(2,1)S(1)} %bitcast.32), channel_id=1, source_target_pairs={{0,6},{1,7},{2,4},{3,5},{4,2},{5,3},{6,0},{7,1},{8,14},{9,15},{10,... | collective-permute-start | bytes 4325384 | tf_op jit(solution)/shard_map/exchange_weights/ppermute | solution.py:252
  53.6 92.8 %collective-permute-start.5 = (bf16[176,4096]{1,0:T(8,128)(2,1)}, bf16[176,4096]{1,0:T(8,128)(2,1)}, u32[]{:S(2)}, u32[]{:S(2)}) collective-permute-start(bf16[176,4096]{1,0:T(8,128)(2,1)} %bitcast.51), channel_id=1, source_target_pairs={{0,6},{1,7},{2,4},{3,5},{4,2},{5,3},{6,0},{7,1},{8,14},{9,15},{10,... | collective-permute-start | bytes 4325384 | tf_op jit(solution)/shard_map/exchange_weights/ppermute | solution.py:253
  53.7 98.6 %collective-permute-start = (bf16[512,1024]{1,0:T(8,128)(2,1)}, bf16[512,1024]{1,0:T(8,128)(2,1)}, u32[]{:S(2)}, u32[]{:S(2)}) collective-permute-start(bf16[512,1024]{1,0:T(8,128)(2,1)} %bitcast.39), channel_id=1, source_target_pairs={{0,2},{2,0},{1,3},{3,1},{4,6},{6,4},{5,7},{7,5},{8,10},{10,8},{9,1... | collective-permute-start | bytes 3145736 | tf_op jit(solution)/shard_map/gather/ppermute | solution.py:221
  54.5 101.2 %collective-permute-start.2 = (bf16[512,1024]{1,0:T(8,128)(2,1)}, bf16[512,1024]{1,0:T(8,128)(2,1)}, u32[]{:S(2)}, u32[]{:S(2)}) collective-permute-start(bf16[512,1024]{1,0:T(8,128)(2,1)} %bitcast.40), channel_id=1, source_target_pairs={{0,1},{1,0},{2,3},{3,2},{4,5},{5,4},{6,7},{7,6},{8,9},{9,8},{10,11... | collective-permute-start | bytes 3145736 | tf_op jit(solution)/shard_map/gather/ppermute | solution.py:221
  154.2 15.3 %collective-permute-start.1 = (bf16[256,1024]{1,0:T(8,128)(2,1)}, bf16[256,1024]{1,0:T(8,128)(2,1)S(1)}, u32[]{:S(2)}, u32[]{:S(2)}) collective-permute-start(bf16[256,1024]{1,0:T(8,128)(2,1)} %slice.16), channel_id=1, source_target_pairs={{0,1},{1,0},{2,3},{3,2},{4,5},{5,4},{6,7},{7,6},{8,9},{9,8},{10,11... | collective-permute-start | bytes 1572872 | tf_op jit(solution)/shard_map/gather/ppermute | solution.py:221
  157.5 12.4 %collective-permute-start.3 = (bf16[256,1024]{1,0:T(8,128)(2,1)}, bf16[256,1024]{1,0:T(8,128)(2,1)}, u32[]{:S(2)}, u32[]{:S(2)}) collective-permute-start(bf16[256,1024]{1,0:T(8,128)(2,1)} %slice.17), channel_id=1, source_target_pairs={{0,2},{2,0},{1,3},{3,1},{4,6},{6,4},{5,7},{7,5},{8,10},{10,8},{9,1... | collective-permute-start | bytes 1572872 | tf_op jit(solution)/shard_map/gather/ppermute | solution.py:221
  157.7 5.2 %copy-start.5 = (f32[512,352]{1,0:T(8,128)S(1)}, f32[512,352]{1,0:T(8,128)}, u32[]{:S(2)}) copy-start(f32[512,352]{1,0:T(8,128)} %copy-done.4) | copy-start | bytes 2162692
  157.7 5.2 %copy-start.7 = (f32[512,352]{1,0:T(8,128)S(1)}, f32[512,352]{1,0:T(8,128)}, u32[]{:S(2)}) copy-start(f32[512,352]{1,0:T(8,128)} %copy-done.6) | copy-start | bytes 2162692
  172.9 11.4 %collective-permute-start.6 = (bf16[512,352]{1,0:T(8,128)(2,1)S(1)}, bf16[512,352]{1,0:T(8,128)(2,1)S(1)}, u32[]{:S(2)}, u32[]{:S(2)}) collective-permute-start(bf16[512,352]{1,0:T(8,128)(2,1)S(1)} %hidden.1.h0), channel_id=1, source_target_pairs={{0,2},{2,0},{1,3},{3,1},{4,6},{6,4},{5,7},{7,5},{8,10},{10,8},{9,1... | collective-permute-start | bytes 1081352 | tf_op jit(solution)/shard_map/hidden_gather/ppermute | solution.py:221
  175.0 12.1 %collective-permute-start.7 = (bf16[512,352]{1,0:T(8,128)(2,1)S(1)}, bf16[512,352]{1,0:T(8,128)(2,1)S(1)}, u32[]{:S(2)}, u32[]{:S(2)}) collective-permute-start(bf16[512,352]{1,0:T(8,128)(2,1)S(1)} %hidden.1.h0), channel_id=1, source_target_pairs={{0,1},{1,0},{2,3},{3,2},{4,5},{5,4},{6,7},{7,6},{8,9},{9,8},{10,11... | collective-permute-start | bytes 1081352 | tf_op jit(solution)/shard_map/hidden_gather/ppermute | solution.py:221
  175.4 17.6 %collective-permute-start.8 = (bf16[512,352]{1,0:T(8,128)(2,1)S(1)}, bf16[512,352]{1,0:T(8,128)(2,1)S(1)}, u32[]{:S(2)}, u32[]{:S(2)}) collective-permute-start(bf16[512,352]{1,0:T(8,128)(2,1)S(1)} %hidden.1.h0), channel_id=1, source_target_pairs={{0,3},{1,2},{2,1},{3,0},{4,7},{5,6},{6,5},{7,4},{8,11},{9,10},{10,... | collective-permute-start | bytes 1081352 | tf_op jit(solution)/shard_map/hidden_gather/ppermute | solution.py:352
  196.9 37.6 %all-to-all-start.2 = ((bf16[64,16,512]{2,1,0:T(8,128)(2,1)}), bf16[64,16,512]{2,1,0:T(8,128)(2,1)S(1)}, u32[]{:S(2)}, u32[]{:S(2)}) async-start(bf16[64,16,512]{2,1,0:T(8,128)(2,1)} %bitcast.21), calls=%async_computation.2 | async-start | bytes 2097152 | tf_op jit(solution)/shard_map/down/all_to_all | solution.py:363
  235.4 1.6 copy-start.3
  241.0 18.5 %copy-start.1 = (bf16[3,3,3,256,256]{4,3,2,1,0:T(8,128)(2,1)S(1)}, bf16[3,3,3,256,256]{4,3,2,1,0:T(8,128)(2,1)}, u32[]{:S(2)}) copy-start(bf16[3,3,3,256,256]{4,3,2,1,0:T(8,128)(2,1)} %time_ref.1) | copy-start | bytes 10616836
  241.0 18.5 %copy-start.24 = (f32[256]{0:T(256)S(1)}, f32[256]{0:T(256)}, u32[]{:S(2)}) copy-start(f32[256]{0:T(256)} %param.23) | copy-start | bytes 3076
  244.5 17.8 %copy-start.25 = (f32[256]{0:T(256)S(1)}, f32[256]{0:T(256)}, u32[]{:S(2)}) copy-start(f32[256]{0:T(256)} %param.25) | copy-start | bytes 3076
  244.5 17.8 %all-to-all-start.3 = ((bf16[8,48,384]{2,1,0:T(8,128)(2,1)}), bf16[8,48,384]{2,1,0:T(8,128)(2,1)}, u32[]{:S(2)}, u32[]{:S(2)}) async-start(bf16[8,48,384]{2,1,0:T(8,128)(2,1)} %copy-done.13), calls=%async_computation.3 | async-start | bytes 589824 | tf_op jit(solution)/shard_map/combine/all_to_all | solution.py:383
  249.7 5.7 %collective-permute-start.9 = (bf16[3,32,256]{2,1,0:T(8,128)(2,1)S(1)}, bf16[3,32,256]{2,1,0:T(8,128)(2,1)S(1)}, u32[]{:S(2)}, u32[]{:S(2)}) collective-permute-start(bf16[3,32,256]{2,1,0:T(8,128)(2,1)S(1)} %get-tuple-element.26), channel_id=1, source_target_pairs={{0,1},{1,2},{2,3},{3,4},{4,5},{5,6},{6,7},{8,9},{9,10},{10,11},{11... | collective-permute-start | bytes 147464 | tf_op jit(solution)/shard_map/cache/ppermute | solution.py:264
  253.6 6.0 %collective-permute-start.10 = (bf16[3,32,256]{2,1,0:T(8,128)(2,1)S(1)}, bf16[3,32,256]{2,1,0:T(8,128)(2,1)S(1)}, u32[]{:S(2)}, u32[]{:S(2)}) collective-permute-start(bf16[3,32,256]{2,1,0:T(8,128)(2,1)S(1)} %get-tuple-element.25), channel_id=1, source_target_pairs={{1,0},{2,1},{3,2},{4,3},{5,4},{6,5},{7,6},{9,8},{10,9},{11,10},{12... | collective-permute-start | bytes 147464 | tf_op jit(solution)/shard_map/cache/ppermute | solution.py:265
  262.3 1.3 copy-start.12
  (17 other events, 15.2 us)

commit v2 on v1

--- a/solution.py
+++ b/solution.py
@@ -10,7 +10,6 @@
 EPS = 1e-06
 F32 = jnp.float32
 BF16 = jnp.bfloat16
-PARAMS = pltpu.CompilerParams(vmem_limit_bytes=48 * 1024 * 1024)
 
 
 def whole(shape):
@@ -18,7 +17,7 @@
     return pl.BlockSpec(shape, lambda i, s: zeros)
 
 
-def call(kernel, name, scalars, operands, specs, outs, scratch=(), aliases=None):
+def call(kernel, name, scalars, operands, specs, outs, scratch=(), limit=12, cost=None):
     single = not isinstance(outs, (list, tuple))
     out_list = [outs] if single else list(outs)
     result = pl.pallas_call(
@@ -32,8 +31,8 @@
             out_specs=[whole(o.shape) for o in out_list],
             scratch_shapes=list(scratch),
         ),
-        compiler_params=PARAMS,
-        input_output_aliases=aliases or {},
+        compiler_params=pltpu.CompilerParams(vmem_limit_bytes=limit * 1024 * 1024),
+        cost_estimate=cost,
     )(scalars, *operands)
     return result[0] if single else result
 
@@ -99,16 +98,19 @@
     up_w[part : 2 * part, :] = other_up[...]
 
 
-def start_kernel(sc, x_ref, w0, w1, w2, w3, gate_ref, up_ref, gate_w, up_w):
-    joined_weights((w0, w1, w2, w3), gate_w, up_w)
-    gate_ref[...] = product(x_ref[...], gate_w[...])
-    up_ref[...] = product(x_ref[...], up_w[...])
-
-
-def more_kernel(sc, x_ref, w0, w1, w2, w3, gate_in, up_in, gate_ref, up_ref, gate_w, up_w):
-    joined_weights((w0, w1, w2, w3), gate_w, up_w)
-    gate_ref[...] = gate_in[...] + product(x_ref[...], gate_w[...])
-    up_ref[...] = up_in[...] + product(x_ref[...], up_w[...])
+def first_kernel(sc, x0, x1, x2, w0, w1, w2, w3, gate_ref, up_ref, gate_w, up_w):
+    width = x0.shape[1]
+    for step, ref in enumerate((x0, x1, x2)):
+        cols = pl.ds(pl.multiple_of(sc[3 + step] * width, width), width)
+        joined_weights([w.at[:, cols] for w in (w0, w1, w2, w3)], gate_w, up_w)
+        gate = product(ref[...], gate_w[...])
+        up = product(ref[...], up_w[...])
+        if step == 0:
+            gate_ref[...] = gate
+            up_ref[...] = up
+        else:
+            gate_ref[...] += gate
+            up_ref[...] += up
 
 
 def last_kernel(sc, top_ref, low_ref, w0, w1, w2, w3, gate_in, up_in, out_ref, gate_w, up_w):
@@ -121,15 +123,25 @@
         out_ref[rows, :] = (gate / (1.0 + jnp.exp(-gate)) * up).astype(BF16)
 
 
-def down_kernel(sc, h0, h1, h2, h3, wd_ref, out_ref):
+def slab_kernel(sc, s0, s1, s2, s3, o0, o1, o2, o3):
+    for ref, out in ((s0, o0), (s1, o1), (s2, o2), (s3, o3)):
+        out[...] = ref[...]
+
+
+def down_kernel(sc, h0, h1, h2, h3, *refs):
+    near_ref, far_ref, out_ref, joined = refs
+    part = near_ref.shape[1]
     share = out_ref.shape[2]
-    for part in range(2):
-        cols = slice(part * share, (part + 1) * share)
-        total = jnp.dot(h0[...], wd_ref[0, :, cols], preferred_element_type=F32)
-        total += jnp.dot(h1[...], wd_ref[1, :, cols], preferred_element_type=F32)
-        total += jnp.dot(h2[...], wd_ref[2, :, cols], preferred_element_type=F32)
-        total += jnp.dot(h3[...], wd_ref[3, :, cols], preferred_element_type=F32)
-        out_ref[part] = total.astype(BF16)
+    for step in range(4):
+        joined[step, 0:part, :] = near_ref[step]
+        joined[step, part : 2 * part, :] = far_ref[step]
+    for side in range(2):
+        cols = slice(side * share, (side + 1) * share)
+        total = jnp.dot(h0[...], joined[0, :, cols], preferred_element_type=F32)
+        total += jnp.dot(h1[...], joined[1, :, cols], preferred_element_type=F32)
+        total += jnp.dot(h2[...], joined[2, :, cols], preferred_element_type=F32)
+        total += jnp.dot(h3[...], joined[3, :, cols], preferred_element_type=F32)
+        out_ref[side] = total.astype(BF16)
 
 
 def combine_kernel(sc, ret_ref, high_ref, low_ref, tok_ref, gain_ref, proj_ref, out_ref):
@@ -217,6 +229,10 @@
     out_ref[...] = (fine[32 : 32 + own, :] + second + bias_ref[...]).astype(BF16)
 
 
+def flipped(x, bits):
+    return lax.ppermute(x, EXP, [(i, i ^ bits) for i in range(8)])
+
+
 def swapped(x, axis):
     return lax.ppermute(x, axis, [(0, 1), (1, 0)])
 
@@ -238,7 +254,8 @@
     cache_head,
 ):
     tile = lax.axis_index(EXP).astype(jnp.int32)
-    half, quarter = tile >> 2, tile & 3
+    half = tile >> 2
+    quarter = (tile & 3) ^ (half << 1)
     scalars = jnp.stack([tile, half, cache_head[0], quarter, quarter ^ 1, quarter ^ 2, quarter ^ 3])
     count, width = tokens.shape[1:]
     hid = w_gate.shape[2]
@@ -250,19 +267,26 @@
     with jax.named_scope("exchange_weights"):
         pairs = [(i, i ^ 6) for i in range(8)]
         other_gate = lax.ppermute(own_gate, EXP, pairs)
-        other_up = lax.ppermute(own_up, EXP, pairs)
-        slabs = jnp.moveaxis(w_down[0].reshape(hid, 4, fourth), 1, 0)
-        slabs = jnp.concatenate([slabs, slabs], axis=0)
-        down = lax.all_to_all(slabs, EXP, 0, 0, tiled=True)
-        order = [tile, tile ^ 6, tile ^ 2, tile ^ 4, tile ^ 1, tile ^ 7, tile ^ 3, tile ^ 5]
-        down = jnp.concatenate(
-            [lax.dynamic_slice_in_dim(down, i, 1, 0) for i in order], axis=0
-        ).reshape(4, 2 * hid, fourth)
+        later, other_gate = lax.optimization_barrier((own_up, other_gate))
+        other_up = lax.ppermute(later, EXP, pairs)
+        slabs = call(
+            slab_kernel,
+            "slabs",
+            scalars,
+            (w_down[0],) * 4,
+            [pl.BlockSpec((hid, fourth), lambda i, s, k=k: (0, s[3 + k])) for k in range(4)],
+            [jax.ShapeDtypeStruct((hid, fourth), BF16)] * 4,
+        )
+        near_2 = flipped(slabs[2], 2)
+        near_1 = flipped(slabs[1], 1)
+        near_3 = flipped(flipped(slabs[3], 1), 2)
+        near = jnp.stack([slabs[0], near_2, near_1, near_3])
 
     with jax.named_scope("cache"):
         frames = frame_cache.reshape(3, 128, channels)
         above = lax.ppermute(frames[:, 96:], EXP, [(i, i + 1) for i in range(7)])
         below = lax.ppermute(frames[:, :32], EXP, [(i + 1, i) for i in range(7)])
+        frames, other_gate = lax.optimization_barrier((frames, other_gate))
         past = call(
             cache_kernel,
             "cache",
@@ -276,6 +300,7 @@
                 whole((1, channels)),
             ],
             jax.ShapeDtypeStruct((160, channels), F32),
+            cost=pl.CostEstimate(flops=8000 * 10**6, bytes_accessed=40 * 10**6, transcendentals=0),
         )
 
     with jax.named_scope("dispatch"):
@@ -307,43 +332,43 @@
         )
 
     with jax.named_scope("gather"):
+        arrived, near, past, high, low = lax.optimization_barrier(
+            (arrived, near, past, high, low)
+        )
         from_y = swapped(arrived, "yl")
         from_x = swapped(arrived, "x")
         corner_top = swapped(from_y[:256], "x")
         corner_low = swapped(from_x[256:], "yl")
+        arrived, from_x, from_y = lax.optimization_barrier((arrived, from_x, from_y))
+        near, other_up = lax.optimization_barrier((near, other_up))
+        far = flipped(near, 6)
 
     with jax.named_scope("experts"):
         weights = (own_gate, other_gate, own_up, other_up)
         pair = [jax.ShapeDtypeStruct((512, 2 * hid), F32)] * 2
         scratch = [pltpu.VMEM((2 * hid, fourth), BF16)] * 2
-        rows = whole((512, fourth))
         acc = whole((512, 2 * hid))
-
-        def columns_of(which):
-            return [pl.BlockSpec((hid, fourth), lambda i, s: (0, s[which]))] * 4
-
         gate, up = call(
-            start_kernel, "start", scalars, (arrived, *weights), [rows] + columns_of(3), pair, scratch
-        )
-        for name, piece, which in (("from_x", from_x, 4), ("from_y", from_y, 5)):
-            gate, up = call(
-                more_kernel,
-                name,
-                scalars,
-                (piece, *weights, gate, up),
-                [rows] + columns_of(which) + [acc, acc],
-                pair,
-                scratch,
-                {6: 0, 7: 1},
-            )
+            first_kernel,
+            "first",
+            scalars,
+            (arrived, from_x, from_y, *weights),
+            [whole((512, fourth))] * 3 + [whole((hid, width))] * 4,
+            pair,
+            scratch,
+            24,
+        )
         hidden = call(
             last_kernel,
             "hidden",
             scalars,
             (corner_top, corner_low, *weights, gate, up),
-            [whole((256, fourth))] * 2 + columns_of(6) + [acc, acc],
+            [whole((256, fourth))] * 2
+            + [pl.BlockSpec((hid, fourth), lambda i, s: (0, s[6]))] * 4
+            + [acc, acc],
             jax.ShapeDtypeStruct((512, 2 * hid), BF16),
             scratch,
+            16,
         )
 
     with jax.named_scope("hidden_gather"):
@@ -356,12 +381,22 @@
             down_kernel,
             "down",
             scalars,
-            (hidden, hidden_y, hidden_x, hidden_c, down),
-            [whole((512, 2 * hid))] * 4 + [whole(down.shape)],
+            (hidden, hidden_y, hidden_x, hidden_c, near, far),
+            [whole((512, 2 * hid))] * 4 + [whole((4, hid, fourth))] * 2,
             jax.ShapeDtypeStruct((2, 512, share), BF16),
+            [pltpu.VMEM((4, 2 * hid, fourth), BF16)],
+            20,
         )
         returned = lax.all_to_all(
-            answer.reshape(64, 16, share), ("yh", "sess"), 0, 0, tiled=True
+            answer.reshape(64, 16, share),
+            ("sess",) + EXP,
+            0,
+            0,
+            axis_index_groups=[
+                [s * 8 + 4 * h + (c ^ (2 * h)) for h in range(2) for s in range(32)]
+                for c in range(4)
+            ],
+            tiled=True,
         ).reshape(1024, share)
 
     with jax.named_scope("combine"):

time: 272 us -> 170 us (0.62); the launches traced: 268 us -> 170 us
  waiting for transfers between devices: 158 us -> 59.7 us
  blocking collectives: 0 us -> 51.1 us
  local copies, waits for them, and re-layouts: 36.5 us -> 4.62 us
  starting transfers between devices: 43.9 us -> 31.7 us
  Pallas kernels: 26.6 us -> 20.5 us
    ppermute x1, waiting for transfers between devices: 61.3 us -> 0.01 us  [body(): other_gate = lax.ppermute(own_gate, EXP, pairs)]
    all_to_all x0 -> x2, blocking collectives: none -> 51.1 us  [the longest x1 39 us: body(): lax.all_to_all(answer.reshape(64, 16, share), ('sess',) + EXP, 0, 0, axis...]
    all_to_all x3 -> x0, waiting for transfers between devices: 26.6 us -> none  [the longest x1 26.6 us: body(): lax.all_to_all(answer.reshape(64, 16, share), ('yh', 'sess'), 0, 0, tiled...]
    all_to_all x1, waiting for transfers between devices: 22.6 us -> 0.01 us  [body(): lax.all_to_all(outgoing.reshape(32, 16, fourth), 'sess', 0, 0, tiled=True)]
    unnamed x59 -> x40, local copies, waits for them, and re-layouts: 26.9 us -> 4.46 us
    all_to_all x3 -> x0, starting transfers between devices: 17.1 us -> none  [the longest x1 8.23 us: body(): lax.all_to_all(answer.reshape(64, 16, share), ('yh', 'sess'), 0, 0, tiled...]
    ppermute x6, waiting for transfers between devices: 7.57 us -> 20.1 us  [swapped(): return lax.ppermute(x, axis, [(0, 1), (1, 0)])]
    pallas_call x10 -> x9, Pallas kernels: 26.6 us -> 20.5 us  [call(): pl.pallas_call(kernel, name=name, out_shape=out_list, grid_spec=pltpu.Pre...]
  transfers between devices with their start and end apart: 15 -> 17, of which waited for: 10 -> 10; matrix products, arithmetic and copies ran while one was open for 7% -> 1% of each run, Pallas kernels for 4% -> 8%
where the time goes in v2:
time: 170 us
  waiting for transfers between devices  59.7 us (35%)
  blocking collectives  51.1 us (30%)
  starting transfers between devices  31.7 us (19%)
  Pallas kernels  20.5 us (12%)
  local copies, waits for them, and re-layouts  4.62 us (3%)
    all_to_all x1, blocking collectives, body(): lax.all_to_all(answer.reshape(64, 16, share), ('sess',) + EXP, 0, 0, axis...  39 us
    pallas_call x9, Pallas kernels, call(): pl.pallas_call(kernel, name=name, out_shape=out_list, grid_spec=pltpu.Pre...  20.5 us
    ppermute x6, waiting for transfers between devices, swapped(): return lax.ppermute(x, axis, [(0, 1), (1, 0)])  20.1 us
    ppermute x5, waiting for transfers between devices, flipped(): return lax.ppermute(x, EXP, [(i, i ^ bits) for i in range(8)])  18.2 us
    ppermute x1, waiting for transfers between devices, body(): other_up = lax.ppermute(later, EXP, pairs)  16.2 us
    all_to_all x1, blocking collectives, body(): blocks = lax.all_to_all(blocks, EXP, 0, 0, tiled=True)  12.1 us
    all_to_all x1, starting transfers between devices, body(): lax.all_to_all(outgoing.reshape(32, 16, fourth), 'sess', 0, 0, tiled=True)  10.9 us
    ppermute x6, starting transfers between devices, swapped(): return lax.ppermute(x, axis, [(0, 1), (1, 0)])  7.5 us
  transfers between devices with their start and end apart: 17, of which 10 were waited for; matrix products, arithmetic and copies ran while one was open for 1% of the time, Pallas kernels for 8%

profile of v2, /device:TPU:64, one launch (start us, length us, event | category | flops | bytes accessed | tf_op | source)
XLA Modules:
  0.0 169.8 jit_solution(16395631776020419227)
XLA Ops:
  0.0 3.0 %collective-permute-start.4 = (bf16[176,4096]{1,0:T(8,128)(2,1)}, bf16[176,4096]{1,0:T(8,128)(2,1)}, u32[]{:S(2)}, u32[]{:S(2)}) collective-permute-start(bf16[176,4096]{1,0:T(8,128)(2,1)} %bitcast.39), channel_id=1, source_target_pairs={{0,6},{1,7},{2,4},{3,5},{4,2},{5,3},{6,0},{7,1},{8,14},{9,15},{10,... | collective-permute-start | bytes 4325384 | tf_op jit(solution)/shard_map/exchange_weights/ppermute | solution.py:269
  3.8 1.6 copy-done.1
  6.7 2.1 %dispatch.1 = (bf16[512,1024]{1,0:T(8,128)(2,1)}, f32[256,128]{1,0:T(8,128)S(1)}) custom-call(s32[7]{0:T(128)S(1)} %stack.42.sc, s32[2,256]{1,0:T(2,128)S(1)} %bitcast.51, f32[2,256]{1,0:T(2,128)S(1)} %bitcast.52, bf16[256,4096]{1,0:T(8,128)(2,1)S(1)} %bitcast.37), custom_call_target="tpu_custom_call" | custom-call | tf_op jit(solution)/shard_map/dispatch/dispatch/pallas_call | solution.py:23
  8.8 10.9 %all-to-all-start = ((bf16[32,16,1024]{2,1,0:T(8,128)(2,1)}), bf16[32,16,1024]{2,1,0:T(8,128)(2,1)}, u32[]{:S(2)}, u32[]{:S(2)}) async-start(bf16[32,16,1024]{2,1,0:T(8,128)(2,1)} %bitcast.11), calls=%async_computation | async-start | bytes 2097152 | tf_op jit(solution)/shard_map/dispatch/all_to_all | solution.py:322
  22.7 14.7 %collective-permute-done.2 = bf16[176,1024]{1,0:T(8,128)(2,1)S(1)} collective-permute-done((bf16[176,1024]{1,0:T(8,128)(2,1)S(1)}, bf16[176,1024]{1,0:T(8,128)(2,1)S(1)}, u32[]{:S(2)}, u32[]{:S(2)}) %collective-permute-start.2) | collective-permute-done | bytes 360480 | tf_op jit(solution)/shard_map/exchange_weights/ppermute | solution.py:233
  38.7 3.2 %collective-permute-start.5 = (bf16[3,32,256]{2,1,0:T(8,128)(2,1)S(1)}, bf16[3,32,256]{2,1,0:T(8,128)(2,1)S(1)}, u32[]{:S(2)}, u32[]{:S(2)}) collective-permute-start(bf16[3,32,256]{2,1,0:T(8,128)(2,1)S(1)} %get-tuple-element.54), channel_id=1, source_target_pairs={{0,1},{1,2},{2,3},{3,4},{4,5},{5,6},{6,7},{8,9},{9,10},{10,11},{11... | collective-permute-start | bytes 147464 | tf_op jit(solution)/shard_map/cache/ppermute | solution.py:287
  45.1 3.5 %collective-permute-done.1 = bf16[176,1024]{1,0:T(8,128)(2,1)S(1)} collective-permute-done((bf16[176,1024]{1,0:T(8,128)(2,1)S(1)}, bf16[176,1024]{1,0:T(8,128)(2,1)S(1)}, u32[]{:S(2)}, u32[]{:S(2)}) %collective-permute-start.1) | collective-permute-done | bytes 360480 | tf_op jit(solution)/shard_map/exchange_weights/ppermute | solution.py:233
  53.4 2.1 %collective-permute-start.7 = (bf16[512,1024]{1,0:T(8,128)(2,1)}, bf16[512,1024]{1,0:T(8,128)(2,1)S(1)}, u32[]{:S(2)}, u32[]{:S(2)}) collective-permute-start(bf16[512,1024]{1,0:T(8,128)(2,1)} %bitcast.12.x0), channel_id=1, source_target_pairs={{0,2},{2,0},{1,3},{3,1},{4,6},{6,4},{5,7},{7,5},{8,10},{10,8},{9,1... | collective-permute-start | bytes 3145736 | tf_op jit(solution)/shard_map/gather/ppermute | solution.py:237
  55.5 16.2 %collective-permute-done.11.w3 = bf16[176,4096]{1,0:T(8,128)(2,1)} collective-permute-done((bf16[176,4096]{1,0:T(8,128)(2,1)S(1)}, bf16[176,4096]{1,0:T(8,128)(2,1)}, u32[]{:S(2)}, u32[]{:S(2)}) %collective-permute-start.11) | collective-permute-done | bytes 1441824 | tf_op jit(solution)/shard_map/exchange_weights/ppermute | solution.py:271
  72.6 4.7 %collective-permute-done.9.x1 = bf16[512,1024]{1,0:T(8,128)(2,1)S(1)} collective-permute-done((bf16[512,1024]{1,0:T(8,128)(2,1)}, bf16[512,1024]{1,0:T(8,128)(2,1)S(1)}, u32[]{:S(2)}, u32[]{:S(2)}) %collective-permute-start.9) | collective-permute-done | bytes 1048608 | tf_op jit(solution)/shard_map/gather/ppermute | solution.py:237
  77.7 1.6 collective-permute-start.8
  79.3 6.1 %first.1 = (f32[512,352]{1,0:T(8,128)S(1)}, f32[512,352]{1,0:T(8,128)S(1)}) custom-call(s32[7]{0:T(128)S(1)} %stack.42.sc, bf16[512,1024]{1,0:T(8,128)(2,1)} %bitcast.12.x0, bf16[512,1024]{1,0:T(8,128)(2,1)S(1)} %collective-permute-done.9.x1, bf16[512,1024]{1,0:T(8,128)(2,1)S(1)} %collective-permute-done.7.x2, bf16[176,4096]{1,0:T(8,128)(2,1)S(1)} %bitcast.40, ...), custom_call_target="tpu_custom_call" | custom-call | tf_op jit(solution)/shard_map/experts/first/pallas_call | solution.py:23
  85.4 4.8 %collective-permute-done.10.low_ref = bf16[256,1024]{1,0:T(8,128)(2,1)S(1)} collective-permute-done((bf16[256,1024]{1,0:T(8,128)(2,1)S(1)}, bf16[256,1024]{1,0:T(8,128)(2,1)S(1)}, u32[]{:S(2)}, u32[]{:S(2)}) %collective-permute-start.10) | collective-permute-done | bytes 524320 | tf_op jit(solution)/shard_map/gather/ppermute | solution.py:237
  90.5 2.9 %hidden.1.h0 = bf16[512,352]{1,0:T(8,128)(2,1)S(1)} custom-call(s32[7]{0:T(128)S(1)} %stack.42.sc, bf16[256,1024]{1,0:T(8,128)(2,1)S(1)} %collective-permute-done.8.top_ref, bf16[256,1024]{1,0:T(8,128)(2,1)S(1)} %collective-permute-done.10.low_ref, bf16[176,4096]{1,0:T(8,128)(2,1)S(1)} %bitcast.41, bf16[176,4096]{1,0:T(8,128)(2,1)} %collective-permute-done.4.w1, ...), custom_call_target="tpu_custom_call" | custom-call | tf_op jit(solution)/shard_map/experts/hidden/pallas_call | solution.py:23
  93.5 1.8 %collective-permute-start.12 = (bf16[512,352]{1,0:T(8,128)(2,1)S(1)}, bf16[512,352]{1,0:T(8,128)(2,1)S(1)}, u32[]{:S(2)}, u32[]{:S(2)}) collective-permute-start(bf16[512,352]{1,0:T(8,128)(2,1)S(1)} %hidden.1.h0), channel_id=1, source_target_pairs={{0,2},{2,0},{1,3},{3,1},{4,6},{6,4},{5,7},{7,5},{8,10},{10,8},{9,1... | collective-permute-start | bytes 1081352 | tf_op jit(solution)/shard_map/hidden_gather/ppermute | solution.py:237
  95.6 1.5 collective-permute-start.14
  97.0 7.5 %collective-permute-done.12.h1 = bf16[512,352]{1,0:T(8,128)(2,1)S(1)} collective-permute-done((bf16[512,352]{1,0:T(8,128)(2,1)S(1)}, bf16[512,352]{1,0:T(8,128)(2,1)S(1)}, u32[]{:S(2)}, u32[]{:S(2)}) %collective-permute-start.12) | collective-permute-done | bytes 360480 | tf_op jit(solution)/shard_map/hidden_gather/ppermute | solution.py:237
  104.5 2.8 %collective-permute-done.13.h2 = bf16[512,352]{1,0:T(8,128)(2,1)S(1)} collective-permute-done((bf16[512,352]{1,0:T(8,128)(2,1)S(1)}, bf16[512,352]{1,0:T(8,128)(2,1)S(1)}, u32[]{:S(2)}, u32[]{:S(2)}) %collective-permute-start.13) | collective-permute-done | bytes 360480 | tf_op jit(solution)/shard_map/hidden_gather/ppermute | solution.py:237
  107.3 4.7 %collective-permute-done.14.h3 = bf16[512,352]{1,0:T(8,128)(2,1)S(1)} collective-permute-done((bf16[512,352]{1,0:T(8,128)(2,1)S(1)}, bf16[512,352]{1,0:T(8,128)(2,1)S(1)}, u32[]{:S(2)}, u32[]{:S(2)}) %collective-permute-start.14) | collective-permute-done | bytes 360480 | tf_op jit(solution)/shard_map/hidden_gather/ppermute | solution.py:377
  112.1 2.9 %down.1 = bf16[2,512,512]{2,1,0:T(8,128)(2,1)S(1)} custom-call(s32[7]{0:T(128)S(1)} %stack.42.sc, bf16[512,352]{1,0:T(8,128)(2,1)S(1)} %hidden.1.h0, bf16[512,352]{1,0:T(8,128)(2,1)S(1)} %collective-permute-done.12.h1, bf16[512,352]{1,0:T(8,128)(2,1)S(1)} %collective-permute-done.13.h2, bf16[512,352]{1,0:T(8,128)(2,1)S(1)} %collective-permute-done.14.h3, ...), custom_call_target="tpu_custom_call" | custom-call | tf_op jit(solution)/shard_map/down/down/pallas_call | solution.py:23
  115.0 39.0 %all_to_all.15 = bf16[64,16,512]{2,1,0:T(8,128)(2,1)S(1)} all-to-all(bf16[64,16,512]{2,1,0:T(8,128)(2,1)S(1)} %bitcast.45), channel_id=1, replica_groups={{0,8,16,24,32,40,48,56,64,72,80,88,96,104,112,120,128,136,144,152,160,1..., dimensions={0} | all-to-all | bytes 2097152 | tf_op jit(solution)/shard_map/down/all_to_all | solution.py:390
  154.0 1.4 combine.1
  155.5 12.1 %all_to_all.16.arr_ref = bf16[8,48,384]{2,1,0:T(8,128)(2,1)S(1)} all-to-all(bf16[8,48,384]{2,1,0:T(8,128)(2,1)S(1)} %combine.1), channel_id=1, replica_groups=mesh['sess'=32,'yh'=2,'yl'=2,'x'=2] {'yh','yl','x'}, dimensions={0} | all-to-all | bytes 589824 | tf_op jit(solution)/shard_map/combine/all_to_all | solution.py:418
  167.6 2.2 %decode.1 = bf16[128,256]{1,0:T(8,128)(2,1)} custom-call(s32[7]{0:T(128)S(1)} %stack.42.sc, bf16[8,48,384]{2,1,0:T(8,128)(2,1)S(1)} %all_to_all.16.arr_ref, f32[160,256]{1,0:T(8,128)S(1)} %copy-done.13, bf16[3,3,3,256,256]{4,3,2,1,0:T(8,128)(2,1)S(1)} %copy-done.7, bf16[3,3,256,256]{3,2,1,0:T(8,128)(2,1)S(1)} %copy-done.9, f32[1,256]{1,0:T(1,128)S(1)} %bitcast.53), custom_call_target="tpu_custom_call" | custom-call | tf_op jit(solution)/shard_map/decode/decode/pallas_call | solution.py:23
  (66 shorter events, 15.5 us)
Async XLA Ops:
  0.0 37.6 %collective-permute-start.4 = (bf16[176,4096]{1,0:T(8,128)(2,1)}, bf16[176,4096]{1,0:T(8,128)(2,1)}, u32[]{:S(2)}, u32[]{:S(2)}) collective-permute-start(bf16[176,4096]{1,0:T(8,128)(2,1)} %bitcast.39), channel_id=1, source_target_pairs={{0,6},{1,7},{2,4},{3,5},{4,2},{5,3},{6,0},{7,1},{8,14},{9,15},{10,... | collective-permute-start | bytes 4325384 | tf_op jit(solution)/shard_map/exchange_weights/ppermute | solution.py:269
  8.8 43.3 %all-to-all-start = ((bf16[32,16,1024]{2,1,0:T(8,128)(2,1)}), bf16[32,16,1024]{2,1,0:T(8,128)(2,1)}, u32[]{:S(2)}, u32[]{:S(2)}) async-start(bf16[32,16,1024]{2,1,0:T(8,128)(2,1)} %bitcast.11), calls=%async_computation | async-start | bytes 2097152 | tf_op jit(solution)/shard_map/dispatch/all_to_all | solution.py:322
  19.8 30.5 %copy-start.6 = (bf16[3,3,3,256,256]{4,3,2,1,0:T(8,128)(2,1)S(1)}, bf16[3,3,3,256,256]{4,3,2,1,0:T(8,128)(2,1)}, u32[]{:S(2)}) copy-start(bf16[3,3,3,256,256]{4,3,2,1,0:T(8,128)(2,1)} %time_ref.1) | copy-start | bytes 10616836
  20.5 17.0 %collective-permute-start.2 = (bf16[176,1024]{1,0:T(8,128)(2,1)S(1)}, bf16[176,1024]{1,0:T(8,128)(2,1)S(1)}, u32[]{:S(2)}, u32[]{:S(2)}) collective-permute-start(bf16[176,1024]{1,0:T(8,128)(2,1)S(1)} %get-tuple-element.33), channel_id=1, source_target_pairs={{0,1},{1,0},{2,3},{3,2},{4,5},{5,4},{6,7},{7,6},{8,9},{9,8},{10,11... | collective-permute-start | bytes 1081352 | tf_op jit(solution)/shard_map/exchange_weights/ppermute | solution.py:233
  21.1 22.7 %collective-permute-start = (bf16[176,1024]{1,0:T(8,128)(2,1)S(1)}, bf16[176,1024]{1,0:T(8,128)(2,1)S(1)}, u32[]{:S(2)}, u32[]{:S(2)}) collective-permute-start(bf16[176,1024]{1,0:T(8,128)(2,1)S(1)} %get-tuple-element.31), channel_id=1, source_target_pairs={{0,2},{1,3},{2,0},{3,1},{4,6},{5,7},{6,4},{7,5},{8,10},{9,11},{10,... | collective-permute-start | bytes 1081352 | tf_op jit(solution)/shard_map/exchange_weights/ppermute | solution.py:233
  21.3 27.3 %collective-permute-start.1 = (bf16[176,1024]{1,0:T(8,128)(2,1)S(1)}, bf16[176,1024]{1,0:T(8,128)(2,1)S(1)}, u32[]{:S(2)}, u32[]{:S(2)}) collective-permute-start(bf16[176,1024]{1,0:T(8,128)(2,1)S(1)} %get-tuple-element.32), channel_id=1, source_target_pairs={{0,1},{1,0},{2,3},{3,2},{4,5},{5,4},{6,7},{7,6},{8,9},{9,8},{10,11... | collective-permute-start | bytes 1081352 | tf_op jit(solution)/shard_map/exchange_weights/ppermute | solution.py:233
  37.4 11.1 %collective-permute-start.3 = (bf16[176,1024]{1,0:T(8,128)(2,1)S(1)}, bf16[176,1024]{1,0:T(8,128)(2,1)S(1)}, u32[]{:S(2)}, u32[]{:S(2)}) collective-permute-start(bf16[176,1024]{1,0:T(8,128)(2,1)S(1)} %collective-permute-done.2), channel_id=1, source_target_pairs={{0,2},{1,3},{2,0},{3,1},{4,6},{5,7},{6,4},{7,5},{8,10},{9,11},{10,... | collective-permute-start | bytes 1081352 | tf_op jit(solution)/shard_map/exchange_weights/ppermute | solution.py:233
  37.6 34.2 %collective-permute-start.11 = (bf16[176,4096]{1,0:T(8,128)(2,1)S(1)}, bf16[176,4096]{1,0:T(8,128)(2,1)}, u32[]{:S(2)}, u32[]{:S(2)}) collective-permute-start(bf16[176,4096]{1,0:T(8,128)(2,1)S(1)} %bitcast.42), channel_id=1, source_target_pairs={{0,6},{1,7},{2,4},{3,5},{4,2},{5,3},{6,0},{7,1},{8,14},{9,15},{10,... | collective-permute-start | bytes 4325384 | tf_op jit(solution)/shard_map/exchange_weights/ppermute | solution.py:271
  38.7 11.2 %collective-permute-start.5 = (bf16[3,32,256]{2,1,0:T(8,128)(2,1)S(1)}, bf16[3,32,256]{2,1,0:T(8,128)(2,1)S(1)}, u32[]{:S(2)}, u32[]{:S(2)}) collective-permute-start(bf16[3,32,256]{2,1,0:T(8,128)(2,1)S(1)} %get-tuple-element.54), channel_id=1, source_target_pairs={{0,1},{1,2},{2,3},{3,4},{4,5},{5,6},{6,7},{8,9},{9,10},{10,11},{11... | collective-permute-start | bytes 147464 | tf_op jit(solution)/shard_map/cache/ppermute | solution.py:287
  43.8 6.5 %collective-permute-start.6 = (bf16[3,32,256]{2,1,0:T(8,128)(2,1)S(1)}, bf16[3,32,256]{2,1,0:T(8,128)(2,1)S(1)}, u32[]{:S(2)}, u32[]{:S(2)}) collective-permute-start(bf16[3,32,256]{2,1,0:T(8,128)(2,1)S(1)} %get-tuple-element.53), channel_id=1, source_target_pairs={{1,0},{2,1},{3,2},{4,3},{5,4},{6,5},{7,6},{9,8},{10,9},{11,10},{12... | collective-permute-start | bytes 147464 | tf_op jit(solution)/shard_map/cache/ppermute | solution.py:288
  52.1 27.2 %copy-start.3 = (bf16[1,4096,176]{1,2,0:T(8,128)(2,1)S(1)}, bf16[1,4096,176]{1,2,0:T(8,128)(2,1)}, u32[]{:S(2)}) copy-start(bf16[1,4096,176]{1,2,0:T(8,128)(2,1)} %param.17) | copy-start | bytes 4325380
  52.1 25.1 %collective-permute-start.9 = (bf16[512,1024]{1,0:T(8,128)(2,1)}, bf16[512,1024]{1,0:T(8,128)(2,1)S(1)}, u32[]{:S(2)}, u32[]{:S(2)}) collective-permute-start(bf16[512,1024]{1,0:T(8,128)(2,1)} %bitcast.12.x0), channel_id=1, source_target_pairs={{0,1},{1,0},{2,3},{3,2},{4,5},{5,4},{6,7},{7,6},{8,9},{9,8},{10,11... | collective-permute-start | bytes 3145736 | tf_op jit(solution)/shard_map/gather/ppermute | solution.py:237
  53.4 24.3 %collective-permute-start.7 = (bf16[512,1024]{1,0:T(8,128)(2,1)}, bf16[512,1024]{1,0:T(8,128)(2,1)S(1)}, u32[]{:S(2)}, u32[]{:S(2)}) collective-permute-start(bf16[512,1024]{1,0:T(8,128)(2,1)} %bitcast.12.x0), channel_id=1, source_target_pairs={{0,2},{2,0},{1,3},{3,1},{4,6},{6,4},{5,7},{7,5},{8,10},{10,8},{9,1... | collective-permute-start | bytes 3145736 | tf_op jit(solution)/shard_map/gather/ppermute | solution.py:237
  71.8 40.3 %collective-permute-start.15 = (bf16[4,176,1024]{2,1,0:T(8,128)(2,1)}, bf16[4,176,1024]{2,1,0:T(8,128)(2,1)S(1)}, u32[]{:S(2)}, u32[]{:S(2)}) collective-permute-start(bf16[4,176,1024]{2,1,0:T(8,128)(2,1)} %pad_maximum_fusion.refs_0_), channel_id=1, source_target_pairs={{0,6},{1,7},{2,4},{3,5},{4,2},{5,3},{6,0},{7,1},{8,14},{9,15},{10,... | collective-permute-start | bytes 4325384 | tf_op jit(solution)/shard_map/gather/ppermute | solution.py:233
  77.3 12.9 %collective-permute-start.10 = (bf16[256,1024]{1,0:T(8,128)(2,1)S(1)}, bf16[256,1024]{1,0:T(8,128)(2,1)S(1)}, u32[]{:S(2)}, u32[]{:S(2)}) collective-permute-start(bf16[256,1024]{1,0:T(8,128)(2,1)S(1)} %slice.19), channel_id=1, source_target_pairs={{0,2},{2,0},{1,3},{3,1},{4,6},{6,4},{5,7},{7,5},{8,10},{10,8},{9,1... | collective-permute-start | bytes 1572872 | tf_op jit(solution)/shard_map/gather/ppermute | solution.py:237
  77.7 12.8 %collective-permute-start.8 = (bf16[256,1024]{1,0:T(8,128)(2,1)S(1)}, bf16[256,1024]{1,0:T(8,128)(2,1)S(1)}, u32[]{:S(2)}, u32[]{:S(2)}) collective-permute-start(bf16[256,1024]{1,0:T(8,128)(2,1)S(1)} %slice.18), channel_id=1, source_target_pairs={{0,1},{1,0},{2,3},{3,2},{4,5},{5,4},{6,7},{7,6},{8,9},{9,8},{10,11... | collective-permute-start | bytes 1572872 | tf_op jit(solution)/shard_map/gather/ppermute | solution.py:237
  90.5 21.5 %copy-start.5 = (bf16[4,176,1024]{2,1,0:T(8,128)(2,1)S(1)}, bf16[4,176,1024]{2,1,0:T(8,128)(2,1)}, u32[]{:S(2)}) copy-start(bf16[4,176,1024]{2,1,0:T(8,128)(2,1)} %pad_maximum_fusion.refs_0_) | copy-start | bytes 4325380
  93.5 11.1 %collective-permute-start.12 = (bf16[512,352]{1,0:T(8,128)(2,1)S(1)}, bf16[512,352]{1,0:T(8,128)(2,1)S(1)}, u32[]{:S(2)}, u32[]{:S(2)}) collective-permute-start(bf16[512,352]{1,0:T(8,128)(2,1)S(1)} %hidden.1.h0), channel_id=1, source_target_pairs={{0,2},{2,0},{1,3},{3,1},{4,6},{6,4},{5,7},{7,5},{8,10},{10,8},{9,1... | collective-permute-start | bytes 1081352 | tf_op jit(solution)/shard_map/hidden_gather/ppermute | solution.py:237
  95.3 12.1 %collective-permute-start.13 = (bf16[512,352]{1,0:T(8,128)(2,1)S(1)}, bf16[512,352]{1,0:T(8,128)(2,1)S(1)}, u32[]{:S(2)}, u32[]{:S(2)}) collective-permute-start(bf16[512,352]{1,0:T(8,128)(2,1)S(1)} %hidden.1.h0), channel_id=1, source_target_pairs={{0,1},{1,0},{2,3},{3,2},{4,5},{5,4},{6,7},{7,6},{8,9},{9,8},{10,11... | collective-permute-start | bytes 1081352 | tf_op jit(solution)/shard_map/hidden_gather/ppermute | solution.py:237
  95.6 16.5 %collective-permute-start.14 = (bf16[512,352]{1,0:T(8,128)(2,1)S(1)}, bf16[512,352]{1,0:T(8,128)(2,1)S(1)}, u32[]{:S(2)}, u32[]{:S(2)}) collective-permute-start(bf16[512,352]{1,0:T(8,128)(2,1)S(1)} %hidden.1.h0), channel_id=1, source_target_pairs={{0,3},{1,2},{2,1},{3,0},{4,7},{5,6},{6,5},{7,4},{8,11},{9,10},{10,... | collective-permute-start | bytes 1081352 | tf_op jit(solution)/shard_map/hidden_gather/ppermute | solution.py:377
  112.1 41.9 %copy-start.8 = (bf16[4096,256]{1,0:T(8,128)(2,1)S(1)}, bf16[4096,256]{1,0:T(8,128)(2,1)}, u32[]{:S(2)}) copy-start(bf16[4096,256]{1,0:T(8,128)(2,1)} %proj_ref.1) | copy-start | bytes 6291460
  112.1 41.9 %copy-start.11 = (bf16[256,1024]{1,0:T(8,128)(2,1)S(1)}, bf16[256,1024]{1,0:T(8,128)(2,1)}, u32[]{:S(2)}) copy-start(bf16[256,1024]{1,0:T(8,128)(2,1)} %copy-done.10) | copy-start | bytes 1572868
  112.1 41.9 %copy-start.15 = (f32[4096]{0:T(1024)S(1)}, f32[4096]{0:T(1024)}, u32[]{:S(2)}) copy-start(f32[4096]{0:T(1024)} %param.20) | copy-start | bytes 49156
  115.0 39.0 %copy-start.2 = (bf16[1,256,4096]{2,1,0:T(8,128)(2,1)S(1)}, bf16[1,256,4096]{2,1,0:T(8,128)(2,1)}, u32[]{:S(2)}) copy-start(bf16[1,256,4096]{2,1,0:T(8,128)(2,1)} %param.14) | copy-start | bytes 6291460
  (13 other events, 108.2 us)

commit v3 on v2

--- a/solution.py
+++ b/solution.py
@@ -89,6 +89,10 @@
     return lax.dot_general(rows, weights, (((1,), (1,)), ((), ())), preferred_element_type=F32)
 
 
+def turned(hidden, weights):
+    return lax.dot_general(hidden, weights, (((0,), (0,)), ((), ())), preferred_element_type=F32)
+
+
 def joined_weights(refs, gate_w, up_w):
     own_gate, other_gate, own_up, other_up = refs
     part = own_gate.shape[0]
@@ -103,8 +107,8 @@
     for step, ref in enumerate((x0, x1, x2)):
         cols = pl.ds(pl.multiple_of(sc[3 + step] * width, width), width)
         joined_weights([w.at[:, cols] for w in (w0, w1, w2, w3)], gate_w, up_w)
-        gate = product(ref[...], gate_w[...])
-        up = product(ref[...], up_w[...])
+        gate = product(gate_w[...], ref[...])
+        up = product(up_w[...], ref[...])
         if step == 0:
             gate_ref[...] = gate
             up_ref[...] = up
@@ -118,9 +122,9 @@
     middle = top_ref.shape[0]
     for ref, begin in ((top_ref, 0), (low_ref, middle)):
         rows = slice(begin, begin + middle)
-        gate = gate_in[rows, :] + product(ref[...], gate_w[...])
-        up = up_in[rows, :] + product(ref[...], up_w[...])
-        out_ref[rows, :] = (gate / (1.0 + jnp.exp(-gate)) * up).astype(BF16)
+        gate = gate_in[:, rows] + product(gate_w[...], ref[...])
+        up = up_in[:, rows] + product(up_w[...], ref[...])
+        out_ref[:, rows] = (gate / (1.0 + jnp.exp(-gate)) * up).astype(BF16)
 
 
 def slab_kernel(sc, s0, s1, s2, s3, o0, o1, o2, o3):
@@ -137,10 +141,10 @@
         joined[step, part : 2 * part, :] = far_ref[step]
     for side in range(2):
         cols = slice(side * share, (side + 1) * share)
-        total = jnp.dot(h0[...], joined[0, :, cols], preferred_element_type=F32)
-        total += jnp.dot(h1[...], joined[1, :, cols], preferred_element_type=F32)
-        total += jnp.dot(h2[...], joined[2, :, cols], preferred_element_type=F32)
-        total += jnp.dot(h3[...], joined[3, :, cols], preferred_element_type=F32)
+        total = turned(h0[...], joined[0, :, cols])
+        total += turned(h1[...], joined[1, :, cols])
+        total += turned(h2[...], joined[2, :, cols])
+        total += turned(h3[...], joined[3, :, cols])
         out_ref[side] = total.astype(BF16)
 
 
@@ -229,6 +233,10 @@
     out_ref[...] = (fine[32 : 32 + own, :] + second + bias_ref[...]).astype(BF16)
 
 
+def in_hbm(x):
+    return pltpu.with_memory_space_constraint(x, pltpu.HBM)
+
+
 def flipped(x, bits):
     return lax.ppermute(x, EXP, [(i, i ^ bits) for i in range(8)])
 
@@ -267,8 +275,6 @@
     with jax.named_scope("exchange_weights"):
         pairs = [(i, i ^ 6) for i in range(8)]
         other_gate = lax.ppermute(own_gate, EXP, pairs)
-        later, other_gate = lax.optimization_barrier((own_up, other_gate))
-        other_up = lax.ppermute(later, EXP, pairs)
         slabs = call(
             slab_kernel,
             "slabs",
@@ -277,21 +283,26 @@
             [pl.BlockSpec((hid, fourth), lambda i, s, k=k: (0, s[3 + k])) for k in range(4)],
             [jax.ShapeDtypeStruct((hid, fourth), BF16)] * 4,
         )
-        near_2 = flipped(slabs[2], 2)
-        near_1 = flipped(slabs[1], 1)
-        near_3 = flipped(flipped(slabs[3], 1), 2)
-        near = jnp.stack([slabs[0], near_2, near_1, near_3])
+        near_1, near_2, near_3 = [flipped(slabs[k], k) for k in (1, 2, 3)]
+        later, other_gate = lax.optimization_barrier((own_up, other_gate))
+        other_up = lax.ppermute(later, EXP, pairs)
 
     with jax.named_scope("cache"):
         frames = frame_cache.reshape(3, 128, channels)
         above = lax.ppermute(frames[:, 96:], EXP, [(i, i + 1) for i in range(7)])
         below = lax.ppermute(frames[:, :32], EXP, [(i + 1, i) for i in range(7)])
-        frames, other_gate = lax.optimization_barrier((frames, other_gate))
+        frames, *_ = lax.optimization_barrier((frames, near_1, near_2, near_3))
         past = call(
             cache_kernel,
             "cache",
             scalars,
-            (frames, above, below, conv_time, bias_time.reshape(1, channels)),
+            (
+                in_hbm(frames),
+                above,
+                below,
+                in_hbm(conv_time),
+                in_hbm(bias_time.reshape(1, channels)),
+            ),
             [
                 whole(frames.shape),
                 whole(above.shape),
@@ -300,7 +311,7 @@
                 whole((1, channels)),
             ],
             jax.ShapeDtypeStruct((160, channels), F32),
-            cost=pl.CostEstimate(flops=8000 * 10**6, bytes_accessed=40 * 10**6, transcendentals=0),
+            cost=pl.CostEstimate(flops=16000 * 10**6, bytes_accessed=80 * 10**6, transcendentals=0),
         )
 
     with jax.named_scope("dispatch"):
@@ -308,7 +319,7 @@
             dispatch_kernel,
             "dispatch",
             scalars,
-            (routes[0].T, gates[0].T, tokens[0]),
+            (in_hbm(routes[0].T), in_hbm(gates[0].T), in_hbm(tokens[0])),
             [
                 whole((2, count)),
                 whole((2, count)),
@@ -322,6 +333,7 @@
         arrived = lax.all_to_all(
             outgoing.reshape(32, 16, fourth), "sess", 0, 0, tiled=True
         ).reshape(512, fourth)
+        columns, _ = lax.optimization_barrier((columns, other_gate))
         high, low = call(
             weights_kernel,
             "weights",
@@ -329,14 +341,17 @@
             (columns,),
             [whole((count, 128))],
             [jax.ShapeDtypeStruct((count, 1024), BF16)] * 2,
+            cost=pl.CostEstimate(flops=12000 * 10**6, bytes_accessed=60 * 10**6, transcendentals=0),
         )
 
     with jax.named_scope("gather"):
-        arrived, near, past, high, low = lax.optimization_barrier(
-            (arrived, near, past, high, low)
-        )
+        arrived, near_1, near_2, near_3, high, low = lax.optimization_barrier(
+            (arrived, near_1, near_2, near_3, high, low)
+        )
+        near = jnp.stack([slabs[0], near_2, near_1, near_3])
         from_y = swapped(arrived, "yl")
         from_x = swapped(arrived, "x")
+        from_x, from_y, past = lax.optimization_barrier((from_x, from_y, past))
         corner_top = swapped(from_y[:256], "x")
         corner_low = swapped(from_x[256:], "yl")
         arrived, from_x, from_y = lax.optimization_barrier((arrived, from_x, from_y))
@@ -345,9 +360,9 @@
 
     with jax.named_scope("experts"):
         weights = (own_gate, other_gate, own_up, other_up)
-        pair = [jax.ShapeDtypeStruct((512, 2 * hid), F32)] * 2
+        pair = [jax.ShapeDtypeStruct((2 * hid, 512), F32)] * 2
         scratch = [pltpu.VMEM((2 * hid, fourth), BF16)] * 2
-        acc = whole((512, 2 * hid))
+        acc = whole((2 * hid, 512))
         gate, up = call(
             first_kernel,
             "first",
@@ -366,7 +381,7 @@
             [whole((256, fourth))] * 2
             + [pl.BlockSpec((hid, fourth), lambda i, s: (0, s[6]))] * 4
             + [acc, acc],
-            jax.ShapeDtypeStruct((512, 2 * hid), BF16),
+            jax.ShapeDtypeStruct((2 * hid, 512), BF16),
             scratch,
             16,
         )
@@ -382,7 +397,7 @@
             "down",
             scalars,
             (hidden, hidden_y, hidden_x, hidden_c, near, far),
-            [whole((512, 2 * hid))] * 4 + [whole((4, hid, fourth))] * 2,
+            [whole((2 * hid, 512))] * 4 + [whole((4, hid, fourth))] * 2,
             jax.ShapeDtypeStruct((2, 512, share), BF16),
             [pltpu.VMEM((4, 2 * hid, fourth), BF16)],
             20,

time: 170 us -> 166 us (0.976)
  waiting for transfers between devices: 59.7 us -> 49.6 us
  starting transfers between devices: 31.7 us -> 38.7 us
    ppermute x5 -> x4, waiting for transfers between devices: 18.2 us -> 2.47 us  [flipped(): return lax.ppermute(x, EXP, [(i, i ^ bits) for i in range(8)])]
    ppermute x1, waiting for transfers between devices: 0.01 us -> 12.1 us  [body(): other_gate = lax.ppermute(own_gate, EXP, pairs)]
    ppermute x6, waiting for transfers between devices: 20.1 us -> 15.9 us  [swapped(): return lax.ppermute(x, axis, [(0, 1), (1, 0)])]
    ppermute x5 -> x4, starting transfers between devices: 3.2 us -> 6.37 us  [flipped(): return lax.ppermute(x, EXP, [(i, i ^ bits) for i in range(8)])]
    unnamed x40 -> x32, local copies, waits for them, and re-layouts: 4.46 us -> 2.33 us
    ppermute x1, starting transfers between devices: 1.07 us -> 2.95 us  [body(): other_up = lax.ppermute(later, EXP, pairs)]
  transfers between devices with their start and end apart: 17 -> 16, of which waited for: 10 -> 9; matrix products, arithmetic and copies ran while one was open for 1% -> 1% of each run, Pallas kernels for 8% -> 9%
where the time goes in v3:
time: 166 us; the launch traced here: 165 us
  blocking collectives  50.2 us (30%)
  waiting for transfers between devices  49.6 us (30%)
  starting transfers between devices  38.7 us (23%)
  Pallas kernels  21.5 us (13%)
  local copies, waits for them, and re-layouts  3.12 us (2%)
    all_to_all x1, blocking collectives, body(): lax.all_to_all(answer.reshape(64, 16, share), ('sess',) + EXP, 0, 0, axis...  38.3 us
    pallas_call x9, Pallas kernels, call(): pl.pallas_call(kernel, name=name, out_shape=out_list, grid_spec=pltpu.Pre...  21.5 us
    ppermute x6, waiting for transfers between devices, swapped(): return lax.ppermute(x, axis, [(0, 1), (1, 0)])  15.9 us
    ppermute x1, waiting for transfers between devices, body(): other_up = lax.ppermute(later, EXP, pairs)  15 us
    ppermute x1, waiting for transfers between devices, body(): other_gate = lax.ppermute(own_gate, EXP, pairs)  12.1 us
    all_to_all x1, blocking collectives, body(): blocks = lax.all_to_all(blocks, EXP, 0, 0, tiled=True)  11.9 us
    all_to_all x1, starting transfers between devices, body(): lax.all_to_all(outgoing.reshape(32, 16, fourth), 'sess', 0, 0, tiled=True)  10.9 us
    ppermute x6, starting transfers between devices, swapped(): return lax.ppermute(x, axis, [(0, 1), (1, 0)])  8.77 us
  transfers between devices with their start and end apart: 16, of which 9 were waited for; matrix products, arithmetic and copies ran while one was open for 1% of the time, Pallas kernels for 9%

profile of v3, /device:TPU:64, one launch (start us, length us, event | category | flops | bytes accessed | tf_op | source)
XLA Modules:
  0.0 165.5 jit_solution(3010154432005957157)
XLA Ops:
  0.0 3.0 %collective-permute-start.3 = (bf16[176,4096]{1,0:T(8,128)(2,1)}, bf16[176,4096]{1,0:T(8,128)(2,1)}, u32[]{:S(2)}, u32[]{:S(2)}) collective-permute-start(bf16[176,4096]{1,0:T(8,128)(2,1)} %bitcast.39), channel_id=1, source_target_pairs={{0,6},{1,7},{2,4},{3,5},{4,2},{5,3},{6,0},{7,1},{8,14},{9,15},{10,... | collective-permute-start | bytes 4325384 | tf_op jit(solution)/shard_map/exchange_weights/ppermute | solution.py:277
  3.8 3.2 %dispatch.1 = (bf16[512,1024]{1,0:T(8,128)(2,1)}, f32[256,128]{1,0:T(8,128)S(1)}) custom-call(s32[7]{0:T(128)S(1)} %stack.42.sc, s32[2,256]{1,0:T(2,128)} %bitcast.55, f32[2,256]{1,0:T(2,128)} %bitcast.56, bf16[256,4096]{1,0:T(8,128)(2,1)} %bitcast.37), custom_call_target="tpu_custom_call" | custom-call | tf_op jit(solution)/shard_map/dispatch/dispatch/pallas_call | solution.py:23
  6.9 10.9 %all-to-all-start = ((bf16[32,16,1024]{2,1,0:T(8,128)(2,1)}), bf16[32,16,1024]{2,1,0:T(8,128)(2,1)}, u32[]{:S(2)}, u32[]{:S(2)}) async-start(bf16[32,16,1024]{2,1,0:T(8,128)(2,1)} %bitcast.11), calls=%async_computation | async-start | bytes 2097152 | tf_op jit(solution)/shard_map/dispatch/all_to_all | solution.py:333
  20.0 2.8 %collective-permute-start.2 = (bf16[176,1024]{1,0:T(8,128)(2,1)S(1)}, bf16[176,1024]{1,0:T(8,128)(2,1)S(1)}, u32[]{:S(2)}, u32[]{:S(2)}) collective-permute-start(bf16[176,1024]{1,0:T(8,128)(2,1)S(1)} %get-tuple-element.36), channel_id=1, source_target_pairs={{0,3},{1,2},{2,1},{3,0},{4,7},{5,6},{6,5},{7,4},{8,11},{9,10},{10,... | collective-permute-start | bytes 1081352 | tf_op jit(solution)/shard_map/exchange_weights/ppermute | solution.py:241
  22.8 12.1 %collective-permute-done.3.w1 = bf16[176,4096]{1,0:T(8,128)(2,1)} collective-permute-done((bf16[176,4096]{1,0:T(8,128)(2,1)}, bf16[176,4096]{1,0:T(8,128)(2,1)}, u32[]{:S(2)}, u32[]{:S(2)}) %collective-permute-start.3) | collective-permute-done | bytes 1441824 | tf_op jit(solution)/shard_map/exchange_weights/ppermute | solution.py:277
  34.9 3.0 %collective-permute-start.10 = (bf16[176,4096]{1,0:T(8,128)(2,1)S(1)}, bf16[176,4096]{1,0:T(8,128)(2,1)S(1)}, u32[]{:S(2)}, u32[]{:S(2)}) collective-permute-start(bf16[176,4096]{1,0:T(8,128)(2,1)S(1)} %bitcast.42), channel_id=1, source_target_pairs={{0,6},{1,7},{2,4},{3,5},{4,2},{5,3},{6,0},{7,1},{8,14},{9,15},{10,... | collective-permute-start | bytes 4325384 | tf_op jit(solution)/shard_map/exchange_weights/ppermute | solution.py:288
  38.5 4.0 %collective-permute-start.6 = (bf16[3,32,256]{2,1,0:T(8,128)(2,1)}, bf16[3,32,256]{2,1,0:T(8,128)(2,1)}, u32[]{:S(2)}, u32[]{:S(2)}) collective-permute-start(bf16[3,32,256]{2,1,0:T(8,128)(2,1)} %get-tuple-element.62), channel_id=1, source_target_pairs={{0,1},{1,2},{2,3},{3,4},{4,5},{5,6},{6,7},{8,9},{9,10},{10,11},{11... | collective-permute-start | bytes 147464 | tf_op jit(solution)/shard_map/cache/ppermute | solution.py:292
  43.8 2.5 %collective-permute-done.2 = bf16[176,1024]{1,0:T(8,128)(2,1)S(1)} collective-permute-done((bf16[176,1024]{1,0:T(8,128)(2,1)S(1)}, bf16[176,1024]{1,0:T(8,128)(2,1)S(1)}, u32[]{:S(2)}, u32[]{:S(2)}) %collective-permute-start.2) | collective-permute-done | bytes 360480 | tf_op jit(solution)/shard_map/exchange_weights/ppermute | solution.py:241
  50.3 1.9 %collective-permute-start.5 = (bf16[512,1024]{1,0:T(8,128)(2,1)}, bf16[512,1024]{1,0:T(8,128)(2,1)S(1)}, u32[]{:S(2)}, u32[]{:S(2)}) collective-permute-start(bf16[512,1024]{1,0:T(8,128)(2,1)} %bitcast.12.x0), channel_id=1, source_target_pairs={{0,2},{2,0},{1,3},{3,1},{4,6},{6,4},{5,7},{7,5},{8,10},{10,8},{9,1... | collective-permute-start | bytes 3145736 | tf_op jit(solution)/shard_map/gather/ppermute | solution.py:245
  53.7 15.0 %collective-permute-done.10.w3 = bf16[176,4096]{1,0:T(8,128)(2,1)S(1)} collective-permute-done((bf16[176,4096]{1,0:T(8,128)(2,1)S(1)}, bf16[176,4096]{1,0:T(8,128)(2,1)S(1)}, u32[]{:S(2)}, u32[]{:S(2)}) %collective-permute-start.10) | collective-permute-done | bytes 1441824 | tf_op jit(solution)/shard_map/exchange_weights/ppermute | solution.py:288
  68.7 2.9 %collective-permute-start.14 = (bf16[4,176,1024]{2,1,0:T(8,128)(2,1)S(1)}, bf16[4,176,1024]{2,1,0:T(8,128)(2,1)S(1)}, u32[]{:S(2)}, u32[]{:S(2)}) collective-permute-start(bf16[4,176,1024]{2,1,0:T(8,128)(2,1)S(1)} %pad_maximum_fusion.refs_0_), channel_id=1, source_target_pairs={{0,6},{1,7},{2,4},{3,5},{4,2},{5,3},{6,0},{7,1},{8,14},{9,15},{10,... | collective-permute-start | bytes 4325384 | tf_op jit(solution)/shard_map/gather/ppermute | solution.py:241
  71.5 2.8 %cache.1.past_ref = f32[160,256]{1,0:T(8,128)S(1)} custom-call(s32[7]{0:T(128)S(1)} %stack.42.sc, bf16[3,128,256]{2,1,0:T(8,128)(2,1)} %bitcast.53, bf16[3,32,256]{2,1,0:T(8,128)(2,1)} %collective-permute-done.6.above_ref, bf16[3,32,256]{2,1,0:T(8,128)(2,1)} %collective-permute-done.7.below_ref, bf16[3,3,3,256,256]{4,3,2,1,0:T(8,128)(2,1)} %time_ref.1, ...), custom_call_target="tpu_custom_call" | custom-call | flops 16000000000 | bytes 80000000 | tf_op jit(solution)/shard_map/cache/cache/pallas_call | solution.py:23
  76.3 1.8 %collective-permute-start.9 = (bf16[256,1024]{1,0:T(8,128)(2,1)S(1)}, bf16[256,1024]{1,0:T(8,128)(2,1)S(1)}, u32[]{:S(2)}, u32[]{:S(2)}) collective-permute-start(bf16[256,1024]{1,0:T(8,128)(2,1)S(1)} %slice.15), channel_id=1, source_target_pairs={{0,2},{2,0},{1,3},{3,1},{4,6},{6,4},{5,7},{7,5},{8,10},{10,8},{9,1... | collective-permute-start | bytes 1572872 | tf_op jit(solution)/shard_map/gather/ppermute | solution.py:245
  78.1 4.7 %first.1 = (f32[352,512]{1,0:T(8,128)S(1)}, f32[352,512]{1,0:T(8,128)S(1)}) custom-call(s32[7]{0:T(128)S(1)} %stack.42.sc, bf16[512,1024]{1,0:T(8,128)(2,1)} %bitcast.12.x0, bf16[512,1024]{1,0:T(8,128)(2,1)S(1)} %collective-permute-done.4.x1, bf16[512,1024]{1,0:T(8,128)(2,1)S(1)} %collective-permute-done.5.x2, bf16[176,4096]{1,0:T(8,128)(2,1)S(1)} %bitcast.40, ...), custom_call_target="tpu_custom_call" | custom-call | tf_op jit(solution)/shard_map/experts/first/pallas_call | solution.py:23
  82.7 4.8 %collective-permute-done.8.top_ref = bf16[256,1024]{1,0:T(8,128)(2,1)S(1)} collective-permute-done((bf16[256,1024]{1,0:T(8,128)(2,1)S(1)}, bf16[256,1024]{1,0:T(8,128)(2,1)S(1)}, u32[]{:S(2)}, u32[]{:S(2)}) %collective-permute-start.8) | collective-permute-done | bytes 524320 | tf_op jit(solution)/shard_map/gather/ppermute | solution.py:245
  88.9 2.5 %hidden.1.h0 = bf16[352,512]{1,0:T(8,128)(2,1)S(1)} custom-call(s32[7]{0:T(128)S(1)} %stack.42.sc, bf16[256,1024]{1,0:T(8,128)(2,1)S(1)} %collective-permute-done.8.top_ref, bf16[256,1024]{1,0:T(8,128)(2,1)S(1)} %collective-permute-done.9.low_ref, bf16[176,4096]{1,0:T(8,128)(2,1)S(1)} %bitcast.41, bf16[176,4096]{1,0:T(8,128)(2,1)} %collective-permute-done.3.w1, ...), custom_call_target="tpu_custom_call" | custom-call | tf_op jit(solution)/shard_map/experts/hidden/pallas_call | solution.py:23
  91.5 1.6 collective-permute-start.11
  95.1 7.0 %collective-permute-done.11.h1 = bf16[352,512]{1,0:T(8,128)(2,1)S(1)} collective-permute-done((bf16[352,512]{1,0:T(8,128)(2,1)S(1)}, bf16[352,512]{1,0:T(8,128)(2,1)S(1)}, u32[]{:S(2)}, u32[]{:S(2)}) %collective-permute-start.11) | collective-permute-done | bytes 360480 | tf_op jit(solution)/shard_map/hidden_gather/ppermute | solution.py:245
  102.0 2.4 %collective-permute-done.12.h2 = bf16[352,512]{1,0:T(8,128)(2,1)S(1)} collective-permute-done((bf16[352,512]{1,0:T(8,128)(2,1)S(1)}, bf16[352,512]{1,0:T(8,128)(2,1)S(1)}, u32[]{:S(2)}, u32[]{:S(2)}) %collective-permute-start.12) | collective-permute-done | bytes 360480 | tf_op jit(solution)/shard_map/hidden_gather/ppermute | solution.py:245
  104.4 4.2 %collective-permute-done.13.h3 = bf16[352,512]{1,0:T(8,128)(2,1)S(1)} collective-permute-done((bf16[352,512]{1,0:T(8,128)(2,1)S(1)}, bf16[352,512]{1,0:T(8,128)(2,1)S(1)}, u32[]{:S(2)}, u32[]{:S(2)}) %collective-permute-start.13) | collective-permute-done | bytes 360480 | tf_op jit(solution)/shard_map/hidden_gather/ppermute | solution.py:392
  108.6 2.9 %down.1 = bf16[2,512,512]{2,1,0:T(8,128)(2,1)S(1)} custom-call(s32[7]{0:T(128)S(1)} %stack.42.sc, bf16[352,512]{1,0:T(8,128)(2,1)S(1)} %hidden.1.h0, bf16[352,512]{1,0:T(8,128)(2,1)S(1)} %collective-permute-done.11.h1, bf16[352,512]{1,0:T(8,128)(2,1)S(1)} %collective-permute-done.12.h2, bf16[352,512]{1,0:T(8,128)(2,1)S(1)} %collective-permute-done.13.h3, ...), custom_call_target="tpu_custom_call" | custom-call | tf_op jit(solution)/shard_map/down/down/pallas_call | solution.py:23
  111.6 38.3 %all_to_all.15 = bf16[64,16,512]{2,1,0:T(8,128)(2,1)S(1)} all-to-all(bf16[64,16,512]{2,1,0:T(8,128)(2,1)S(1)} %bitcast.45), channel_id=1, replica_groups={{0,8,16,24,32,40,48,56,64,72,80,88,96,104,112,120,128,136,144,152,160,1..., dimensions={0} | all-to-all | bytes 2097152 | tf_op jit(solution)/shard_map/down/all_to_all | solution.py:405
  151.4 11.9 %all_to_all.16.arr_ref = bf16[8,48,384]{2,1,0:T(8,128)(2,1)S(1)} all-to-all(bf16[8,48,384]{2,1,0:T(8,128)(2,1)S(1)} %combine.1), channel_id=1, replica_groups=mesh['sess'=32,'yh'=2,'yl'=2,'x'=2] {'yh','yl','x'}, dimensions={0} | all-to-all | bytes 589824 | tf_op jit(solution)/shard_map/combine/all_to_all | solution.py:433
  163.3 2.2 %decode.1 = bf16[128,256]{1,0:T(8,128)(2,1)} custom-call(s32[7]{0:T(128)S(1)} %stack.42.sc, bf16[8,48,384]{2,1,0:T(8,128)(2,1)S(1)} %all_to_all.16.arr_ref, f32[160,256]{1,0:T(8,128)S(1)} %cache.1.past_ref, bf16[3,3,3,256,256]{4,3,2,1,0:T(8,128)(2,1)S(1)} %copy-done.4, bf16[3,3,256,256]{3,2,1,0:T(8,128)(2,1)S(1)} %copy-done.6, f32[1,256]{1,0:T(1,128)S(1)} %bitcast.49), custom_call_target="tpu_custom_call" | custom-call | tf_op jit(solution)/shard_map/decode/decode/pallas_call | solution.py:23
  (56 shorter events, 16.4 us)
Async XLA Ops:
  0.0 34.9 %collective-permute-start.3 = (bf16[176,4096]{1,0:T(8,128)(2,1)}, bf16[176,4096]{1,0:T(8,128)(2,1)}, u32[]{:S(2)}, u32[]{:S(2)}) collective-permute-start(bf16[176,4096]{1,0:T(8,128)(2,1)} %bitcast.39), channel_id=1, source_target_pairs={{0,6},{1,7},{2,4},{3,5},{4,2},{5,3},{6,0},{7,1},{8,14},{9,15},{10,... | collective-permute-start | bytes 4325384 | tf_op jit(solution)/shard_map/exchange_weights/ppermute | solution.py:277
  6.9 42.0 %all-to-all-start = ((bf16[32,16,1024]{2,1,0:T(8,128)(2,1)}), bf16[32,16,1024]{2,1,0:T(8,128)(2,1)}, u32[]{:S(2)}, u32[]{:S(2)}) async-start(bf16[32,16,1024]{2,1,0:T(8,128)(2,1)} %bitcast.11), calls=%async_computation | async-start | bytes 2097152 | tf_op jit(solution)/shard_map/dispatch/all_to_all | solution.py:333
  17.9 17.0 %copy-start.3 = (bf16[1,4096,176]{1,2,0:T(8,128)(2,1)S(1)}, bf16[1,4096,176]{1,2,0:T(8,128)(2,1)}, u32[]{:S(2)}) copy-start(bf16[1,4096,176]{1,2,0:T(8,128)(2,1)} %param.18) | copy-start | bytes 4325380
  17.9 20.0 %copy-start.15 = (bf16[3,1,8,16,256]{4,3,2,1,0:T(8,128)(2,1)S(1)}, bf16[3,1,8,16,256]{4,3,2,1,0:T(8,128)(2,1)}, u32[]{:S(2)}) copy-start(bf16[3,1,8,16,256]{4,3,2,1,0:T(8,128)(2,1)} %param.26) | copy-start | bytes 589828
  19.3 23.2 %collective-permute-start = (bf16[176,1024]{1,0:T(8,128)(2,1)S(1)}, bf16[176,1024]{1,0:T(8,128)(2,1)S(1)}, u32[]{:S(2)}, u32[]{:S(2)}) collective-permute-start(bf16[176,1024]{1,0:T(8,128)(2,1)S(1)} %get-tuple-element.34), channel_id=1, source_target_pairs={{0,1},{1,0},{2,3},{3,2},{4,5},{5,4},{6,7},{7,6},{8,9},{9,8},{10,11... | collective-permute-start | bytes 1081352 | tf_op jit(solution)/shard_map/exchange_weights/ppermute | solution.py:241
  19.9 23.9 %collective-permute-start.1 = (bf16[176,1024]{1,0:T(8,128)(2,1)S(1)}, bf16[176,1024]{1,0:T(8,128)(2,1)S(1)}, u32[]{:S(2)}, u32[]{:S(2)}) collective-permute-start(bf16[176,1024]{1,0:T(8,128)(2,1)S(1)} %get-tuple-element.35), channel_id=1, source_target_pairs={{0,2},{1,3},{2,0},{3,1},{4,6},{5,7},{6,4},{7,5},{8,10},{9,11},{10,... | collective-permute-start | bytes 1081352 | tf_op jit(solution)/shard_map/exchange_weights/ppermute | solution.py:241
  20.0 26.3 %collective-permute-start.2 = (bf16[176,1024]{1,0:T(8,128)(2,1)S(1)}, bf16[176,1024]{1,0:T(8,128)(2,1)S(1)}, u32[]{:S(2)}, u32[]{:S(2)}) collective-permute-start(bf16[176,1024]{1,0:T(8,128)(2,1)S(1)} %get-tuple-element.36), channel_id=1, source_target_pairs={{0,3},{1,2},{2,1},{3,0},{4,7},{5,6},{6,5},{7,4},{8,11},{9,10},{10,... | collective-permute-start | bytes 1081352 | tf_op jit(solution)/shard_map/exchange_weights/ppermute | solution.py:241
  34.9 33.7 %collective-permute-start.10 = (bf16[176,4096]{1,0:T(8,128)(2,1)S(1)}, bf16[176,4096]{1,0:T(8,128)(2,1)S(1)}, u32[]{:S(2)}, u32[]{:S(2)}) collective-permute-start(bf16[176,4096]{1,0:T(8,128)(2,1)S(1)} %bitcast.42), channel_id=1, source_target_pairs={{0,6},{1,7},{2,4},{3,5},{4,2},{5,3},{6,0},{7,1},{8,14},{9,15},{10,... | collective-permute-start | bytes 4325384 | tf_op jit(solution)/shard_map/exchange_weights/ppermute | solution.py:288
  38.5 33.0 %collective-permute-start.6 = (bf16[3,32,256]{2,1,0:T(8,128)(2,1)}, bf16[3,32,256]{2,1,0:T(8,128)(2,1)}, u32[]{:S(2)}, u32[]{:S(2)}) collective-permute-start(bf16[3,32,256]{2,1,0:T(8,128)(2,1)} %get-tuple-element.62), channel_id=1, source_target_pairs={{0,1},{1,2},{2,3},{3,4},{4,5},{5,6},{6,7},{8,9},{9,10},{10,11},{11... | collective-permute-start | bytes 147464 | tf_op jit(solution)/shard_map/cache/ppermute | solution.py:292
  42.5 29.0 %collective-permute-start.7 = (bf16[3,32,256]{2,1,0:T(8,128)(2,1)}, bf16[3,32,256]{2,1,0:T(8,128)(2,1)}, u32[]{:S(2)}, u32[]{:S(2)}) collective-permute-start(bf16[3,32,256]{2,1,0:T(8,128)(2,1)} %get-tuple-element.61), channel_id=1, source_target_pairs={{1,0},{2,1},{3,2},{4,3},{5,4},{6,5},{7,6},{9,8},{10,9},{11,10},{12... | collective-permute-start | bytes 147464 | tf_op jit(solution)/shard_map/cache/ppermute | solution.py:293
  48.9 25.4 %collective-permute-start.4 = (bf16[512,1024]{1,0:T(8,128)(2,1)}, bf16[512,1024]{1,0:T(8,128)(2,1)S(1)}, u32[]{:S(2)}, u32[]{:S(2)}) collective-permute-start(bf16[512,1024]{1,0:T(8,128)(2,1)} %bitcast.12.x0), channel_id=1, source_target_pairs={{0,1},{1,0},{2,3},{3,2},{4,5},{5,4},{6,7},{7,6},{8,9},{9,8},{10,11... | collective-permute-start | bytes 3145736 | tf_op jit(solution)/shard_map/gather/ppermute | solution.py:245
  50.3 24.4 %collective-permute-start.5 = (bf16[512,1024]{1,0:T(8,128)(2,1)}, bf16[512,1024]{1,0:T(8,128)(2,1)S(1)}, u32[]{:S(2)}, u32[]{:S(2)}) collective-permute-start(bf16[512,1024]{1,0:T(8,128)(2,1)} %bitcast.12.x0), channel_id=1, source_target_pairs={{0,2},{2,0},{1,3},{3,1},{4,6},{6,4},{5,7},{7,5},{8,10},{10,8},{9,1... | collective-permute-start | bytes 3145736 | tf_op jit(solution)/shard_map/gather/ppermute | solution.py:245
  68.7 40.0 %collective-permute-start.14 = (bf16[4,176,1024]{2,1,0:T(8,128)(2,1)S(1)}, bf16[4,176,1024]{2,1,0:T(8,128)(2,1)S(1)}, u32[]{:S(2)}, u32[]{:S(2)}) collective-permute-start(bf16[4,176,1024]{2,1,0:T(8,128)(2,1)S(1)} %pad_maximum_fusion.refs_0_), channel_id=1, source_target_pairs={{0,6},{1,7},{2,4},{3,5},{4,2},{5,3},{6,0},{7,1},{8,14},{9,15},{10,... | collective-permute-start | bytes 4325384 | tf_op jit(solution)/shard_map/gather/ppermute | solution.py:241
  74.7 12.8 %collective-permute-start.8 = (bf16[256,1024]{1,0:T(8,128)(2,1)S(1)}, bf16[256,1024]{1,0:T(8,128)(2,1)S(1)}, u32[]{:S(2)}, u32[]{:S(2)}) collective-permute-start(bf16[256,1024]{1,0:T(8,128)(2,1)S(1)} %slice.14), channel_id=1, source_target_pairs={{0,1},{1,0},{2,3},{3,2},{4,5},{5,4},{6,7},{7,6},{8,9},{9,8},{10,11... | collective-permute-start | bytes 1572872 | tf_op jit(solution)/shard_map/gather/ppermute | solution.py:245
  76.3 12.7 %collective-permute-start.9 = (bf16[256,1024]{1,0:T(8,128)(2,1)S(1)}, bf16[256,1024]{1,0:T(8,128)(2,1)S(1)}, u32[]{:S(2)}, u32[]{:S(2)}) collective-permute-start(bf16[256,1024]{1,0:T(8,128)(2,1)S(1)} %slice.15), channel_id=1, source_target_pairs={{0,2},{2,0},{1,3},{3,1},{4,6},{6,4},{5,7},{7,5},{8,10},{10,8},{9,1... | collective-permute-start | bytes 1572872 | tf_op jit(solution)/shard_map/gather/ppermute | solution.py:245
  91.5 10.5 %collective-permute-start.11 = (bf16[352,512]{1,0:T(8,128)(2,1)S(1)}, bf16[352,512]{1,0:T(8,128)(2,1)S(1)}, u32[]{:S(2)}, u32[]{:S(2)}) collective-permute-start(bf16[352,512]{1,0:T(8,128)(2,1)S(1)} %hidden.1.h0), channel_id=1, source_target_pairs={{0,2},{2,0},{1,3},{3,1},{4,6},{6,4},{5,7},{7,5},{8,10},{10,8},{9,1... | collective-permute-start | bytes 1081352 | tf_op jit(solution)/shard_map/hidden_gather/ppermute | solution.py:245
  93.1 11.3 %collective-permute-start.12 = (bf16[352,512]{1,0:T(8,128)(2,1)S(1)}, bf16[352,512]{1,0:T(8,128)(2,1)S(1)}, u32[]{:S(2)}, u32[]{:S(2)}) collective-permute-start(bf16[352,512]{1,0:T(8,128)(2,1)S(1)} %hidden.1.h0), channel_id=1, source_target_pairs={{0,1},{1,0},{2,3},{3,2},{4,5},{5,4},{6,7},{7,6},{8,9},{9,8},{10,11... | collective-permute-start | bytes 1081352 | tf_op jit(solution)/shard_map/hidden_gather/ppermute | solution.py:245
  93.7 14.9 %collective-permute-start.13 = (bf16[352,512]{1,0:T(8,128)(2,1)S(1)}, bf16[352,512]{1,0:T(8,128)(2,1)S(1)}, u32[]{:S(2)}, u32[]{:S(2)}) collective-permute-start(bf16[352,512]{1,0:T(8,128)(2,1)S(1)} %hidden.1.h0), channel_id=1, source_target_pairs={{0,3},{1,2},{2,1},{3,0},{4,7},{5,6},{6,5},{7,4},{8,11},{9,10},{10,... | collective-permute-start | bytes 1081352 | tf_op jit(solution)/shard_map/hidden_gather/ppermute | solution.py:392
  108.6 41.2 %copy-start.5 = (bf16[4096,256]{1,0:T(8,128)(2,1)S(1)}, bf16[4096,256]{1,0:T(8,128)(2,1)}, u32[]{:S(2)}) copy-start(bf16[4096,256]{1,0:T(8,128)(2,1)} %proj_ref.1) | copy-start | bytes 6291460
  108.6 41.2 %copy-start.8 = (bf16[256,1024]{1,0:T(8,128)(2,1)S(1)}, bf16[256,1024]{1,0:T(8,128)(2,1)}, u32[]{:S(2)}) copy-start(bf16[256,1024]{1,0:T(8,128)(2,1)} %copy-done.7) | copy-start | bytes 1572868
  108.6 41.2 %copy-start.10 = (f32[4096]{0:T(1024)S(1)}, f32[4096]{0:T(1024)}, u32[]{:S(2)}) copy-start(f32[4096]{0:T(1024)} %param.20) | copy-start | bytes 49156
  111.5 38.3 %copy-start.1 = (bf16[1,256,4096]{2,1,0:T(8,128)(2,1)S(1)}, bf16[1,256,4096]{2,1,0:T(8,128)(2,1)}, u32[]{:S(2)}) copy-start(bf16[1,256,4096]{2,1,0:T(8,128)(2,1)} %param.14) | copy-start | bytes 6291460
  149.9 13.4 %copy-start.4 = (bf16[3,3,3,256,256]{4,3,2,1,0:T(8,128)(2,1)S(1)}, bf16[3,3,3,256,256]{4,3,2,1,0:T(8,128)(2,1)}, u32[]{:S(2)}) copy-start(bf16[3,3,3,256,256]{4,3,2,1,0:T(8,128)(2,1)} %time_ref.1) | copy-start | bytes 10616836
  149.9 13.3 %copy-start.6 = (bf16[3,3,256,256]{3,2,1,0:T(8,128)(2,1)S(1)}, bf16[3,3,256,256]{3,2,1,0:T(8,128)(2,1)}, u32[]{:S(2)}) copy-start(bf16[3,3,256,256]{3,2,1,0:T(8,128)(2,1)} %space_ref.1) | copy-start | bytes 3538948
  (8 other events, 36.5 us)

commit v4 on v3

--- a/solution.py
+++ b/solution.py
@@ -133,18 +133,16 @@
 
 
 def down_kernel(sc, h0, h1, h2, h3, *refs):
-    near_ref, far_ref, out_ref, joined = refs
+    near_ref, far_ref, out_ref = refs
     part = near_ref.shape[1]
     share = out_ref.shape[2]
-    for step in range(4):
-        joined[step, 0:part, :] = near_ref[step]
-        joined[step, part : 2 * part, :] = far_ref[step]
     for side in range(2):
         cols = slice(side * share, (side + 1) * share)
-        total = turned(h0[...], joined[0, :, cols])
-        total += turned(h1[...], joined[1, :, cols])
-        total += turned(h2[...], joined[2, :, cols])
-        total += turned(h3[...], joined[3, :, cols])
+        total = turned(h0[0:part, :], near_ref[0, :, cols])
+        for step, ref in enumerate((h0, h1, h2, h3)):
+            if step:
+                total += turned(ref[0:part, :], near_ref[step, :, cols])
+            total += turned(ref[part : 2 * part, :], far_ref[step, :, cols])
         out_ref[side] = total.astype(BF16)
 
 
@@ -399,7 +397,7 @@
             (hidden, hidden_y, hidden_x, hidden_c, near, far),
             [whole((2 * hid, 512))] * 4 + [whole((4, hid, fourth))] * 2,
             jax.ShapeDtypeStruct((2, 512, share), BF16),
-            [pltpu.VMEM((4, 2 * hid, fourth), BF16)],
+            [],
             20,
         )
         returned = lax.all_to_all(

time: 166 us -> 166 us (level)
  no operation moved by 1% of the time
where the time goes in v4:
time: 166 us; the launch traced here: 165 us
  blocking collectives  50.2 us (30%)
  waiting for transfers between devices  49.6 us (30%)
  starting transfers between devices  38.7 us (23%)
  Pallas kernels  21.5 us (13%)
  local copies, waits for them, and re-layouts  3.12 us (2%)
    all_to_all x1, blocking collectives, body(): lax.all_to_all(answer.reshape(64, 16, share), ('sess',) + EXP, 0, 0, axis...  38.3 us
    pallas_call x9, Pallas kernels, call(): pl.pallas_call(kernel, name=name, out_shape=out_list, grid_spec=pltpu.Pre...  21.5 us
    ppermute x6, waiting for transfers between devices, swapped(): return lax.ppermute(x, axis, [(0, 1), (1, 0)])  15.9 us
    ppermute x1, waiting for transfers between devices, body(): other_up = lax.ppermute(later, EXP, pairs)  15 us
    ppermute x1, waiting for transfers between devices, body(): other_gate = lax.ppermute(own_gate, EXP, pairs)  12.1 us
    all_to_all x1, blocking collectives, body(): blocks = lax.all_to_all(blocks, EXP, 0, 0, tiled=True)  11.9 us
    all_to_all x1, starting transfers between devices, body(): lax.all_to_all(outgoing.reshape(32, 16, fourth), 'sess', 0, 0, tiled=True)  10.9 us
    ppermute x6, starting transfers between devices, swapped(): return lax.ppermute(x, axis, [(0, 1), (1, 0)])  8.77 us
  transfers between devices with their start and end apart: 16, of which 9 were waited for; matrix products, arithmetic and copies ran while one was open for 1% of the time, Pallas kernels for 9%

profile of v4, /device:TPU:64, one launch (start us, length us, event | category | flops | bytes accessed | tf_op | source)
XLA Modules:
  0.0 165.5 jit_solution(8552490597353270309)
XLA Ops:
  0.0 3.0 %collective-permute-start.3 = (bf16[176,4096]{1,0:T(8,128)(2,1)}, bf16[176,4096]{1,0:T(8,128)(2,1)}, u32[]{:S(2)}, u32[]{:S(2)}) collective-permute-start(bf16[176,4096]{1,0:T(8,128)(2,1)} %bitcast.39), channel_id=1, source_target_pairs={{0,6},{1,7},{2,4},{3,5},{4,2},{5,3},{6,0},{7,1},{8,14},{9,15},{10,... | collective-permute-start | bytes 4325384 | tf_op jit(solution)/shard_map/exchange_weights/ppermute | solution.py:275
  3.8 3.2 %dispatch.1 = (bf16[512,1024]{1,0:T(8,128)(2,1)}, f32[256,128]{1,0:T(8,128)S(1)}) custom-call(s32[7]{0:T(128)S(1)} %stack.42.sc, s32[2,256]{1,0:T(2,128)} %bitcast.55, f32[2,256]{1,0:T(2,128)} %bitcast.56, bf16[256,4096]{1,0:T(8,128)(2,1)} %bitcast.37), custom_call_target="tpu_custom_call" | custom-call | tf_op jit(solution)/shard_map/dispatch/dispatch/pallas_call | solution.py:23
  6.9 10.9 %all-to-all-start = ((bf16[32,16,1024]{2,1,0:T(8,128)(2,1)}), bf16[32,16,1024]{2,1,0:T(8,128)(2,1)}, u32[]{:S(2)}, u32[]{:S(2)}) async-start(bf16[32,16,1024]{2,1,0:T(8,128)(2,1)} %bitcast.11), calls=%async_computation | async-start | bytes 2097152 | tf_op jit(solution)/shard_map/dispatch/all_to_all | solution.py:331
  20.0 2.8 %collective-permute-start.2 = (bf16[176,1024]{1,0:T(8,128)(2,1)S(1)}, bf16[176,1024]{1,0:T(8,128)(2,1)S(1)}, u32[]{:S(2)}, u32[]{:S(2)}) collective-permute-start(bf16[176,1024]{1,0:T(8,128)(2,1)S(1)} %get-tuple-element.36), channel_id=1, source_target_pairs={{0,3},{1,2},{2,1},{3,0},{4,7},{5,6},{6,5},{7,4},{8,11},{9,10},{10,... | collective-permute-start | bytes 1081352 | tf_op jit(solution)/shard_map/exchange_weights/ppermute | solution.py:239
  22.8 12.1 %collective-permute-done.3.w1 = bf16[176,4096]{1,0:T(8,128)(2,1)} collective-permute-done((bf16[176,4096]{1,0:T(8,128)(2,1)}, bf16[176,4096]{1,0:T(8,128)(2,1)}, u32[]{:S(2)}, u32[]{:S(2)}) %collective-permute-start.3) | collective-permute-done | bytes 1441824 | tf_op jit(solution)/shard_map/exchange_weights/ppermute | solution.py:275
  34.9 3.0 %collective-permute-start.10 = (bf16[176,4096]{1,0:T(8,128)(2,1)S(1)}, bf16[176,4096]{1,0:T(8,128)(2,1)S(1)}, u32[]{:S(2)}, u32[]{:S(2)}) collective-permute-start(bf16[176,4096]{1,0:T(8,128)(2,1)S(1)} %bitcast.42), channel_id=1, source_target_pairs={{0,6},{1,7},{2,4},{3,5},{4,2},{5,3},{6,0},{7,1},{8,14},{9,15},{10,... | collective-permute-start | bytes 4325384 | tf_op jit(solution)/shard_map/exchange_weights/ppermute | solution.py:286
  38.5 4.0 %collective-permute-start.6 = (bf16[3,32,256]{2,1,0:T(8,128)(2,1)}, bf16[3,32,256]{2,1,0:T(8,128)(2,1)}, u32[]{:S(2)}, u32[]{:S(2)}) collective-permute-start(bf16[3,32,256]{2,1,0:T(8,128)(2,1)} %get-tuple-element.62), channel_id=1, source_target_pairs={{0,1},{1,2},{2,3},{3,4},{4,5},{5,6},{6,7},{8,9},{9,10},{10,11},{11... | collective-permute-start | bytes 147464 | tf_op jit(solution)/shard_map/cache/ppermute | solution.py:290
  43.8 2.5 %collective-permute-done.2 = bf16[176,1024]{1,0:T(8,128)(2,1)S(1)} collective-permute-done((bf16[176,1024]{1,0:T(8,128)(2,1)S(1)}, bf16[176,1024]{1,0:T(8,128)(2,1)S(1)}, u32[]{:S(2)}, u32[]{:S(2)}) %collective-permute-start.2) | collective-permute-done | bytes 360480 | tf_op jit(solution)/shard_map/exchange_weights/ppermute | solution.py:239
  50.3 1.9 %collective-permute-start.5 = (bf16[512,1024]{1,0:T(8,128)(2,1)}, bf16[512,1024]{1,0:T(8,128)(2,1)S(1)}, u32[]{:S(2)}, u32[]{:S(2)}) collective-permute-start(bf16[512,1024]{1,0:T(8,128)(2,1)} %bitcast.12.x0), channel_id=1, source_target_pairs={{0,2},{2,0},{1,3},{3,1},{4,6},{6,4},{5,7},{7,5},{8,10},{10,8},{9,1... | collective-permute-start | bytes 3145736 | tf_op jit(solution)/shard_map/gather/ppermute | solution.py:243
  53.7 15.0 %collective-permute-done.10.w3 = bf16[176,4096]{1,0:T(8,128)(2,1)S(1)} collective-permute-done((bf16[176,4096]{1,0:T(8,128)(2,1)S(1)}, bf16[176,4096]{1,0:T(8,128)(2,1)S(1)}, u32[]{:S(2)}, u32[]{:S(2)}) %collective-permute-start.10) | collective-permute-done | bytes 1441824 | tf_op jit(solution)/shard_map/exchange_weights/ppermute | solution.py:286
  68.7 2.9 %collective-permute-start.14 = (bf16[4,176,1024]{2,1,0:T(8,128)(2,1)S(1)}, bf16[4,176,1024]{2,1,0:T(8,128)(2,1)S(1)}, u32[]{:S(2)}, u32[]{:S(2)}) collective-permute-start(bf16[4,176,1024]{2,1,0:T(8,128)(2,1)S(1)} %pad_maximum_fusion.refs_0_), channel_id=1, source_target_pairs={{0,6},{1,7},{2,4},{3,5},{4,2},{5,3},{6,0},{7,1},{8,14},{9,15},{10,... | collective-permute-start | bytes 4325384 | tf_op jit(solution)/shard_map/gather/ppermute | solution.py:239
  71.5 2.8 %cache.1.past_ref = f32[160,256]{1,0:T(8,128)S(1)} custom-call(s32[7]{0:T(128)S(1)} %stack.42.sc, bf16[3,128,256]{2,1,0:T(8,128)(2,1)} %bitcast.53, bf16[3,32,256]{2,1,0:T(8,128)(2,1)} %collective-permute-done.6.above_ref, bf16[3,32,256]{2,1,0:T(8,128)(2,1)} %collective-permute-done.7.below_ref, bf16[3,3,3,256,256]{4,3,2,1,0:T(8,128)(2,1)} %time_ref.1, ...), custom_call_target="tpu_custom_call" | custom-call | flops 16000000000 | bytes 80000000 | tf_op jit(solution)/shard_map/cache/cache/pallas_call | solution.py:23
  76.3 1.8 %collective-permute-start.9 = (bf16[256,1024]{1,0:T(8,128)(2,1)S(1)}, bf16[256,1024]{1,0:T(8,128)(2,1)S(1)}, u32[]{:S(2)}, u32[]{:S(2)}) collective-permute-start(bf16[256,1024]{1,0:T(8,128)(2,1)S(1)} %slice.15), channel_id=1, source_target_pairs={{0,2},{2,0},{1,3},{3,1},{4,6},{6,4},{5,7},{7,5},{8,10},{10,8},{9,1... | collective-permute-start | bytes 1572872 | tf_op jit(solution)/shard_map/gather/ppermute | solution.py:243
  78.1 4.7 %first.1 = (f32[352,512]{1,0:T(8,128)S(1)}, f32[352,512]{1,0:T(8,128)S(1)}) custom-call(s32[7]{0:T(128)S(1)} %stack.42.sc, bf16[512,1024]{1,0:T(8,128)(2,1)} %bitcast.12.x0, bf16[512,1024]{1,0:T(8,128)(2,1)S(1)} %collective-permute-done.4.x1, bf16[512,1024]{1,0:T(8,128)(2,1)S(1)} %collective-permute-done.5.x2, bf16[176,4096]{1,0:T(8,128)(2,1)S(1)} %bitcast.40, ...), custom_call_target="tpu_custom_call" | custom-call | tf_op jit(solution)/shard_map/experts/first/pallas_call | solution.py:23
  82.7 4.8 %collective-permute-done.8.top_ref = bf16[256,1024]{1,0:T(8,128)(2,1)S(1)} collective-permute-done((bf16[256,1024]{1,0:T(8,128)(2,1)S(1)}, bf16[256,1024]{1,0:T(8,128)(2,1)S(1)}, u32[]{:S(2)}, u32[]{:S(2)}) %collective-permute-start.8) | collective-permute-done | bytes 524320 | tf_op jit(solution)/shard_map/gather/ppermute | solution.py:243
  88.9 2.5 %hidden.1.h0 = bf16[352,512]{1,0:T(8,128)(2,1)S(1)} custom-call(s32[7]{0:T(128)S(1)} %stack.42.sc, bf16[256,1024]{1,0:T(8,128)(2,1)S(1)} %collective-permute-done.8.top_ref, bf16[256,1024]{1,0:T(8,128)(2,1)S(1)} %collective-permute-done.9.low_ref, bf16[176,4096]{1,0:T(8,128)(2,1)S(1)} %bitcast.41, bf16[176,4096]{1,0:T(8,128)(2,1)} %collective-permute-done.3.w1, ...), custom_call_target="tpu_custom_call" | custom-call | tf_op jit(solution)/shard_map/experts/hidden/pallas_call | solution.py:23
  91.5 1.6 collective-permute-start.11
  95.1 7.0 %collective-permute-done.11.h1 = bf16[352,512]{1,0:T(8,128)(2,1)S(1)} collective-permute-done((bf16[352,512]{1,0:T(8,128)(2,1)S(1)}, bf16[352,512]{1,0:T(8,128)(2,1)S(1)}, u32[]{:S(2)}, u32[]{:S(2)}) %collective-permute-start.11) | collective-permute-done | bytes 360480 | tf_op jit(solution)/shard_map/hidden_gather/ppermute | solution.py:243
  102.0 2.4 %collective-permute-done.12.h2 = bf16[352,512]{1,0:T(8,128)(2,1)S(1)} collective-permute-done((bf16[352,512]{1,0:T(8,128)(2,1)S(1)}, bf16[352,512]{1,0:T(8,128)(2,1)S(1)}, u32[]{:S(2)}, u32[]{:S(2)}) %collective-permute-start.12) | collective-permute-done | bytes 360480 | tf_op jit(solution)/shard_map/hidden_gather/ppermute | solution.py:243
  104.4 4.2 %collective-permute-done.13.h3 = bf16[352,512]{1,0:T(8,128)(2,1)S(1)} collective-permute-done((bf16[352,512]{1,0:T(8,128)(2,1)S(1)}, bf16[352,512]{1,0:T(8,128)(2,1)S(1)}, u32[]{:S(2)}, u32[]{:S(2)}) %collective-permute-start.13) | collective-permute-done | bytes 360480 | tf_op jit(solution)/shard_map/hidden_gather/ppermute | solution.py:390
  108.6 2.9 %down.1 = bf16[2,512,512]{2,1,0:T(8,128)(2,1)S(1)} custom-call(s32[7]{0:T(128)S(1)} %stack.42.sc, bf16[352,512]{1,0:T(8,128)(2,1)S(1)} %hidden.1.h0, bf16[352,512]{1,0:T(8,128)(2,1)S(1)} %collective-permute-done.11.h1, bf16[352,512]{1,0:T(8,128)(2,1)S(1)} %collective-permute-done.12.h2, bf16[352,512]{1,0:T(8,128)(2,1)S(1)} %collective-permute-done.13.h3, ...), custom_call_target="tpu_custom_call" | custom-call | tf_op jit(solution)/shard_map/down/down/pallas_call | solution.py:23
  111.6 38.3 %all_to_all.15 = bf16[64,16,512]{2,1,0:T(8,128)(2,1)S(1)} all-to-all(bf16[64,16,512]{2,1,0:T(8,128)(2,1)S(1)} %bitcast.45), channel_id=1, replica_groups={{0,8,16,24,32,40,48,56,64,72,80,88,96,104,112,120,128,136,144,152,160,1..., dimensions={0} | all-to-all | bytes 2097152 | tf_op jit(solution)/shard_map/down/all_to_all | solution.py:403
  151.4 11.9 %all_to_all.16.arr_ref = bf16[8,48,384]{2,1,0:T(8,128)(2,1)S(1)} all-to-all(bf16[8,48,384]{2,1,0:T(8,128)(2,1)S(1)} %combine.1), channel_id=1, replica_groups=mesh['sess'=32,'yh'=2,'yl'=2,'x'=2] {'yh','yl','x'}, dimensions={0} | all-to-all | bytes 589824 | tf_op jit(solution)/shard_map/combine/all_to_all | solution.py:431
  163.3 2.2 %decode.1 = bf16[128,256]{1,0:T(8,128)(2,1)} custom-call(s32[7]{0:T(128)S(1)} %stack.42.sc, bf16[8,48,384]{2,1,0:T(8,128)(2,1)S(1)} %all_to_all.16.arr_ref, f32[160,256]{1,0:T(8,128)S(1)} %cache.1.past_ref, bf16[3,3,3,256,256]{4,3,2,1,0:T(8,128)(2,1)S(1)} %copy-done.4, bf16[3,3,256,256]{3,2,1,0:T(8,128)(2,1)S(1)} %copy-done.6, f32[1,256]{1,0:T(1,128)S(1)} %bitcast.49), custom_call_target="tpu_custom_call" | custom-call | tf_op jit(solution)/shard_map/decode/decode/pallas_call | solution.py:23
  (56 shorter events, 16.4 us)
Async XLA Ops:
  0.0 34.9 %collective-permute-start.3 = (bf16[176,4096]{1,0:T(8,128)(2,1)}, bf16[176,4096]{1,0:T(8,128)(2,1)}, u32[]{:S(2)}, u32[]{:S(2)}) collective-permute-start(bf16[176,4096]{1,0:T(8,128)(2,1)} %bitcast.39), channel_id=1, source_target_pairs={{0,6},{1,7},{2,4},{3,5},{4,2},{5,3},{6,0},{7,1},{8,14},{9,15},{10,... | collective-permute-start | bytes 4325384 | tf_op jit(solution)/shard_map/exchange_weights/ppermute | solution.py:275
  6.9 42.0 %all-to-all-start = ((bf16[32,16,1024]{2,1,0:T(8,128)(2,1)}), bf16[32,16,1024]{2,1,0:T(8,128)(2,1)}, u32[]{:S(2)}, u32[]{:S(2)}) async-start(bf16[32,16,1024]{2,1,0:T(8,128)(2,1)} %bitcast.11), calls=%async_computation | async-start | bytes 2097152 | tf_op jit(solution)/shard_map/dispatch/all_to_all | solution.py:331
  17.9 17.0 %copy-start.3 = (bf16[1,4096,176]{1,2,0:T(8,128)(2,1)S(1)}, bf16[1,4096,176]{1,2,0:T(8,128)(2,1)}, u32[]{:S(2)}) copy-start(bf16[1,4096,176]{1,2,0:T(8,128)(2,1)} %param.18) | copy-start | bytes 4325380
  17.9 20.0 %copy-start.15 = (bf16[3,1,8,16,256]{4,3,2,1,0:T(8,128)(2,1)S(1)}, bf16[3,1,8,16,256]{4,3,2,1,0:T(8,128)(2,1)}, u32[]{:S(2)}) copy-start(bf16[3,1,8,16,256]{4,3,2,1,0:T(8,128)(2,1)} %param.26) | copy-start | bytes 589828
  19.3 23.2 %collective-permute-start = (bf16[176,1024]{1,0:T(8,128)(2,1)S(1)}, bf16[176,1024]{1,0:T(8,128)(2,1)S(1)}, u32[]{:S(2)}, u32[]{:S(2)}) collective-permute-start(bf16[176,1024]{1,0:T(8,128)(2,1)S(1)} %get-tuple-element.34), channel_id=1, source_target_pairs={{0,1},{1,0},{2,3},{3,2},{4,5},{5,4},{6,7},{7,6},{8,9},{9,8},{10,11... | collective-permute-start | bytes 1081352 | tf_op jit(solution)/shard_map/exchange_weights/ppermute | solution.py:239
  19.9 23.9 %collective-permute-start.1 = (bf16[176,1024]{1,0:T(8,128)(2,1)S(1)}, bf16[176,1024]{1,0:T(8,128)(2,1)S(1)}, u32[]{:S(2)}, u32[]{:S(2)}) collective-permute-start(bf16[176,1024]{1,0:T(8,128)(2,1)S(1)} %get-tuple-element.35), channel_id=1, source_target_pairs={{0,2},{1,3},{2,0},{3,1},{4,6},{5,7},{6,4},{7,5},{8,10},{9,11},{10,... | collective-permute-start | bytes 1081352 | tf_op jit(solution)/shard_map/exchange_weights/ppermute | solution.py:239
  20.0 26.3 %collective-permute-start.2 = (bf16[176,1024]{1,0:T(8,128)(2,1)S(1)}, bf16[176,1024]{1,0:T(8,128)(2,1)S(1)}, u32[]{:S(2)}, u32[]{:S(2)}) collective-permute-start(bf16[176,1024]{1,0:T(8,128)(2,1)S(1)} %get-tuple-element.36), channel_id=1, source_target_pairs={{0,3},{1,2},{2,1},{3,0},{4,7},{5,6},{6,5},{7,4},{8,11},{9,10},{10,... | collective-permute-start | bytes 1081352 | tf_op jit(solution)/shard_map/exchange_weights/ppermute | solution.py:239
  34.9 33.7 %collective-permute-start.10 = (bf16[176,4096]{1,0:T(8,128)(2,1)S(1)}, bf16[176,4096]{1,0:T(8,128)(2,1)S(1)}, u32[]{:S(2)}, u32[]{:S(2)}) collective-permute-start(bf16[176,4096]{1,0:T(8,128)(2,1)S(1)} %bitcast.42), channel_id=1, source_target_pairs={{0,6},{1,7},{2,4},{3,5},{4,2},{5,3},{6,0},{7,1},{8,14},{9,15},{10,... | collective-permute-start | bytes 4325384 | tf_op jit(solution)/shard_map/exchange_weights/ppermute | solution.py:286
  38.5 33.0 %collective-permute-start.6 = (bf16[3,32,256]{2,1,0:T(8,128)(2,1)}, bf16[3,32,256]{2,1,0:T(8,128)(2,1)}, u32[]{:S(2)}, u32[]{:S(2)}) collective-permute-start(bf16[3,32,256]{2,1,0:T(8,128)(2,1)} %get-tuple-element.62), channel_id=1, source_target_pairs={{0,1},{1,2},{2,3},{3,4},{4,5},{5,6},{6,7},{8,9},{9,10},{10,11},{11... | collective-permute-start | bytes 147464 | tf_op jit(solution)/shard_map/cache/ppermute | solution.py:290
  42.5 29.0 %collective-permute-start.7 = (bf16[3,32,256]{2,1,0:T(8,128)(2,1)}, bf16[3,32,256]{2,1,0:T(8,128)(2,1)}, u32[]{:S(2)}, u32[]{:S(2)}) collective-permute-start(bf16[3,32,256]{2,1,0:T(8,128)(2,1)} %get-tuple-element.61), channel_id=1, source_target_pairs={{1,0},{2,1},{3,2},{4,3},{5,4},{6,5},{7,6},{9,8},{10,9},{11,10},{12... | collective-permute-start | bytes 147464 | tf_op jit(solution)/shard_map/cache/ppermute | solution.py:291
  48.9 25.4 %collective-permute-start.4 = (bf16[512,1024]{1,0:T(8,128)(2,1)}, bf16[512,1024]{1,0:T(8,128)(2,1)S(1)}, u32[]{:S(2)}, u32[]{:S(2)}) collective-permute-start(bf16[512,1024]{1,0:T(8,128)(2,1)} %bitcast.12.x0), channel_id=1, source_target_pairs={{0,1},{1,0},{2,3},{3,2},{4,5},{5,4},{6,7},{7,6},{8,9},{9,8},{10,11... | collective-permute-start | bytes 3145736 | tf_op jit(solution)/shard_map/gather/ppermute | solution.py:243
  50.3 24.4 %collective-permute-start.5 = (bf16[512,1024]{1,0:T(8,128)(2,1)}, bf16[512,1024]{1,0:T(8,128)(2,1)S(1)}, u32[]{:S(2)}, u32[]{:S(2)}) collective-permute-start(bf16[512,1024]{1,0:T(8,128)(2,1)} %bitcast.12.x0), channel_id=1, source_target_pairs={{0,2},{2,0},{1,3},{3,1},{4,6},{6,4},{5,7},{7,5},{8,10},{10,8},{9,1... | collective-permute-start | bytes 3145736 | tf_op jit(solution)/shard_map/gather/ppermute | solution.py:243
  68.7 40.0 %collective-permute-start.14 = (bf16[4,176,1024]{2,1,0:T(8,128)(2,1)S(1)}, bf16[4,176,1024]{2,1,0:T(8,128)(2,1)S(1)}, u32[]{:S(2)}, u32[]{:S(2)}) collective-permute-start(bf16[4,176,1024]{2,1,0:T(8,128)(2,1)S(1)} %pad_maximum_fusion.refs_0_), channel_id=1, source_target_pairs={{0,6},{1,7},{2,4},{3,5},{4,2},{5,3},{6,0},{7,1},{8,14},{9,15},{10,... | collective-permute-start | bytes 4325384 | tf_op jit(solution)/shard_map/gather/ppermute | solution.py:239
  74.7 12.8 %collective-permute-start.8 = (bf16[256,1024]{1,0:T(8,128)(2,1)S(1)}, bf16[256,1024]{1,0:T(8,128)(2,1)S(1)}, u32[]{:S(2)}, u32[]{:S(2)}) collective-permute-start(bf16[256,1024]{1,0:T(8,128)(2,1)S(1)} %slice.14), channel_id=1, source_target_pairs={{0,1},{1,0},{2,3},{3,2},{4,5},{5,4},{6,7},{7,6},{8,9},{9,8},{10,11... | collective-permute-start | bytes 1572872 | tf_op jit(solution)/shard_map/gather/ppermute | solution.py:243
  76.3 12.7 %collective-permute-start.9 = (bf16[256,1024]{1,0:T(8,128)(2,1)S(1)}, bf16[256,1024]{1,0:T(8,128)(2,1)S(1)}, u32[]{:S(2)}, u32[]{:S(2)}) collective-permute-start(bf16[256,1024]{1,0:T(8,128)(2,1)S(1)} %slice.15), channel_id=1, source_target_pairs={{0,2},{2,0},{1,3},{3,1},{4,6},{6,4},{5,7},{7,5},{8,10},{10,8},{9,1... | collective-permute-start | bytes 1572872 | tf_op jit(solution)/shard_map/gather/ppermute | solution.py:243
  91.5 10.5 %collective-permute-start.11 = (bf16[352,512]{1,0:T(8,128)(2,1)S(1)}, bf16[352,512]{1,0:T(8,128)(2,1)S(1)}, u32[]{:S(2)}, u32[]{:S(2)}) collective-permute-start(bf16[352,512]{1,0:T(8,128)(2,1)S(1)} %hidden.1.h0), channel_id=1, source_target_pairs={{0,2},{2,0},{1,3},{3,1},{4,6},{6,4},{5,7},{7,5},{8,10},{10,8},{9,1... | collective-permute-start | bytes 1081352 | tf_op jit(solution)/shard_map/hidden_gather/ppermute | solution.py:243
  93.1 11.3 %collective-permute-start.12 = (bf16[352,512]{1,0:T(8,128)(2,1)S(1)}, bf16[352,512]{1,0:T(8,128)(2,1)S(1)}, u32[]{:S(2)}, u32[]{:S(2)}) collective-permute-start(bf16[352,512]{1,0:T(8,128)(2,1)S(1)} %hidden.1.h0), channel_id=1, source_target_pairs={{0,1},{1,0},{2,3},{3,2},{4,5},{5,4},{6,7},{7,6},{8,9},{9,8},{10,11... | collective-permute-start | bytes 1081352 | tf_op jit(solution)/shard_map/hidden_gather/ppermute | solution.py:243
  93.7 14.9 %collective-permute-start.13 = (bf16[352,512]{1,0:T(8,128)(2,1)S(1)}, bf16[352,512]{1,0:T(8,128)(2,1)S(1)}, u32[]{:S(2)}, u32[]{:S(2)}) collective-permute-start(bf16[352,512]{1,0:T(8,128)(2,1)S(1)} %hidden.1.h0), channel_id=1, source_target_pairs={{0,3},{1,2},{2,1},{3,0},{4,7},{5,6},{6,5},{7,4},{8,11},{9,10},{10,... | collective-permute-start | bytes 1081352 | tf_op jit(solution)/shard_map/hidden_gather/ppermute | solution.py:390
  108.6 41.3 %copy-start.5 = (bf16[4096,256]{1,0:T(8,128)(2,1)S(1)}, bf16[4096,256]{1,0:T(8,128)(2,1)}, u32[]{:S(2)}) copy-start(bf16[4096,256]{1,0:T(8,128)(2,1)} %proj_ref.1) | copy-start | bytes 6291460
  108.6 41.3 %copy-start.8 = (bf16[256,1024]{1,0:T(8,128)(2,1)S(1)}, bf16[256,1024]{1,0:T(8,128)(2,1)}, u32[]{:S(2)}) copy-start(bf16[256,1024]{1,0:T(8,128)(2,1)} %copy-done.7) | copy-start | bytes 1572868
  108.6 41.3 %copy-start.10 = (f32[4096]{0:T(1024)S(1)}, f32[4096]{0:T(1024)}, u32[]{:S(2)}) copy-start(f32[4096]{0:T(1024)} %param.20) | copy-start | bytes 49156
  111.6 38.3 %copy-start.1 = (bf16[1,256,4096]{2,1,0:T(8,128)(2,1)S(1)}, bf16[1,256,4096]{2,1,0:T(8,128)(2,1)}, u32[]{:S(2)}) copy-start(bf16[1,256,4096]{2,1,0:T(8,128)(2,1)} %param.14) | copy-start | bytes 6291460
  149.9 13.4 %copy-start.4 = (bf16[3,3,3,256,256]{4,3,2,1,0:T(8,128)(2,1)S(1)}, bf16[3,3,3,256,256]{4,3,2,1,0:T(8,128)(2,1)}, u32[]{:S(2)}) copy-start(bf16[3,3,3,256,256]{4,3,2,1,0:T(8,128)(2,1)} %time_ref.1) | copy-start | bytes 10616836
  149.9 13.3 %copy-start.6 = (bf16[3,3,256,256]{3,2,1,0:T(8,128)(2,1)S(1)}, bf16[3,3,256,256]{3,2,1,0:T(8,128)(2,1)}, u32[]{:S(2)}) copy-start(bf16[3,3,256,256]{3,2,1,0:T(8,128)(2,1)} %space_ref.1) | copy-start | bytes 3538948
  (8 other events, 36.5 us)

commit v5 on v4

--- a/solution.py
+++ b/solution.py
@@ -41,10 +41,8 @@
     return lax.broadcasted_iota(jnp.int32, shape, dim)
 
 
-def dispatch_kernel(sc, routes_ref, gates_ref, tok_ref, out_ref, col_ref):
-    half = sc[1]
+def places_of(routes_ref, rows):
     count = routes_ref.shape[1]
-    rows = out_ref.shape[0]
     experts = iota((32, count), 0)
     first = routes_ref[0:1, :]
     second = routes_ref[1:2, :]
@@ -57,9 +55,22 @@
     pos_b = jnp.sum(jnp.where(is_second, before, 0.0), axis=0, keepdims=True).astype(jnp.int32)
     place_a = (pos_a >> 4) * rows + first * 16 + (pos_a & 15)
     place_b = (pos_b >> 4) * rows + second * 16 + (pos_b & 15)
+    return place_a, place_b
+
+
+def dispatch_kernel(sc, routes_ref, tok_ref, out_ref):
+    half = sc[1]
+    count = routes_ref.shape[1]
+    rows = out_ref.shape[0]
+    place_a, place_b = places_of(routes_ref, rows)
     slot = iota((rows, count), 0) + half * rows
     pick = jnp.where((slot == place_a) | (slot == place_b), 1.0, 0.0).astype(BF16)
     out_ref[...] = jnp.dot(pick, tok_ref[...], preferred_element_type=F32).astype(BF16)
+
+
+def columns_kernel(sc, routes_ref, gates_ref, col_ref):
+    count = routes_ref.shape[1]
+    place_a, place_b = places_of(routes_ref, 512)
     line = iota((128, count), 0)
     table = jnp.where(
         line == 0,
@@ -282,7 +293,15 @@
             [jax.ShapeDtypeStruct((hid, fourth), BF16)] * 4,
         )
         near_1, near_2, near_3 = [flipped(slabs[k], k) for k in (1, 2, 3)]
-        later, other_gate = lax.optimization_barrier((own_up, other_gate))
+        columns = call(
+            columns_kernel,
+            "columns",
+            scalars,
+            (in_hbm(routes[0].T), in_hbm(gates[0].T)),
+            [whole((2, count))] * 2,
+            jax.ShapeDtypeStruct((count, 128), F32),
+        )
+        later, other_gate, columns = lax.optimization_barrier((own_up, other_gate, columns))
         other_up = lax.ppermute(later, EXP, pairs)
 
     with jax.named_scope("cache"):
@@ -313,20 +332,13 @@
         )
 
     with jax.named_scope("dispatch"):
-        outgoing, columns = call(
+        outgoing = call(
             dispatch_kernel,
             "dispatch",
             scalars,
-            (in_hbm(routes[0].T), in_hbm(gates[0].T), in_hbm(tokens[0])),
-            [
-                whole((2, count)),
-                whole((2, count)),
-                pl.BlockSpec((count, fourth), lambda i, s: (0, s[3])),
-            ],
-            [
-                jax.ShapeDtypeStruct((512, fourth), BF16),
-                jax.ShapeDtypeStruct((count, 128), F32),
-            ],
+            (in_hbm(routes[0].T), in_hbm(tokens[0])),
+            [whole((2, count)), pl.BlockSpec((count, fourth), lambda i, s: (0, s[3]))],
+            jax.ShapeDtypeStruct((512, fourth), BF16),
         )
         arrived = lax.all_to_all(
             outgoing.reshape(32, 16, fourth), "sess", 0, 0, tiled=True

time: 166 us -> 166 us (level)
    pallas_call x9 -> x10, Pallas kernels: 21.5 us -> 23 us  [call(): pl.pallas_call(kernel, name=name, out_shape=out_list, grid_spec=pltpu.Pre...]
  transfers between devices with their start and end apart: 16 -> 16, of which waited for: 9 -> 8; matrix products, arithmetic and copies ran while one was open for 1% -> 1% of each run, Pallas kernels for 9% -> 10%
where the time goes in v5:
time: 166 us; the launch traced here: 165 us
  blocking collectives  50.5 us (30%)
  waiting for transfers between devices  48.1 us (29%)
  starting transfers between devices  37.8 us (23%)
  Pallas kernels  23 us (14%)
  local copies, waits for them, and re-layouts  3.11 us (2%)
    all_to_all x1, blocking collectives, body(): lax.all_to_all(answer.reshape(64, 16, share), ('sess',) + EXP, 0, 0, axis...  38.4 us
    pallas_call x10, Pallas kernels, call(): pl.pallas_call(kernel, name=name, out_shape=out_list, grid_spec=pltpu.Pre...  23 us
    ppermute x1, waiting for transfers between devices, body(): other_up = lax.ppermute(later, EXP, pairs)  15.6 us
    ppermute x6, waiting for transfers between devices, swapped(): return lax.ppermute(x, axis, [(0, 1), (1, 0)])  15.6 us
    all_to_all x1, blocking collectives, body(): blocks = lax.all_to_all(blocks, EXP, 0, 0, tiled=True)  12.1 us
    all_to_all x1, starting transfers between devices, body(): lax.all_to_all(outgoing.reshape(32, 16, fourth), 'sess', 0, 0, tiled=True)  10.9 us
    ppermute x1, waiting for transfers between devices, body(): other_gate = lax.ppermute(own_gate, EXP, pairs)  10.6 us
    ppermute x6, starting transfers between devices, swapped(): return lax.ppermute(x, axis, [(0, 1), (1, 0)])  8.45 us
  transfers between devices with their start and end apart: 16, of which 8 were waited for; matrix products, arithmetic and copies ran while one was open for 1% of the time, Pallas kernels for 10%

profile of v5, /device:TPU:64, one launch (start us, length us, event | category | flops | bytes accessed | tf_op | source)
XLA Modules:
  0.0 164.8 jit_solution(16964743737158270862)
XLA Ops:
  0.0 3.0 %collective-permute-start.3 = (bf16[176,4096]{1,0:T(8,128)(2,1)}, bf16[176,4096]{1,0:T(8,128)(2,1)}, u32[]{:S(2)}, u32[]{:S(2)}) collective-permute-start(bf16[176,4096]{1,0:T(8,128)(2,1)} %bitcast.39), channel_id=1, source_target_pairs={{0,6},{1,7},{2,4},{3,5},{4,2},{5,3},{6,0},{7,1},{8,14},{9,15},{10,... | collective-permute-start | bytes 4325384 | tf_op jit(solution)/shard_map/exchange_weights/ppermute | solution.py:286
  3.8 3.2 %dispatch.1 = bf16[512,1024]{1,0:T(8,128)(2,1)} custom-call(s32[7]{0:T(128)S(1)} %stack.42.sc, s32[2,256]{1,0:T(2,128)} %bitcast.54, bf16[256,4096]{1,0:T(8,128)(2,1)} %bitcast.37), custom_call_target="tpu_custom_call" | custom-call | tf_op jit(solution)/shard_map/dispatch/dispatch/pallas_call | solution.py:23
  6.9 10.9 %all-to-all-start = ((bf16[32,16,1024]{2,1,0:T(8,128)(2,1)}), bf16[32,16,1024]{2,1,0:T(8,128)(2,1)}, u32[]{:S(2)}, u32[]{:S(2)}) async-start(bf16[32,16,1024]{2,1,0:T(8,128)(2,1)} %bitcast.9), calls=%async_computation | async-start | bytes 2097152 | tf_op jit(solution)/shard_map/dispatch/all_to_all | solution.py:343
  20.0 2.8 %collective-permute-start.2 = (bf16[176,1024]{1,0:T(8,128)(2,1)S(1)}, bf16[176,1024]{1,0:T(8,128)(2,1)}, u32[]{:S(2)}, u32[]{:S(2)}) collective-permute-start(bf16[176,1024]{1,0:T(8,128)(2,1)S(1)} %get-tuple-element.34), channel_id=1, source_target_pairs={{0,3},{1,2},{2,1},{3,0},{4,7},{5,6},{6,5},{7,4},{8,11},{9,10},{10,... | collective-permute-start | bytes 1081352 | tf_op jit(solution)/shard_map/exchange_weights/ppermute | solution.py:250
  24.3 10.6 %collective-permute-done.3.w1 = bf16[176,4096]{1,0:T(8,128)(2,1)} collective-permute-done((bf16[176,4096]{1,0:T(8,128)(2,1)}, bf16[176,4096]{1,0:T(8,128)(2,1)}, u32[]{:S(2)}, u32[]{:S(2)}) %collective-permute-start.3) | collective-permute-done | bytes 1441824 | tf_op jit(solution)/shard_map/exchange_weights/ppermute | solution.py:286
  34.9 3.0 %collective-permute-start.10 = (bf16[176,4096]{1,0:T(8,128)(2,1)S(1)}, bf16[176,4096]{1,0:T(8,128)(2,1)S(1)}, u32[]{:S(2)}, u32[]{:S(2)}) collective-permute-start(bf16[176,4096]{1,0:T(8,128)(2,1)S(1)} %bitcast.42), channel_id=1, source_target_pairs={{0,6},{1,7},{2,4},{3,5},{4,2},{5,3},{6,0},{7,1},{8,14},{9,15},{10,... | collective-permute-start | bytes 4325384 | tf_op jit(solution)/shard_map/exchange_weights/ppermute | solution.py:305
  38.5 3.4 %collective-permute-start.6 = (bf16[3,32,256]{2,1,0:T(8,128)(2,1)}, bf16[3,32,256]{2,1,0:T(8,128)(2,1)S(1)}, u32[]{:S(2)}, u32[]{:S(2)}) collective-permute-start(bf16[3,32,256]{2,1,0:T(8,128)(2,1)} %get-tuple-element.60), channel_id=1, source_target_pairs={{0,1},{1,2},{2,3},{3,4},{4,5},{5,6},{6,7},{8,9},{9,10},{10,11},{11... | collective-permute-start | bytes 147464 | tf_op jit(solution)/shard_map/cache/ppermute | solution.py:309
  44.0 2.4 %collective-permute-done.2 = bf16[176,1024]{1,0:T(8,128)(2,1)} collective-permute-done((bf16[176,1024]{1,0:T(8,128)(2,1)S(1)}, bf16[176,1024]{1,0:T(8,128)(2,1)}, u32[]{:S(2)}, u32[]{:S(2)}) %collective-permute-start.2) | collective-permute-done | bytes 360480 | tf_op jit(solution)/shard_map/exchange_weights/ppermute | solution.py:250
  49.6 1.9 %collective-permute-start.5 = (bf16[512,1024]{1,0:T(8,128)(2,1)}, bf16[512,1024]{1,0:T(8,128)(2,1)S(1)}, u32[]{:S(2)}, u32[]{:S(2)}) collective-permute-start(bf16[512,1024]{1,0:T(8,128)(2,1)} %bitcast.10.x0), channel_id=1, source_target_pairs={{0,2},{2,0},{1,3},{3,1},{4,6},{6,4},{5,7},{7,5},{8,10},{10,8},{9,1... | collective-permute-start | bytes 3145736 | tf_op jit(solution)/shard_map/gather/ppermute | solution.py:254
  53.0 15.6 %collective-permute-done.10.w3 = bf16[176,4096]{1,0:T(8,128)(2,1)S(1)} collective-permute-done((bf16[176,4096]{1,0:T(8,128)(2,1)S(1)}, bf16[176,4096]{1,0:T(8,128)(2,1)S(1)}, u32[]{:S(2)}, u32[]{:S(2)}) %collective-permute-start.10) | collective-permute-done | bytes 1441824 | tf_op jit(solution)/shard_map/exchange_weights/ppermute | solution.py:305
  68.7 2.9 %collective-permute-start.14 = (bf16[4,176,1024]{2,1,0:T(8,128)(2,1)S(1)}, bf16[4,176,1024]{2,1,0:T(8,128)(2,1)S(1)}, u32[]{:S(2)}, u32[]{:S(2)}) collective-permute-start(bf16[4,176,1024]{2,1,0:T(8,128)(2,1)S(1)} %pad_maximum_fusion.refs_0_), channel_id=1, source_target_pairs={{0,6},{1,7},{2,4},{3,5},{4,2},{5,3},{6,0},{7,1},{8,14},{9,15},{10,... | collective-permute-start | bytes 4325384 | tf_op jit(solution)/shard_map/gather/ppermute | solution.py:250
  71.5 2.8 %cache.1.past_ref = f32[160,256]{1,0:T(8,128)S(1)} custom-call(s32[7]{0:T(128)S(1)} %stack.42.sc, bf16[3,128,256]{2,1,0:T(8,128)(2,1)} %bitcast.52, bf16[3,32,256]{2,1,0:T(8,128)(2,1)S(1)} %collective-permute-done.6.above_ref, bf16[3,32,256]{2,1,0:T(8,128)(2,1)S(1)} %collective-permute-done.7.below_ref, bf16[3,3,3,256,256]{4,3,2,1,0:T(8,128)(2,1)} %time_ref.1, ...), custom_call_target="tpu_custom_call" | custom-call | flops 16000000000 | bytes 80000000 | tf_op jit(solution)/shard_map/cache/cache/pallas_call | solution.py:23
  77.4 4.7 %first.1 = (f32[352,512]{1,0:T(8,128)S(1)}, f32[352,512]{1,0:T(8,128)S(1)}) custom-call(s32[7]{0:T(128)S(1)} %stack.42.sc, bf16[512,1024]{1,0:T(8,128)(2,1)} %bitcast.10.x0, bf16[512,1024]{1,0:T(8,128)(2,1)S(1)} %collective-permute-done.4.x1, bf16[512,1024]{1,0:T(8,128)(2,1)S(1)} %collective-permute-done.5.x2, bf16[176,4096]{1,0:T(8,128)(2,1)S(1)} %bitcast.40, ...), custom_call_target="tpu_custom_call" | custom-call | tf_op jit(solution)/shard_map/experts/first/pallas_call | solution.py:23
  82.1 4.6 %collective-permute-done.8.top_ref = bf16[256,1024]{1,0:T(8,128)(2,1)S(1)} collective-permute-done((bf16[256,1024]{1,0:T(8,128)(2,1)S(1)}, bf16[256,1024]{1,0:T(8,128)(2,1)S(1)}, u32[]{:S(2)}, u32[]{:S(2)}) %collective-permute-start.8) | collective-permute-done | bytes 524320 | tf_op jit(solution)/shard_map/gather/ppermute | solution.py:254
  86.7 1.6 collective-permute-done.9.low_ref
  88.3 2.5 %hidden.1.h0 = bf16[352,512]{1,0:T(8,128)(2,1)S(1)} custom-call(s32[7]{0:T(128)S(1)} %stack.42.sc, bf16[256,1024]{1,0:T(8,128)(2,1)S(1)} %collective-permute-done.8.top_ref, bf16[256,1024]{1,0:T(8,128)(2,1)S(1)} %collective-permute-done.9.low_ref, bf16[176,4096]{1,0:T(8,128)(2,1)S(1)} %bitcast.41, bf16[176,4096]{1,0:T(8,128)(2,1)} %collective-permute-done.3.w1, ...), custom_call_target="tpu_custom_call" | custom-call | tf_op jit(solution)/shard_map/experts/hidden/pallas_call | solution.py:23
  90.8 1.6 collective-permute-start.11
  94.4 6.8 %collective-permute-done.11.h1 = bf16[352,512]{1,0:T(8,128)(2,1)S(1)} collective-permute-done((bf16[352,512]{1,0:T(8,128)(2,1)S(1)}, bf16[352,512]{1,0:T(8,128)(2,1)S(1)}, u32[]{:S(2)}, u32[]{:S(2)}) %collective-permute-start.11) | collective-permute-done | bytes 360480 | tf_op jit(solution)/shard_map/hidden_gather/ppermute | solution.py:254
  101.2 2.5 %collective-permute-done.12.h2 = bf16[352,512]{1,0:T(8,128)(2,1)S(1)} collective-permute-done((bf16[352,512]{1,0:T(8,128)(2,1)S(1)}, bf16[352,512]{1,0:T(8,128)(2,1)S(1)}, u32[]{:S(2)}, u32[]{:S(2)}) %collective-permute-start.12) | collective-permute-done | bytes 360480 | tf_op jit(solution)/shard_map/hidden_gather/ppermute | solution.py:254
  103.8 3.8 %collective-permute-done.13.h3 = bf16[352,512]{1,0:T(8,128)(2,1)S(1)} collective-permute-done((bf16[352,512]{1,0:T(8,128)(2,1)S(1)}, bf16[352,512]{1,0:T(8,128)(2,1)S(1)}, u32[]{:S(2)}, u32[]{:S(2)}) %collective-permute-start.13) | collective-permute-done | bytes 360480 | tf_op jit(solution)/shard_map/hidden_gather/ppermute | solution.py:402
  107.6 3.0 %down.1 = bf16[2,512,512]{2,1,0:T(8,128)(2,1)S(1)} custom-call(s32[7]{0:T(128)S(1)} %stack.42.sc, bf16[352,512]{1,0:T(8,128)(2,1)S(1)} %hidden.1.h0, bf16[352,512]{1,0:T(8,128)(2,1)S(1)} %collective-permute-done.11.h1, bf16[352,512]{1,0:T(8,128)(2,1)S(1)} %collective-permute-done.12.h2, bf16[352,512]{1,0:T(8,128)(2,1)S(1)} %collective-permute-done.13.h3, ...), custom_call_target="tpu_custom_call" | custom-call | tf_op jit(solution)/shard_map/down/down/pallas_call | solution.py:23
  110.6 38.4 %all_to_all.15 = bf16[64,16,512]{2,1,0:T(8,128)(2,1)S(1)} all-to-all(bf16[64,16,512]{2,1,0:T(8,128)(2,1)S(1)} %bitcast.45), channel_id=1, replica_groups={{0,8,16,24,32,40,48,56,64,72,80,88,96,104,112,120,128,136,144,152,160,1..., dimensions={0} | all-to-all | bytes 2097152 | tf_op jit(solution)/shard_map/down/all_to_all | solution.py:415
  150.5 12.1 %all_to_all.16.arr_ref = bf16[8,48,384]{2,1,0:T(8,128)(2,1)S(1)} all-to-all(bf16[8,48,384]{2,1,0:T(8,128)(2,1)S(1)} %combine.1), channel_id=1, replica_groups=mesh['sess'=32,'yh'=2,'yl'=2,'x'=2] {'yh','yl','x'}, dimensions={0} | all-to-all | bytes 589824 | tf_op jit(solution)/shard_map/combine/all_to_all | solution.py:443
  162.6 2.2 %decode.1 = bf16[128,256]{1,0:T(8,128)(2,1)} custom-call(s32[7]{0:T(128)S(1)} %stack.42.sc, bf16[8,48,384]{2,1,0:T(8,128)(2,1)S(1)} %all_to_all.16.arr_ref, f32[160,256]{1,0:T(8,128)S(1)} %cache.1.past_ref, bf16[3,3,3,256,256]{4,3,2,1,0:T(8,128)(2,1)S(1)} %copy-done.4, bf16[3,3,256,256]{3,2,1,0:T(8,128)(2,1)S(1)} %copy-done.6, f32[1,256]{1,0:T(1,128)S(1)} %bitcast.49), custom_call_target="tpu_custom_call" | custom-call | tf_op jit(solution)/shard_map/decode/decode/pallas_call | solution.py:23
  (55 shorter events, 17.7 us)
Async XLA Ops:
  0.0 34.9 %collective-permute-start.3 = (bf16[176,4096]{1,0:T(8,128)(2,1)}, bf16[176,4096]{1,0:T(8,128)(2,1)}, u32[]{:S(2)}, u32[]{:S(2)}) collective-permute-start(bf16[176,4096]{1,0:T(8,128)(2,1)} %bitcast.39), channel_id=1, source_target_pairs={{0,6},{1,7},{2,4},{3,5},{4,2},{5,3},{6,0},{7,1},{8,14},{9,15},{10,... | collective-permute-start | bytes 4325384 | tf_op jit(solution)/shard_map/exchange_weights/ppermute | solution.py:286
  6.9 41.3 %all-to-all-start = ((bf16[32,16,1024]{2,1,0:T(8,128)(2,1)}), bf16[32,16,1024]{2,1,0:T(8,128)(2,1)}, u32[]{:S(2)}, u32[]{:S(2)}) async-start(bf16[32,16,1024]{2,1,0:T(8,128)(2,1)} %bitcast.9), calls=%async_computation | async-start | bytes 2097152 | tf_op jit(solution)/shard_map/dispatch/all_to_all | solution.py:343
  17.9 17.0 %copy-start.3 = (bf16[1,4096,176]{1,2,0:T(8,128)(2,1)S(1)}, bf16[1,4096,176]{1,2,0:T(8,128)(2,1)}, u32[]{:S(2)}) copy-start(bf16[1,4096,176]{1,2,0:T(8,128)(2,1)} %param.18) | copy-start | bytes 4325380
  17.9 20.0 %copy-start.14 = (bf16[3,1,8,16,256]{4,3,2,1,0:T(8,128)(2,1)S(1)}, bf16[3,1,8,16,256]{4,3,2,1,0:T(8,128)(2,1)}, u32[]{:S(2)}) copy-start(bf16[3,1,8,16,256]{4,3,2,1,0:T(8,128)(2,1)} %param.26) | copy-start | bytes 589828
  19.3 22.6 %collective-permute-start = (bf16[176,1024]{1,0:T(8,128)(2,1)S(1)}, bf16[176,1024]{1,0:T(8,128)(2,1)S(1)}, u32[]{:S(2)}, u32[]{:S(2)}) collective-permute-start(bf16[176,1024]{1,0:T(8,128)(2,1)S(1)} %get-tuple-element.32), channel_id=1, source_target_pairs={{0,1},{1,0},{2,3},{3,2},{4,5},{5,4},{6,7},{7,6},{8,9},{9,8},{10,11... | collective-permute-start | bytes 1081352 | tf_op jit(solution)/shard_map/exchange_weights/ppermute | solution.py:250
  19.9 23.4 %collective-permute-start.1 = (bf16[176,1024]{1,0:T(8,128)(2,1)S(1)}, bf16[176,1024]{1,0:T(8,128)(2,1)S(1)}, u32[]{:S(2)}, u32[]{:S(2)}) collective-permute-start(bf16[176,1024]{1,0:T(8,128)(2,1)S(1)} %get-tuple-element.33), channel_id=1, source_target_pairs={{0,2},{1,3},{2,0},{3,1},{4,6},{5,7},{6,4},{7,5},{8,10},{9,11},{10,... | collective-permute-start | bytes 1081352 | tf_op jit(solution)/shard_map/exchange_weights/ppermute | solution.py:250
  20.0 26.4 %collective-permute-start.2 = (bf16[176,1024]{1,0:T(8,128)(2,1)S(1)}, bf16[176,1024]{1,0:T(8,128)(2,1)}, u32[]{:S(2)}, u32[]{:S(2)}) collective-permute-start(bf16[176,1024]{1,0:T(8,128)(2,1)S(1)} %get-tuple-element.34), channel_id=1, source_target_pairs={{0,3},{1,2},{2,1},{3,0},{4,7},{5,6},{6,5},{7,4},{8,11},{9,10},{10,... | collective-permute-start | bytes 1081352 | tf_op jit(solution)/shard_map/exchange_weights/ppermute | solution.py:250
  34.9 33.7 %collective-permute-start.10 = (bf16[176,4096]{1,0:T(8,128)(2,1)S(1)}, bf16[176,4096]{1,0:T(8,128)(2,1)S(1)}, u32[]{:S(2)}, u32[]{:S(2)}) collective-permute-start(bf16[176,4096]{1,0:T(8,128)(2,1)S(1)} %bitcast.42), channel_id=1, source_target_pairs={{0,6},{1,7},{2,4},{3,5},{4,2},{5,3},{6,0},{7,1},{8,14},{9,15},{10,... | collective-permute-start | bytes 4325384 | tf_op jit(solution)/shard_map/exchange_weights/ppermute | solution.py:305
  38.5 33.0 %collective-permute-start.6 = (bf16[3,32,256]{2,1,0:T(8,128)(2,1)}, bf16[3,32,256]{2,1,0:T(8,128)(2,1)S(1)}, u32[]{:S(2)}, u32[]{:S(2)}) collective-permute-start(bf16[3,32,256]{2,1,0:T(8,128)(2,1)} %get-tuple-element.60), channel_id=1, source_target_pairs={{0,1},{1,2},{2,3},{3,4},{4,5},{5,6},{6,7},{8,9},{9,10},{10,11},{11... | collective-permute-start | bytes 147464 | tf_op jit(solution)/shard_map/cache/ppermute | solution.py:309
  41.9 29.6 %collective-permute-start.7 = (bf16[3,32,256]{2,1,0:T(8,128)(2,1)}, bf16[3,32,256]{2,1,0:T(8,128)(2,1)S(1)}, u32[]{:S(2)}, u32[]{:S(2)}) collective-permute-start(bf16[3,32,256]{2,1,0:T(8,128)(2,1)} %get-tuple-element.59), channel_id=1, source_target_pairs={{1,0},{2,1},{3,2},{4,3},{5,4},{6,5},{7,6},{9,8},{10,9},{11,10},{12... | collective-permute-start | bytes 147464 | tf_op jit(solution)/shard_map/cache/ppermute | solution.py:310
  48.3 26.1 %collective-permute-start.4 = (bf16[512,1024]{1,0:T(8,128)(2,1)}, bf16[512,1024]{1,0:T(8,128)(2,1)S(1)}, u32[]{:S(2)}, u32[]{:S(2)}) collective-permute-start(bf16[512,1024]{1,0:T(8,128)(2,1)} %bitcast.10.x0), channel_id=1, source_target_pairs={{0,1},{1,0},{2,3},{3,2},{4,5},{5,4},{6,7},{7,6},{8,9},{9,8},{10,11... | collective-permute-start | bytes 3145736 | tf_op jit(solution)/shard_map/gather/ppermute | solution.py:254
  49.6 24.7 %collective-permute-start.5 = (bf16[512,1024]{1,0:T(8,128)(2,1)}, bf16[512,1024]{1,0:T(8,128)(2,1)S(1)}, u32[]{:S(2)}, u32[]{:S(2)}) collective-permute-start(bf16[512,1024]{1,0:T(8,128)(2,1)} %bitcast.10.x0), channel_id=1, source_target_pairs={{0,2},{2,0},{1,3},{3,1},{4,6},{6,4},{5,7},{7,5},{8,10},{10,8},{9,1... | collective-permute-start | bytes 3145736 | tf_op jit(solution)/shard_map/gather/ppermute | solution.py:254
  68.7 39.0 %collective-permute-start.14 = (bf16[4,176,1024]{2,1,0:T(8,128)(2,1)S(1)}, bf16[4,176,1024]{2,1,0:T(8,128)(2,1)S(1)}, u32[]{:S(2)}, u32[]{:S(2)}) collective-permute-start(bf16[4,176,1024]{2,1,0:T(8,128)(2,1)S(1)} %pad_maximum_fusion.refs_0_), channel_id=1, source_target_pairs={{0,6},{1,7},{2,4},{3,5},{4,2},{5,3},{6,0},{7,1},{8,14},{9,15},{10,... | collective-permute-start | bytes 4325384 | tf_op jit(solution)/shard_map/gather/ppermute | solution.py:250
  74.4 12.3 %collective-permute-start.8 = (bf16[256,1024]{1,0:T(8,128)(2,1)S(1)}, bf16[256,1024]{1,0:T(8,128)(2,1)S(1)}, u32[]{:S(2)}, u32[]{:S(2)}) collective-permute-start(bf16[256,1024]{1,0:T(8,128)(2,1)S(1)} %slice.14), channel_id=1, source_target_pairs={{0,1},{1,0},{2,3},{3,2},{4,5},{5,4},{6,7},{7,6},{8,9},{9,8},{10,11... | collective-permute-start | bytes 1572872 | tf_op jit(solution)/shard_map/gather/ppermute | solution.py:254
  76.0 12.3 %collective-permute-start.9 = (bf16[256,1024]{1,0:T(8,128)(2,1)S(1)}, bf16[256,1024]{1,0:T(8,128)(2,1)S(1)}, u32[]{:S(2)}, u32[]{:S(2)}) collective-permute-start(bf16[256,1024]{1,0:T(8,128)(2,1)S(1)} %slice.15), channel_id=1, source_target_pairs={{0,2},{2,0},{1,3},{3,1},{4,6},{6,4},{5,7},{7,5},{8,10},{10,8},{9,1... | collective-permute-start | bytes 1572872 | tf_op jit(solution)/shard_map/gather/ppermute | solution.py:254
  90.8 10.4 %collective-permute-start.11 = (bf16[352,512]{1,0:T(8,128)(2,1)S(1)}, bf16[352,512]{1,0:T(8,128)(2,1)S(1)}, u32[]{:S(2)}, u32[]{:S(2)}) collective-permute-start(bf16[352,512]{1,0:T(8,128)(2,1)S(1)} %hidden.1.h0), channel_id=1, source_target_pairs={{0,2},{2,0},{1,3},{3,1},{4,6},{6,4},{5,7},{7,5},{8,10},{10,8},{9,1... | collective-permute-start | bytes 1081352 | tf_op jit(solution)/shard_map/hidden_gather/ppermute | solution.py:254
  92.4 11.4 %collective-permute-start.12 = (bf16[352,512]{1,0:T(8,128)(2,1)S(1)}, bf16[352,512]{1,0:T(8,128)(2,1)S(1)}, u32[]{:S(2)}, u32[]{:S(2)}) collective-permute-start(bf16[352,512]{1,0:T(8,128)(2,1)S(1)} %hidden.1.h0), channel_id=1, source_target_pairs={{0,1},{1,0},{2,3},{3,2},{4,5},{5,4},{6,7},{7,6},{8,9},{9,8},{10,11... | collective-permute-start | bytes 1081352 | tf_op jit(solution)/shard_map/hidden_gather/ppermute | solution.py:254
  93.0 14.6 %collective-permute-start.13 = (bf16[352,512]{1,0:T(8,128)(2,1)S(1)}, bf16[352,512]{1,0:T(8,128)(2,1)S(1)}, u32[]{:S(2)}, u32[]{:S(2)}) collective-permute-start(bf16[352,512]{1,0:T(8,128)(2,1)S(1)} %hidden.1.h0), channel_id=1, source_target_pairs={{0,3},{1,2},{2,1},{3,0},{4,7},{5,6},{6,5},{7,4},{8,11},{9,10},{10,... | collective-permute-start | bytes 1081352 | tf_op jit(solution)/shard_map/hidden_gather/ppermute | solution.py:402
  107.6 41.4 %copy-start.5 = (bf16[4096,256]{1,0:T(8,128)(2,1)S(1)}, bf16[4096,256]{1,0:T(8,128)(2,1)}, u32[]{:S(2)}) copy-start(bf16[4096,256]{1,0:T(8,128)(2,1)} %proj_ref.1) | copy-start | bytes 6291460
  107.6 41.4 %copy-start.8 = (bf16[256,1024]{1,0:T(8,128)(2,1)S(1)}, bf16[256,1024]{1,0:T(8,128)(2,1)}, u32[]{:S(2)}) copy-start(bf16[256,1024]{1,0:T(8,128)(2,1)} %copy-done.7) | copy-start | bytes 1572868
  107.6 41.4 %copy-start.10 = (f32[4096]{0:T(1024)S(1)}, f32[4096]{0:T(1024)}, u32[]{:S(2)}) copy-start(f32[4096]{0:T(1024)} %param.20) | copy-start | bytes 49156
  110.6 38.4 %copy-start.1 = (bf16[1,256,4096]{2,1,0:T(8,128)(2,1)S(1)}, bf16[1,256,4096]{2,1,0:T(8,128)(2,1)}, u32[]{:S(2)}) copy-start(bf16[1,256,4096]{2,1,0:T(8,128)(2,1)} %param.14) | copy-start | bytes 6291460
  149.0 13.6 %copy-start.4 = (bf16[3,3,3,256,256]{4,3,2,1,0:T(8,128)(2,1)S(1)}, bf16[3,3,3,256,256]{4,3,2,1,0:T(8,128)(2,1)}, u32[]{:S(2)}) copy-start(bf16[3,3,3,256,256]{4,3,2,1,0:T(8,128)(2,1)} %time_ref.1) | copy-start | bytes 10616836
  149.0 13.6 %copy-start.6 = (bf16[3,3,256,256]{3,2,1,0:T(8,128)(2,1)S(1)}, bf16[3,3,256,256]{3,2,1,0:T(8,128)(2,1)}, u32[]{:S(2)}) copy-start(bf16[3,3,256,256]{3,2,1,0:T(8,128)(2,1)} %space_ref.1) | copy-start | bytes 3538948
  (7 other events, 34.4 us)
